TPU v7x, 512 devices: a whole 4x4x16 slice. The times are simulated.
512 devices in a mesh: frames: 8 (over x_hi, y), queries: 64 (over x_lo, z, core).
Axes of the slice: x: 4 (x_hi: 2, x_lo: 2; x = x_hi * 2 + x_lo), y: 4, z: 16, core: 2. Of those that a mesh axis runs over, the one named last changes fastest.
Arguments:
- frame_maps: bfloat16 [16, 4096, 256], P('frames', 'queries'), may hold values from -6 to 6
- query_table: bfloat16 [8, 4096, 256], P('frames', 'queries'), may hold values from -6 to 6
- start_frame: int32 [4096], P('queries'), may hold values from 0 to 15
- row_ids: int32 [4096], P('queries'), may hold values from 0 to 63
- conv1_w: bfloat16 [3, 3, 1, 16], replicated, may hold values from -2 to 2
- conv1_b: float32 [16], replicated, may hold values from -3 to 3
- conv2_w: bfloat16 [3, 3, 16, 32], replicated, may hold values from -0.5 to 0.5
- conv2_b: float32 [32], replicated, may hold values from -3 to 3
- proj_w: bfloat16 [32, 512], replicated, may hold values from -1 to 1
- proj_b: float32 [512], replicated, may hold values from -3 to 3
- time_w: float32 [3, 512], replicated, may hold values from -3 to 3
- time_b: float32 [512], replicated, may hold values from -3 to 3
Outputs:
- track_feats: bfloat16 [4096, 16, 512], P('queries', 'frames')
Inputs may be any that keep to these rules, and one draw needn't show every extreme that they name: `start_frame`: the frame in which the query was picked, one of the 16 frames. `row_ids`: a row index within the query's own block of 64 rows.
All inputs are finite; a program needn't handle non-finite values.
Results may differ from a plain program's by a relative error of at most 0.001.
The roundings to bfloat16 on the way count: a program that leaves them out, or rounds other values in their place, can miss the bound.
Values may be sent and summed in bfloat16 or wider, within the bound.
No kernel may reach another device: no remote copies, remote signals or barrier semaphores. Data moves between devices by JAX's collectives and lax.ppermute only.
A program may use at most 64 MiB of HBM per device.

v0:
```python
import jax
import jax.numpy as jnp
from jax import lax
from jax.sharding import PartitionSpec as P

MAP = 64
CH2 = 32


def padded(block, sides, width):
    for axis, dim in sides:
        count = lax.axis_size(axis)
        forward = [(i, i + 1) for i in range(count - 1)]
        backward = [(target, source) for source, target in forward]
        low = lax.ppermute(
            lax.slice_in_dim(block, block.shape[dim] - width, None, axis=dim), axis, forward
        )
        high = lax.ppermute(lax.slice_in_dim(block, 0, width, axis=dim), axis, backward)
        block = jnp.concatenate([low, block, high], axis=dim)
    return block


def per_device(
    frame_maps,
    query_table,
    start_frame,
    row_ids,
    conv1_w,
    conv1_b,
    conv2_w,
    conv2_b,
    proj_w,
    proj_b,
    time_w,
    time_b,
):
    frames_here = frame_maps.shape[0]
    frame_block = lax.axis_index("frames")
    own_rows = query_table[0][row_ids]
    owned = start_frame // frames_here == frame_block
    own_term = jnp.where(owned[:, None], own_rows.astype(jnp.float32), 0.0)
    queries = lax.psum(own_term.astype(jnp.bfloat16), "frames")
    query_count = queries.shape[0]
    every_query = lax.all_gather(queries, "queries", axis=0, tiled=True)
    band = (
        jnp.einsum("frc,qc->rfq", frame_maps, every_query, preferred_element_type=jnp.float32)
        * 0.0625
    ).astype(jnp.bfloat16)
    costs = lax.all_to_all(band, "queries", split_axis=2, concat_axis=0, tiled=True)
    block_size = min(64, query_count)
    block_count = query_count // block_size
    pooled_init = jnp.zeros((CH2, frames_here, query_count), jnp.bfloat16)

    def one_block(block_index, pooled_acc):
        images = costs.reshape(MAP, MAP, 1, frames_here * block_size)
        layer_one = lax.conv_general_dilated(
            images,
            conv1_w,
            (2, 2),
            ((1, 1), (1, 1)),
            dimension_numbers=("HWCN", "HWIO", "HWCN"),
            preferred_element_type=jnp.float32,
        )
        layer_one = jax.nn.relu(layer_one + conv1_b[None, None, :, None]).astype(jnp.bfloat16)
        layer_two = lax.conv_general_dilated(
            layer_one,
            conv2_w,
            (2, 2),
            ((1, 1), (1, 1)),
            dimension_numbers=("HWCN", "HWIO", "HWCN"),
            preferred_element_type=jnp.float32,
        )
        layer_two = jax.nn.relu(layer_two + conv2_b[None, None, :, None])
        pooled_block = (
            jnp.mean(layer_two, axis=(0, 1))
            .astype(jnp.bfloat16)
            .reshape(CH2, frames_here, block_size)
        )
        return pooled_block

    pooled = lax.fori_loop(0, block_count, one_block, pooled_init)
    projected = padded(
        (
            jnp.einsum("cfq,cd->qfd", pooled, proj_w, preferred_element_type=jnp.float32) + proj_b
        ).astype(jnp.bfloat16),
        (("frames", 1),),
        1,
    )
    widened_f32 = projected.astype(jnp.float32)
    mixed = (
        time_w[0] * widened_f32[:, :-2]
        + time_w[1] * widened_f32[:, 1:-1]
        + time_w[2] * widened_f32[:, 2:]
        + time_b
    )
    return mixed.astype(jnp.bfloat16)


def solution(mesh):
    placed = (
        P("frames", "queries", None),
        P("frames", "queries", None),
        P("queries"),
        P("queries"),
        P(),
        P(),
        P(),
        P(),
        P(),
        P(),
        P(),
        P(),
    )
    return jax.shard_map(
        per_device,
        mesh=mesh,
        in_specs=placed,
        out_specs=P("queries", "frames", None),
        check_vma=False,
    )
```

profile of v0, /device:TPU:24, one launch (start us, length us, event | category | flops | bytes accessed | tf_op | source)
XLA Modules:
  0.0 289.1 jit_solution(6858478085503585251)
XLA Ops:
  6.5 0.7 compare_select_fusion
  7.2 1.4 gather_fusion
  8.7 0.7 fusion.18
  9.3 0.1 select_convert_fusion
  9.4 36.9 %psum.7 = bf16[64,256]{1,0:T(8,128)(2,1)} all-reduce(bf16[64,256]{1,0:T(8,128)(2,1)S(1)} %select_convert_fusion), channel_id=1, replica_groups=mesh['frames'=8,'queries'=64] {'frames'}, use_global_device_ids=true, to_apply=%region_0.1 | all-reduce | flops 16384 | bytes 65536 | tf_op jit(solution)/shard_map/psum | solution.py:42
  46.3 0.0 all-gather.2.cloned.1.call-update
  46.3 127.5 %all-gather.2.cloned.1.call-done = bf16[4096,256]{1,0:T(8,128)(2,1)} async-done(((bf16[64,256]{1,0:T(8,128)(2,1)}), bf16[4096,256]{1,0:T(8,128)(2,1)}) %all-gather.2.cloned.1.call-update) | async-done | bytes 2097168 | tf_op jit(solution)/shard_map/all_gather | solution.py:44
  173.8 2.4 fusion.1
  176.2 2.8 copy.21
  179.1 1.5 reshape.32
  180.6 61.2 %all_to_all.15 = bf16[64,2,4096]{2,1,0:T(2,128)(2,1)} all-to-all(bf16[64,2,4096]{2,1,0:T(2,128)(2,1)S(1)} %reshape.32), channel_id=1, replica_groups=mesh['frames'=8,'queries'=64] {'queries'}, dimensions={0} | all-to-all | bytes 2097152 | tf_op jit(solution)/shard_map/all_to_all | solution.py:49
  241.8 5.1 %reshape.33 = bf16[4096,2,64]{2,1,0:T(2,128)(2,1)S(1)} reshape(bf16[64,2,4096]{2,1,0:T(2,128)(2,1)} %all_to_all.15) | data formatting | bytes 2097152
  246.9 6.4 %copy.22 = bf16[64,2,64,64]{3,1,0,2:T(2,128)(2,1)} copy(bf16[64,2,64,64]{0,1,3,2:T(2,128)(2,1)S(1)} %bitcast.22) | data formatting | bytes 2097152 | tf_op jit(solution)/shard_map/all_to_all | solution.py:49
  253.3 7.8 %reshape.31 = bf16[64,64,1,128]{3,2,1,0:T(2,128)(2,1)S(1)} reshape(bf16[64,64,2,64]{3,2,1,0:T(2,128)(2,1)} %bitcast.23) | data formatting | bytes 2097152 | tf_op jit(solution)/shard_map/while/body/eval_jaxpr/reshape | solution.py:55
  261.2 0.0 copy-start.2
  261.2 0.0 copy-start.4
  261.2 5.5 %maximum_reduce_fusion = f32[32,128]{1,0:T(8,128)S(1)} fusion(f32[32]{0:T(128)S(1)} %copy-done.7, bf16[3,3,16,32]{3,2,1,0:T(8,128)(2,1)S(1)} %copy-done.5, f32[16]{0:T(128)S(1)} %copy-done.8, bf16[64,64,1,128]{3,2,1,0:T(2,128)(2,1)S(1)} %reshape.31, bf16[3,3,1,16]{3,1,2,0:T(4,128)(2,1)S(1)} %copy-done.6), kind=kOutput, calls=%fused_computation.6 | convolution fusion | flops 335937536 | bytes 1074656 | tf_op jit(solution)/shard_map/while/body/eval_jaxpr/conv_general_dilated | solution.py:65
  266.7 0.1 convert_element_type.42
  266.8 0.2 fusion.9
  267.0 4.5 %collective-permute-start = (bf16[64,1,512]{2,0,1:T(8,128)(2,1)S(1)}, bf16[64,1,512]{2,0,1:T(8,128)(2,1)S(1)}, u32[]{:S(2)}, u32[]{:S(2)}) collective-permute-start(bf16[64,1,512]{2,0,1:T(8,128)(2,1)S(1)} %get-tuple-element.16), channel_id=1, source_target_pairs={{0,64},{64,128},{128,192},{192,256},{256,320},{320,384},{384,448},... | collective-permute-start | bytes 196616 | tf_op jit(solution)/shard_map/ppermute | solution.py:15
  271.5 1.9 collective-permute-start.1
  273.5 7.8 %collective-permute-done.1 = bf16[64,1,512]{2,0,1:T(8,128)(2,1)S(1)} collective-permute-done((bf16[64,1,512]{2,0,1:T(8,128)(2,1)S(1)}, bf16[64,1,512]{2,0,1:T(8,128)(2,1)S(1)}, u32[]{:S(2)}, u32[]{:S(2)}) %collective-permute-start.1) | collective-permute-done | bytes 65568 | tf_op jit(solution)/shard_map/ppermute | solution.py:18
  281.4 0.1 fusion.12
  281.4 0.8 copy.26
  (23 shorter events, 0.1 us)
Async XLA Ops:
  6.5 167.2 %copy-start = (bf16[2,64,256]{2,1,0:T(8,128)(2,1)S(1)}, bf16[2,64,256]{2,1,0:T(8,128)(2,1)}, u32[]{:S(2)}) copy-start(bf16[2,64,256]{2,1,0:T(8,128)(2,1)} %param.12) | copy-start | bytes 196612
  6.5 167.2 %all-gather.2.cloned.1.call-start = ((), (), s32[]{:S(2)}) async-start(), calls=%async_computation.1 | async-start | bytes 2129920 | tf_op jit(solution)/shard_map/all_gather | solution.py:44
  253.3 7.8 %copy-start.5 = (bf16[3,3,16,32]{3,2,1,0:T(8,128)(2,1)S(1)}, bf16[3,3,16,32]{3,2,1,0:T(8,128)(2,1)}, u32[]{:S(2)}) copy-start(bf16[3,3,16,32]{3,2,1,0:T(8,128)(2,1)} %param.18) | copy-start | bytes 27652
  253.3 7.8 %copy-start.6 = (bf16[3,3,1,16]{3,1,2,0:T(4,128)(2,1)S(1)}, bf16[3,3,1,16]{3,1,2,0:T(4,128)(2,1)}, u32[]{:S(2)}) copy-start(bf16[3,3,1,16]{3,1,2,0:T(4,128)(2,1)} %param.16) | copy-start | bytes 868
  253.3 7.8 %copy-start.7 = (f32[32]{0:T(128)S(1)}, f32[32]{0:T(128)}, u32[]{:S(2)}) copy-start(f32[32]{0:T(128)} %param.19) | copy-start | bytes 388
  253.3 7.8 %copy-start.8 = (f32[16]{0:T(128)S(1)}, f32[16]{0:T(128)}, u32[]{:S(2)}) copy-start(f32[16]{0:T(128)} %param.17) | copy-start | bytes 196
  261.1 5.6 %copy-start.1 = (bf16[32,512]{1,0:T(8,128)(2,1)S(1)}, bf16[32,512]{1,0:T(8,128)(2,1)}, u32[]{:S(2)}) copy-start(bf16[32,512]{1,0:T(8,128)(2,1)} %param.20) | copy-start | bytes 98308
  261.2 5.6 %copy-start.3 = (f32[512]{0:T(512)S(1)}, f32[512]{0:T(512)}, u32[]{:S(2)}) copy-start(f32[512]{0:T(512)} %param.21) | copy-start | bytes 6148
  261.2 12.3 %copy-start.2 = (f32[3,512]{1,0:T(4,128)S(1)}, f32[3,512]{1,0:T(4,128)}, u32[]{:S(2)}) copy-start(f32[3,512]{1,0:T(4,128)} %param.22) | copy-start | bytes 18436
  261.2 20.2 %copy-start.4 = (f32[512]{0:T(512)S(1)}, f32[512]{0:T(512)}, u32[]{:S(2)}) copy-start(f32[512]{0:T(512)} %param.23) | copy-start | bytes 6148
  267.0 6.5 %collective-permute-start = (bf16[64,1,512]{2,0,1:T(8,128)(2,1)S(1)}, bf16[64,1,512]{2,0,1:T(8,128)(2,1)S(1)}, u32[]{:S(2)}, u32[]{:S(2)}) collective-permute-start(bf16[64,1,512]{2,0,1:T(8,128)(2,1)S(1)} %get-tuple-element.16), channel_id=1, source_target_pairs={{0,64},{64,128},{128,192},{192,256},{256,320},{320,384},{384,448},... | collective-permute-start | bytes 196616 | tf_op jit(solution)/shard_map/ppermute | solution.py:15
  271.5 9.8 %collective-permute-start.1 = (bf16[64,1,512]{2,0,1:T(8,128)(2,1)S(1)}, bf16[64,1,512]{2,0,1:T(8,128)(2,1)S(1)}, u32[]{:S(2)}, u32[]{:S(2)}) collective-permute-start(bf16[64,1,512]{2,0,1:T(8,128)(2,1)S(1)} %get-tuple-element.17), channel_id=1, source_target_pairs={{64,0},{128,64},{192,128},{256,192},{320,256},{384,320},{448,384},... | collective-permute-start | bytes 196616 | tf_op jit(solution)/shard_map/ppermute | solution.py:18
Sparse Core Ops, SparseCore 0:
  46.4 127.3 all-gather.1
where the time goes:
time: 290 us; the launch traced here: 289 us
  waiting for transfers between devices  135 us (47%)
  blocking collectives  98.1 us (34%)
  local copies, waits for them, and re-layouts  26 us (9%)
  between operations  13.6 us (5%)
  matrix products  8.09 us (3%)
  starting transfers between devices  6.45 us (2%)
    all_gather x1, waiting for transfers between devices, per_device(): every_query = lax.all_gather(queries, 'queries', axis=0, tiled=True)  127 us
    all_to_all x1, blocking collectives, per_device(): lax.all_to_all(band, 'queries', split_axis=2, concat_axis=0, tiled=True)  61.2 us
    psum x1, blocking collectives, per_device(): queries = lax.psum(own_term.astype(jnp.bfloat16), 'frames')  36.9 us
    ppermute x1, waiting for transfers between devices, padded(): lax.ppermute(lax.slice_in_dim(block, 0, width, axis=dim), axis, backward)  7.81 us
    reshape x1, local copies, waits for them, and re-layouts, one_block(): images = costs.reshape(MAP, MAP, 1, frames_here * block_size)  7.79 us
    unnamed x20, local copies, waits for them, and re-layouts  6.6 us
    all_to_all x1, local copies, waits for them, and re-layouts, per_device(): lax.all_to_all(band, 'queries', split_axis=2, concat_axis=0, tiled=True)  6.44 us
  transfers between devices with their start and end apart: 3, of which 2 were waited for; matrix products, arithmetic and copies ran while one was open for 0% of the time, Pallas kernels for 0%

commit v1 on v0

v1 whole, which is shorter than its diff:
```python
import functools

import jax
import jax.numpy as jnp
from jax import lax
from jax.experimental import pallas as pl
from jax.experimental.pallas import tpu as pltpu
from jax.sharding import Mesh, PartitionSpec as P

MAP = 64
CH1 = 16
CH2 = 32
HALF1 = MAP // 2
HALF2 = MAP // 4
ROW1 = HALF1 * CH1
ROW2 = HALF2 * CH2
BF = jnp.bfloat16
F32 = jnp.float32
INTERPRET = False


def weights_kernel(w1_ref, w2_ref, a_ref, b_ref):
    def iota(shape, dim):
        return lax.broadcasted_iota(jnp.int32, shape, dim)

    pick = (iota((CH1, ROW1), 1) % CH1 == iota((CH1, ROW1), 0)).astype(BF)
    w1_wide = jnp.dot(w1_ref[...], pick, preferred_element_type=F32)
    in_x = iota((MAP, ROW1), 0)
    out_x = iota((MAP, ROW1), 1) // CH1
    a_ref[0:MAP, :] = jnp.zeros((MAP, ROW1), BF)
    for dy in range(3):
        block = jnp.zeros((MAP, ROW1), F32)
        for dx in range(3):
            tap = w1_wide[3 * dy + dx : 3 * dy + dx + 1, :]
            block = jnp.where(in_x == 2 * out_x + dx - 1, tap, block)
        a_ref[MAP * (dy + 1) : MAP * (dy + 2), :] = block.astype(BF)

    rows = (iota((ROW1, CH1), 0) % CH1 == iota((ROW1, CH1), 1)).astype(BF)
    cols = (iota((CH2, ROW2), 1) % CH2 == iota((CH2, ROW2), 0)).astype(BF)
    in_x = iota((ROW1, ROW2), 0) // CH1
    out_x = iota((ROW1, ROW2), 1) // CH2
    for dy in range(3):
        block = jnp.zeros((ROW1, ROW2), F32)
        for dx in range(3):
            wide = jnp.dot(w2_ref[3 * dy + dx], cols, preferred_element_type=F32).astype(BF)
            tall = jnp.dot(rows, wide, preferred_element_type=F32)
            block = jnp.where(in_x == 2 * out_x + dx - 1, tall, block)
        b_ref[ROW1 * dy : ROW1 * (dy + 1), :] = block.astype(BF)


def banded_weights(conv1_w, conv2_w):
    return pl.pallas_call(
        weights_kernel,
        out_shape=(
            jax.ShapeDtypeStruct((4 * MAP, ROW1), BF),
            jax.ShapeDtypeStruct((3 * ROW1, ROW2), BF),
        ),
        cost_estimate=pl.CostEstimate(flops=400_000_000, bytes_accessed=2_000_000, transcendentals=0),
        interpret=INTERPRET,
    )(conv1_w.reshape(9, CH1), conv2_w.reshape(9, CH1, CH2))


def cost_kernel(z_count, where_ref, q_ref, own_ref, *refs):
    far_refs = refs[:-9]
    a_ref, b_ref, bias1_ref, bias2_ref, kept_ref, sent_ref, corr, hid, acc = refs[-9:]
    x, z = where_ref[0], where_ref[1]
    n = q_ref.shape[0]
    corr[0, :, 0:128] = jnp.zeros((n, 128), BF)
    hid[0, :, 0:ROW1] = jnp.zeros((n, ROW1), BF)
    q = q_ref[...]

    def put(low, high, chip):
        cells = jnp.concatenate([low[0:MAP], high[0:MAP], low[MAP:], high[MAP:]], axis=0)
        got = lax.dot_general(q, cells, (((1,), (1,)), ((), ())), preferred_element_type=F32)
        got = (got * 0.0625).astype(BF)
        for side in range(2):
            part = got[:, 128 * side : 128 * (side + 1)]
            y = (x if side == 0 else 1 - x) * z_count + chip
            corr[y, :, 128:256] = part
            corr[y + 1, :, 0:128] = part

    put(own_ref[0], own_ref[1], z)
    distance = 0
    for ref in far_refs:
        per = ref.shape[0] // 4
        for i in range(per):
            distance += 1
            k = 2 * i
            put(ref[k], ref[k + 1], lax.rem(z + z_count - distance, z_count))
            if 2 * distance < z_count:
                k += 2 * per
                put(ref[k], ref[k + 1], lax.rem(z + distance, z_count))

    bias1 = bias1_ref[...]
    rows1 = 8
    for t in range(HALF1 // rows1):
        lhs = corr[rows1 * t : rows1 * (t + 1)].reshape(rows1 * n, 256)
        got = jnp.dot(lhs, a_ref[...], preferred_element_type=F32)
        got = jnp.maximum(got + bias1, 0.0).astype(BF).reshape(rows1, n, ROW1)
        for s in range(rows1):
            y = rows1 * t + s
            j = y // 2
            if y % 2 == 0:
                hid[j, :, ROW1 : 2 * ROW1] = got[s]
            else:
                hid[j, :, 2 * ROW1 : 3 * ROW1] = got[s]
                hid[j + 1, :, 0:ROW1] = got[s]

    bias2 = bias2_ref[...]
    half = ROW2 // 2
    rows2 = 4
    acc[...] = jnp.zeros(acc.shape, F32)
    for t in range(HALF2 // rows2):
        tile = slice(rows2 * t, rows2 * (t + 1))
        left = jnp.zeros((rows2 * n, half), F32)
        for dy in range(3):
            k = slice(ROW1 * dy, ROW1 * dy + ROW1 // 2)
            left += jnp.dot(
                hid[tile, :, k].reshape(rows2 * n, ROW1 // 2),
                b_ref[k, 0:half],
                preferred_element_type=F32,
            )
        right = jnp.dot(
            hid[tile].reshape(rows2 * n, 3 * ROW1), b_ref[:, half:], preferred_element_type=F32
        )
        left = jnp.maximum(left + bias2[:, :half], 0.0).reshape(rows2, n, half)
        right = jnp.maximum(right + bias2[:, half:], 0.0).reshape(rows2, n, half)
        acc[:, :half] += jnp.sum(left, axis=0)
        acc[:, half:] += jnp.sum(right, axis=0)
    total = acc[:, 0:128]
    for k in range(1, ROW2 // 128):
        total = total + acc[:, 128 * k : 128 * (k + 1)]
    total = (total[:, 0:32] + total[:, 32:64]) + (total[:, 64:96] + total[:, 96:128])
    pooled = (total * (1.0 / (HALF2 * HALF2))).astype(BF)
    kept_ref[...] = pooled[: n // 2]
    sent_ref[...] = pooled[n // 2 :]


def pooled_costs(where, queries, own, far, a, b, bias1, bias2):
    n = queries.shape[0]
    z_count = MAP // 4
    vmem = pl.BlockSpec(memory_space=pltpu.VMEM)

    return pl.pallas_call(
        functools.partial(cost_kernel, z_count),
        out_shape=(jax.ShapeDtypeStruct((n // 2, CH2), BF),) * 2,
        in_specs=[pl.BlockSpec(memory_space=pltpu.SMEM)] + [vmem] * (6 + len(far)),
        out_specs=(vmem, vmem),
        scratch_shapes=[
            pltpu.VMEM((HALF1 + 1, n, 256), BF),
            pltpu.VMEM((HALF2 + 1, n, 3 * ROW1), BF),
            pltpu.VMEM((n, ROW2), F32),
        ],
        cost_estimate=pl.CostEstimate(
            flops=5_000_000_000, bytes_accessed=4_000_000, transcendentals=0
        ),
        interpret=INTERPRET,
    )(where, queries, own, *far, a, b, bias1, bias2)


def per_device(
    sizes,
    frame_maps,
    query_table,
    start_frame,
    row_ids,
    conv1_w,
    conv1_b,
    conv2_w,
    conv2_b,
    proj_w,
    proj_b,
    time_w,
    time_b,
):
    xh_count, y_count, _, z_count, _ = sizes
    frame_count = xh_count * y_count
    x = lax.axis_index("xl")
    z = lax.axis_index("z")
    frame_block = lax.axis_index("xh") * y_count + lax.axis_index("y")
    where = jnp.stack([x, z]).astype(jnp.int32)
    swap = [(0, 1), (1, 0)]

    a, b = banded_weights(conv1_w, conv2_w)
    bias1 = jnp.tile(conv1_b, HALF1)[None, :]
    bias2 = jnp.tile(conv2_b, HALF2)[None, :]

    mine = jnp.where(x == 0, frame_maps[0], frame_maps[1])
    other = jnp.where(x == 0, frame_maps[1], frame_maps[0])

    cells_here = query_table.shape[1]
    owned = start_frame // frame_maps.shape[0] == frame_block
    chosen = (row_ids[:, None] == jnp.arange(cells_here)[None, :]) & owned[:, None]
    queries = jnp.dot(chosen.astype(BF), query_table[0], preferred_element_type=F32).astype(BF)
    other, queries = lax.optimization_barrier((other, queries))

    def flip(axis, count, step):
        return lambda v: lax.ppermute(v, axis, [(i, i ^ step) for i in range(count)])

    def along(block, distance):
        pairs = []
        for i in range(z_count):
            pairs.append((2 * i, 2 * ((i + distance) % z_count)))
            pairs.append((2 * i + 1, 2 * ((i - distance) % z_count) + 1))
        return lax.ppermute(block, ("z", "c"), pairs)

    def both(block):
        return lax.all_gather(block, "c", axis=0, tiled=True)

    theirs = lax.ppermute(other, "xl", swap)
    got = flip("y", y_count, 1)(queries)
    theirs, queries = lax.optimization_barrier((theirs, queries + got))

    own = lax.all_gather(jnp.concatenate([mine, theirs], axis=0), "c", axis=0)
    near, next_near = along(own, 1), along(own, 2)
    if y_count > 2:
        queries = queries + flip("y", y_count, 2)(queries)
    near, next_near, queries = lax.optimization_barrier((near, next_near, queries))

    moving = jnp.concatenate([near, next_near], axis=0)
    far = [both(moving)]
    moving = along(moving, 2)
    if xh_count > 1:
        queries = queries + flip("xh", xh_count, 1)(queries)
    moving, queries = lax.optimization_barrier((moving, queries))

    far.append(both(moving))
    moving = along(moving, 2)
    queries = jnp.concatenate([queries, lax.ppermute(queries, "xl", swap)], axis=0)
    moving, queries = lax.optimization_barrier((moving, queries))

    far.append(both(moving))
    moving = along(moving, 2)
    far.append(both(moving))

    kept, sent = pooled_costs(where, queries, own, far, a, b, bias1, bias2)

    def frame_pairs(cross):
        pairs = []
        for f in range(frame_count):
            if f > 0:
                pairs.append((2 * (f - 1) + 1, 2 * f + (0 if cross else 1)))
            if f < frame_count - 1:
                pairs.append((2 * (f + 1), 2 * f + (1 if cross else 0)))
        return pairs

    partner = lax.ppermute(sent, "xl", swap)
    straight = lax.ppermute(kept, ("xh", "y", "xl"), frame_pairs(False))
    crossed = lax.ppermute(sent, ("xh", "y", "xl"), frame_pairs(True))
    first = x == 0
    around = jnp.stack(
        [
            jnp.where(first, crossed, straight),
            jnp.where(first, kept, partner),
            jnp.where(first, partner, kept),
            jnp.where(first, straight, crossed),
        ]
    )
    projected = lax.reduce_precision(
        jnp.einsum("fqc,cd->fqd", around, proj_w, preferred_element_type=F32) + proj_b, 8, 7
    )
    index = jnp.arange(4)
    valid = ((index > 0) | (frame_block > 0)) & ((index < 3) | (frame_block < frame_count - 1))
    wide = jnp.where(valid[:, None, None], projected, 0.0)
    mixed = time_w[0] * wide[:-2] + time_w[1] * wide[1:-1] + time_w[2] * wide[2:] + time_b
    return jnp.transpose(mixed, (1, 0, 2)).astype(BF)


def solution(mesh):

    frames, _ = mesh.devices.shape
    sizes = (frames // 4 or 1, min(frames, 4), 2, MAP // 4, 2)
    fine = Mesh(mesh.devices.reshape(sizes), ("xh", "y", "xl", "z", "c"))
    fr = ("xh", "y")
    qs = ("xl", "z", "c")
    placed = (P(fr, qs, None), P(fr, qs, None), P(qs), P(qs)) + (P(),) * 8
    return jax.shard_map(
        functools.partial(per_device, sizes),
        mesh=fine,
        in_specs=placed,
        out_specs=P(qs, fr, None),
        check_vma=False,
    )
```

time: 290 us -> 103 us (0.36)
  waiting for transfers between devices: 135 us -> 19.8 us
  blocking collectives: 98.1 us -> 11.1 us
  starting transfers between devices: 6.45 us -> 49.2 us
  local copies, waits for them, and re-layouts: 26 us -> 4.26 us
  between operations: 13.6 us -> 0.24 us
  Pallas kernels: 0 us -> 12.4 us
  matrix products: 8.09 us -> 1.18 us
    all_gather x1 -> x0, waiting for transfers between devices: 127 us -> none  [per_device(): every_query = lax.all_gather(queries, 'queries', axis=0, tiled=True)]
    all_to_all x1 -> x0, blocking collectives: 61.2 us -> none  [per_device(): lax.all_to_all(band, 'queries', split_axis=2, concat_axis=0, tiled=True)]
    ppermute x2 -> x13, starting transfers between devices: 6.44 us -> 49.2 us  [the longest x5 23.3 us: along(): return lax.ppermute(block, ('z', 'c'), pairs)]
    psum x1 -> x0, blocking collectives: 36.9 us -> none  [per_device(): queries = lax.psum(own_term.astype(jnp.bfloat16), 'frames')]
    pallas_call x0 -> x2, Pallas kernels: none -> 12.4 us  [the longest x1 7.5 us: pooled_costs(): pl.pallas_call(functools.partial(cost_kernel, z_count), out_shape=(jax.Sh...]
    ppermute x2 -> x13, waiting for transfers between devices: 7.81 us -> 19.8 us  [the longest x5 5.91 us: along(): return lax.ppermute(block, ('z', 'c'), pairs)]
    all_gather x0 -> x5, blocking collectives: none -> 11.1 us  [the longest x4 9.23 us: both(): return lax.all_gather(block, 'c', axis=0, tiled=True)]
    unnamed x20 -> x13, local copies, waits for them, and re-layouts: 6.6 us -> 0.03 us
  transfers between devices with their start and end apart: 3 -> 13, of which waited for: 2 -> 8; matrix products, arithmetic and copies ran while one was open for 0% -> 5% of each run, Pallas kernels for 0% -> 5%
where the time goes in v1:
time: 103 us; the launch traced here: 102 us
  starting transfers between devices  49.2 us (48%)
  waiting for transfers between devices  19.8 us (19%)
  Pallas kernels  12.4 us (12%)
  blocking collectives  11.1 us (11%)
  local copies, waits for them, and re-layouts  4.26 us (4%)
  other arithmetic  3.65 us (4%)
  matrix products  1.18 us (1%)
    ppermute x5, starting transfers between devices, along(): return lax.ppermute(block, ('z', 'c'), pairs)  23.3 us
    ppermute x3, starting transfers between devices, flip(): lax.ppermute(v, axis, [(i, i ^ step) for i in range(count)])  10.6 us
    all_gather x4, blocking collectives, both(): return lax.all_gather(block, 'c', axis=0, tiled=True)  9.23 us
    pallas_call x1, Pallas kernels, pooled_costs(): pl.pallas_call(functools.partial(cost_kernel, z_count), out_shape=(jax.Sh...  7.5 us
    ppermute x5, waiting for transfers between devices, along(): return lax.ppermute(block, ('z', 'c'), pairs)  5.91 us
    ppermute x1, waiting for transfers between devices, per_device(): straight = lax.ppermute(kept, ('xh', 'y', 'xl'), frame_pairs(False))  5.88 us
    pallas_call x1, Pallas kernels, banded_weights(): pl.pallas_call(weights_kernel, out_shape=(jax.ShapeDtypeStruct((4 * MAP,...  4.86 us
    ppermute x3, waiting for transfers between devices, flip(): lax.ppermute(v, axis, [(i, i ^ step) for i in range(count)])  4.7 us
  transfers between devices with their start and end apart: 13, of which 8 were waited for; matrix products, arithmetic and copies ran while one was open for 5% of the time, Pallas kernels for 5%

profile of v1, /device:TPU:24, one launch (start us, length us, event | category | flops | bytes accessed | tf_op | source)
XLA Modules:
  0.0 101.8 jit_solution(10803529245868443966)
XLA Ops:
  2.5 2.7 %collective-permute-start.1 = (bf16[64,256]{1,0:T(8,128)(2,1)S(1)}, bf16[64,256]{1,0:T(8,128)(2,1)S(1)}, u32[]{:S(2)}, u32[]{:S(2)}) collective-permute-start(bf16[64,256]{1,0:T(8,128)(2,1)S(1)} %convolution_convert_fusion), channel_id=1, source_target_pairs={{0,64},{64,0},{128,192},{192,128},{1,65},{65,1},{129,193},{193,129... | collective-permute-start | bytes 98312 | tf_op jit(solution)/shard_map/ppermute | solution.py:198
  5.1 3.4 %collective-permute-start = (bf16[64,256]{1,0:T(8,128)(2,1)S(1)}, bf16[64,256]{1,0:T(8,128)(2,1)S(1)}, u32[]{:S(2)}, u32[]{:S(2)}) collective-permute-start(bf16[64,256]{1,0:T(8,128)(2,1)S(1)} %get-tuple-element.20), channel_id=1, source_target_pairs={{0,32},{32,0},{1,33},{33,1},{2,34},{34,2},{3,35},{35,3},{4,36},{36... | collective-permute-start | bytes 98312 | tf_op jit(solution)/shard_map/ppermute | solution.py:210
  8.6 2.4 %collective-permute-done = bf16[64,256]{1,0:T(8,128)(2,1)S(1)} collective-permute-done((bf16[64,256]{1,0:T(8,128)(2,1)S(1)}, bf16[64,256]{1,0:T(8,128)(2,1)S(1)}, u32[]{:S(2)}, u32[]{:S(2)}) %collective-permute-start) | collective-permute-done | bytes 32800 | tf_op jit(solution)/shard_map/ppermute | solution.py:210
  12.8 3.8 %collective-permute-start.2 = (bf16[2,128,256]{2,1,0:T(8,128)(2,1)S(1)}, bf16[2,128,256]{2,1,0:T(8,128)(2,1)S(1)}, u32[]{:S(2)}, u32[]{:S(2)}) collective-permute-start(bf16[2,128,256]{2,1,0:T(8,128)(2,1)S(1)} %bitcast.29), channel_id=1, source_target_pairs={{0,2},{1,31},{2,4},{3,1},{4,6},{5,3},{6,8},{7,5},{8,10},{9,7},{10,... | collective-permute-start | bytes 393224 | tf_op jit(solution)/shard_map/ppermute | solution.py:205
  16.7 5.2 %collective-permute-start.3 = (bf16[2,128,256]{2,1,0:T(8,128)(2,1)S(1)}, bf16[2,128,256]{2,1,0:T(8,128)(2,1)S(1)}, u32[]{:S(2)}, u32[]{:S(2)}) collective-permute-start(bf16[2,128,256]{2,1,0:T(8,128)(2,1)S(1)} %bitcast.30), channel_id=1, source_target_pairs={{0,4},{1,29},{2,6},{3,31},{4,8},{5,1},{6,10},{7,3},{8,12},{9,5},{1... | collective-permute-start | bytes 393224 | tf_op jit(solution)/shard_map/ppermute | solution.py:205
  21.8 3.0 %collective-permute-start.4 = (bf16[64,256]{1,0:T(8,128)(2,1)S(1)}, bf16[64,256]{1,0:T(8,128)(2,1)S(1)}, u32[]{:S(2)}, u32[]{:S(2)}) collective-permute-start(bf16[64,256]{1,0:T(8,128)(2,1)S(1)} %add.36), channel_id=1, source_target_pairs={{0,128},{64,192},{128,0},{192,64},{1,129},{65,193},{129,1},{193,65... | collective-permute-start | bytes 98312 | tf_op jit(solution)/shard_map/ppermute | solution.py:198
  24.9 4.3 %collective-permute-done.4 = bf16[64,256]{1,0:T(8,128)(2,1)S(1)} collective-permute-done((bf16[64,256]{1,0:T(8,128)(2,1)S(1)}, bf16[64,256]{1,0:T(8,128)(2,1)S(1)}, u32[]{:S(2)}, u32[]{:S(2)}) %collective-permute-start.4) | collective-permute-done | bytes 32800 | tf_op jit(solution)/shard_map/ppermute | solution.py:198
  29.2 2.8 %collective-permute-done.3 = bf16[2,128,256]{2,1,0:T(8,128)(2,1)S(1)} collective-permute-done((bf16[2,128,256]{2,1,0:T(8,128)(2,1)S(1)}, bf16[2,128,256]{2,1,0:T(8,128)(2,1)S(1)}, u32[]{:S(2)}, u32[]{:S(2)}) %collective-permute-start.3) | collective-permute-done | bytes 131104 | tf_op jit(solution)/shard_map/ppermute | solution.py:205
  32.0 3.6 %collective-permute-start.5 = (bf16[4,128,256]{2,1,0:T(8,128)(2,1)S(1)}, bf16[4,128,256]{2,1,0:T(8,128)(2,1)S(1)}, u32[]{:S(2)}, u32[]{:S(2)}) collective-permute-start(bf16[4,128,256]{2,1,0:T(8,128)(2,1)S(1)} %constant_dynamic-update-slice_fusion), channel_id=1, source_target_pairs={{0,4},{1,29},{2,6},{3,31},{4,8},{5,1},{6,10},{7,3},{8,12},{9,5},{1... | collective-permute-start | bytes 786440 | tf_op jit(solution)/shard_map/ppermute | solution.py:205
  36.4 4.9 %collective-permute-start.6 = (bf16[64,256]{1,0:T(8,128)(2,1)S(1)}, bf16[64,256]{1,0:T(8,128)(2,1)S(1)}, u32[]{:S(2)}, u32[]{:S(2)}) collective-permute-start(bf16[64,256]{1,0:T(8,128)(2,1)S(1)} %add.37), channel_id=1, source_target_pairs={{0,256},{256,0},{1,257},{257,1},{2,258},{258,2},{3,259},{259,3},{4... | collective-permute-start | bytes 98312 | tf_op jit(solution)/shard_map/ppermute | solution.py:198
  43.8 5.2 %collective-permute-start.7 = (bf16[4,128,256]{2,1,0:T(8,128)(2,1)S(1)}, bf16[4,128,256]{2,1,0:T(8,128)(2,1)S(1)}, u32[]{:S(2)}, u32[]{:S(2)}) collective-permute-start(bf16[4,128,256]{2,1,0:T(8,128)(2,1)S(1)} %collective-permute-done.5), channel_id=1, source_target_pairs={{0,4},{1,29},{2,6},{3,31},{4,8},{5,1},{6,10},{7,3},{8,12},{9,5},{1... | collective-permute-start | bytes 786440 | tf_op jit(solution)/shard_map/ppermute | solution.py:205
  49.0 4.9 %shard_map.118 = (bf16[256,512]{1,0:T(8,128)(2,1)}, bf16[1536,512]{1,0:T(8,128)(2,1)}) custom-call(bf16[9,16]{1,0:T(8,128)(2,1)} %reshape.28.w1_ref, bf16[9,16,32]{2,1,0:T(8,128)(2,1)} %bitcast.35), custom_call_target="tpu_custom_call" | custom-call | flops 400000000 | bytes 2000000 | tf_op jit(solution)/shard_map/pallas_call | solution.py:52
  55.2 3.4 %collective-permute-start.8 = (bf16[64,256]{1,0:T(8,128)(2,1)S(1)}, bf16[64,256]{1,0:T(8,128)(2,1)S(1)}, u32[]{:S(2)}, u32[]{:S(2)}) collective-permute-start(bf16[64,256]{1,0:T(8,128)(2,1)S(1)} %add.38), channel_id=1, source_target_pairs={{0,32},{32,0},{1,33},{33,1},{2,34},{34,2},{3,35},{35,3},{4,36},{36... | collective-permute-start | bytes 98312 | tf_op jit(solution)/shard_map/ppermute | solution.py:229
  58.6 2.3 %all_gather.20.refs_0_ = bf16[8,128,256]{2,1,0:T(8,128)(2,1)} all-gather(bf16[4,128,256]{2,1,0:T(8,128)(2,1)S(1)} %constant_dynamic-update-slice_fusion), channel_id=1, replica_groups=mesh['xh'=2,'y'=4,'xl'=2,'z'=16,'c'=2] {'c'}, dimensions={0}, use_global_device_ids=true | all-gather | bytes 786432 | tf_op jit(solution)/shard_map/all_gather | solution.py:208
  61.6 5.5 %collective-permute-start.9 = (bf16[4,128,256]{2,1,0:T(8,128)(2,1)S(1)}, bf16[4,128,256]{2,1,0:T(8,128)(2,1)S(1)}, u32[]{:S(2)}, u32[]{:S(2)}) collective-permute-start(bf16[4,128,256]{2,1,0:T(8,128)(2,1)S(1)} %collective-permute-done.7), channel_id=1, source_target_pairs={{0,4},{1,29},{2,6},{3,31},{4,8},{5,1},{6,10},{7,3},{8,12},{9,5},{1... | collective-permute-start | bytes 786440 | tf_op jit(solution)/shard_map/ppermute | solution.py:205
  67.1 2.3 %all_gather.21.refs_1_ = bf16[8,128,256]{2,1,0:T(8,128)(2,1)} all-gather(bf16[4,128,256]{2,1,0:T(8,128)(2,1)S(1)} %collective-permute-done.5), channel_id=1, replica_groups=mesh['xh'=2,'y'=4,'xl'=2,'z'=16,'c'=2] {'c'}, dimensions={0}, use_global_device_ids=true | all-gather | bytes 786432 | tf_op jit(solution)/shard_map/all_gather | solution.py:208
  69.4 2.3 %all_gather.22.refs_2_ = bf16[8,128,256]{2,1,0:T(8,128)(2,1)} all-gather(bf16[4,128,256]{2,1,0:T(8,128)(2,1)S(1)} %collective-permute-done.7), channel_id=1, replica_groups=mesh['xh'=2,'y'=4,'xl'=2,'z'=16,'c'=2] {'c'}, dimensions={0}, use_global_device_ids=true | all-gather | bytes 786432 | tf_op jit(solution)/shard_map/all_gather | solution.py:208
  71.7 3.1 %collective-permute-done.9 = bf16[4,128,256]{2,1,0:T(8,128)(2,1)S(1)} collective-permute-done((bf16[4,128,256]{2,1,0:T(8,128)(2,1)S(1)}, bf16[4,128,256]{2,1,0:T(8,128)(2,1)S(1)}, u32[]{:S(2)}, u32[]{:S(2)}) %collective-permute-start.9) | collective-permute-done | bytes 262176 | tf_op jit(solution)/shard_map/ppermute | solution.py:205
  74.8 2.3 %all_gather.23.refs_3_ = bf16[8,128,256]{2,1,0:T(8,128)(2,1)} all-gather(bf16[4,128,256]{2,1,0:T(8,128)(2,1)S(1)} %collective-permute-done.9), channel_id=1, replica_groups=mesh['xh'=2,'y'=4,'xl'=2,'z'=16,'c'=2] {'c'}, dimensions={0}, use_global_device_ids=true | all-gather | bytes 786432 | tf_op jit(solution)/shard_map/all_gather | solution.py:208
  77.1 7.5 %shard_map.119 = (bf16[64,32]{1,0:T(8,128)(2,1)}, bf16[64,32]{1,0:T(8,128)(2,1)}) custom-call(s32[2]{0:T(128)} %pad_add_fusion.where_ref, bf16[128,256]{1,0:T(8,128)(2,1)} %pad_maximum_fusion.1.q_ref, bf16[2,128,256]{2,1,0:T(8,128)(2,1)} %bitcast.31, bf16[8,128,256]{2,1,0:T(8,128)(2,1)} %all_gather.20.refs_0_, bf16[8,128,256]{2,1,0:T(8,128)(2,1)} %all_gather.21.refs_1_, ...), custom_call_target="tpu_custom_call" | custom-call | flops 5000000000 | bytes 4000000 | tf_op jit(solution)/shard_map/pallas_call | solution.py:144
  84.6 3.4 %collective-permute-start.12 = (bf16[64,32]{1,0:T(8,128)(2,1)}, bf16[64,32]{1,0:T(8,128)(2,1)S(1)}, u32[]{:S(2)}, u32[]{:S(2)}) collective-permute-start(bf16[64,32]{1,0:T(8,128)(2,1)} %get-tuple-element.33), channel_id=1, source_target_pairs={{0,32},{32,0},{1,33},{33,1},{2,34},{34,2},{3,35},{35,3},{4,36},{36... | collective-permute-start | bytes 12296 | tf_op jit(solution)/shard_map/ppermute | solution.py:247
  88.0 3.2 %collective-permute-start.10 = (bf16[64,32]{1,0:T(8,128)(2,1)}, bf16[64,32]{1,0:T(8,128)(2,1)S(1)}, u32[]{:S(2)}, u32[]{:S(2)}) collective-permute-start(bf16[64,32]{1,0:T(8,128)(2,1)} %get-tuple-element.33), channel_id=1, source_target_pairs={{64,32},{32,64},{128,96},{96,128},{192,160},{160,192},{256,224},{2... | collective-permute-start | bytes 12296 | tf_op jit(solution)/shard_map/ppermute | solution.py:249
  91.2 1.9 %collective-permute-start.11 = (bf16[64,32]{1,0:T(8,128)(2,1)}, bf16[64,32]{1,0:T(8,128)(2,1)S(1)}, u32[]{:S(2)}, u32[]{:S(2)}) collective-permute-start(bf16[64,32]{1,0:T(8,128)(2,1)} %get-tuple-element.34), channel_id=1, source_target_pairs={{64,0},{32,96},{128,64},{96,160},{192,128},{160,224},{256,192},{22... | collective-permute-start | bytes 12296 | tf_op jit(solution)/shard_map/ppermute | solution.py:248
  94.8 5.9 %collective-permute-done.11 = bf16[64,32]{1,0:T(8,128)(2,1)S(1)} collective-permute-done((bf16[64,32]{1,0:T(8,128)(2,1)}, bf16[64,32]{1,0:T(8,128)(2,1)S(1)}, u32[]{:S(2)}, u32[]{:S(2)}) %collective-permute-start.11) | collective-permute-done | bytes 4128 | tf_op jit(solution)/shard_map/ppermute | solution.py:248
  (44 shorter events, 12.3 us)
Async XLA Ops:
  0.0 100.7 %copy-start = (bf16[32,512]{1,0:T(8,128)(2,1)S(1)}, bf16[32,512]{1,0:T(8,128)(2,1)}, u32[]{:S(2)}) copy-start(bf16[32,512]{1,0:T(8,128)(2,1)} %param.20) | copy-start | bytes 98308
  0.0 53.8 %copy-start.3 = (f32[16]{0:T(128)S(1)}, f32[16]{0:T(128)}, u32[]{:S(2)}) copy-start(f32[16]{0:T(128)} %param.17) | copy-start | bytes 196
  0.0 54.5 %copy-start.4 = (f32[32]{0:T(128)S(1)}, f32[32]{0:T(128)}, u32[]{:S(2)}) copy-start(f32[32]{0:T(128)} %param.19) | copy-start | bytes 388
  2.5 6.1 %collective-permute-start.1 = (bf16[64,256]{1,0:T(8,128)(2,1)S(1)}, bf16[64,256]{1,0:T(8,128)(2,1)S(1)}, u32[]{:S(2)}, u32[]{:S(2)}) collective-permute-start(bf16[64,256]{1,0:T(8,128)(2,1)S(1)} %convolution_convert_fusion), channel_id=1, source_target_pairs={{0,64},{64,0},{128,192},{192,128},{1,65},{65,1},{129,193},{193,129... | collective-permute-start | bytes 98312 | tf_op jit(solution)/shard_map/ppermute | solution.py:198
  5.1 5.8 %collective-permute-start = (bf16[64,256]{1,0:T(8,128)(2,1)S(1)}, bf16[64,256]{1,0:T(8,128)(2,1)S(1)}, u32[]{:S(2)}, u32[]{:S(2)}) collective-permute-start(bf16[64,256]{1,0:T(8,128)(2,1)S(1)} %get-tuple-element.20), channel_id=1, source_target_pairs={{0,32},{32,0},{1,33},{33,1},{2,34},{34,2},{3,35},{35,3},{4,36},{36... | collective-permute-start | bytes 98312 | tf_op jit(solution)/shard_map/ppermute | solution.py:210
  12.8 48.7 %copy-start.1 = (bf16[256,256]{1,0:T(8,128)(2,1)}, bf16[256,256]{1,0:T(8,128)(2,1)S(1)}, u32[]{:S(2)}) copy-start(bf16[256,256]{1,0:T(8,128)(2,1)S(1)} %all-gather) | copy-start | bytes 393220
  12.8 16.3 %collective-permute-start.2 = (bf16[2,128,256]{2,1,0:T(8,128)(2,1)S(1)}, bf16[2,128,256]{2,1,0:T(8,128)(2,1)S(1)}, u32[]{:S(2)}, u32[]{:S(2)}) collective-permute-start(bf16[2,128,256]{2,1,0:T(8,128)(2,1)S(1)} %bitcast.29), channel_id=1, source_target_pairs={{0,2},{1,31},{2,4},{3,1},{4,6},{5,3},{6,8},{7,5},{8,10},{9,7},{10,... | collective-permute-start | bytes 393224 | tf_op jit(solution)/shard_map/ppermute | solution.py:205
  16.7 15.3 %collective-permute-start.3 = (bf16[2,128,256]{2,1,0:T(8,128)(2,1)S(1)}, bf16[2,128,256]{2,1,0:T(8,128)(2,1)S(1)}, u32[]{:S(2)}, u32[]{:S(2)}) collective-permute-start(bf16[2,128,256]{2,1,0:T(8,128)(2,1)S(1)} %bitcast.30), channel_id=1, source_target_pairs={{0,4},{1,29},{2,6},{3,31},{4,8},{5,1},{6,10},{7,3},{8,12},{9,5},{1... | collective-permute-start | bytes 393224 | tf_op jit(solution)/shard_map/ppermute | solution.py:205
  21.8 7.3 %collective-permute-start.4 = (bf16[64,256]{1,0:T(8,128)(2,1)S(1)}, bf16[64,256]{1,0:T(8,128)(2,1)S(1)}, u32[]{:S(2)}, u32[]{:S(2)}) collective-permute-start(bf16[64,256]{1,0:T(8,128)(2,1)S(1)} %add.36), channel_id=1, source_target_pairs={{0,128},{64,192},{128,0},{192,64},{1,129},{65,193},{129,1},{193,65... | collective-permute-start | bytes 98312 | tf_op jit(solution)/shard_map/ppermute | solution.py:198
  32.0 11.8 %collective-permute-start.5 = (bf16[4,128,256]{2,1,0:T(8,128)(2,1)S(1)}, bf16[4,128,256]{2,1,0:T(8,128)(2,1)S(1)}, u32[]{:S(2)}, u32[]{:S(2)}) collective-permute-start(bf16[4,128,256]{2,1,0:T(8,128)(2,1)S(1)} %constant_dynamic-update-slice_fusion), channel_id=1, source_target_pairs={{0,4},{1,29},{2,6},{3,31},{4,8},{5,1},{6,10},{7,3},{8,12},{9,5},{1... | collective-permute-start | bytes 786440 | tf_op jit(solution)/shard_map/ppermute | solution.py:205
  36.4 7.3 %collective-permute-start.6 = (bf16[64,256]{1,0:T(8,128)(2,1)S(1)}, bf16[64,256]{1,0:T(8,128)(2,1)S(1)}, u32[]{:S(2)}, u32[]{:S(2)}) collective-permute-start(bf16[64,256]{1,0:T(8,128)(2,1)S(1)} %add.37), channel_id=1, source_target_pairs={{0,256},{256,0},{1,257},{257,1},{2,258},{258,2},{3,259},{259,3},{4... | collective-permute-start | bytes 98312 | tf_op jit(solution)/shard_map/ppermute | solution.py:198
  43.8 17.8 %collective-permute-start.7 = (bf16[4,128,256]{2,1,0:T(8,128)(2,1)S(1)}, bf16[4,128,256]{2,1,0:T(8,128)(2,1)S(1)}, u32[]{:S(2)}, u32[]{:S(2)}) collective-permute-start(bf16[4,128,256]{2,1,0:T(8,128)(2,1)S(1)} %collective-permute-done.5), channel_id=1, source_target_pairs={{0,4},{1,29},{2,6},{3,31},{4,8},{5,1},{6,10},{7,3},{8,12},{9,5},{1... | collective-permute-start | bytes 786440 | tf_op jit(solution)/shard_map/ppermute | solution.py:205
  55.2 5.8 %collective-permute-start.8 = (bf16[64,256]{1,0:T(8,128)(2,1)S(1)}, bf16[64,256]{1,0:T(8,128)(2,1)S(1)}, u32[]{:S(2)}, u32[]{:S(2)}) collective-permute-start(bf16[64,256]{1,0:T(8,128)(2,1)S(1)} %add.38), channel_id=1, source_target_pairs={{0,32},{32,0},{1,33},{33,1},{2,34},{34,2},{3,35},{35,3},{4,36},{36... | collective-permute-start | bytes 98312 | tf_op jit(solution)/shard_map/ppermute | solution.py:229
  61.6 13.2 %collective-permute-start.9 = (bf16[4,128,256]{2,1,0:T(8,128)(2,1)S(1)}, bf16[4,128,256]{2,1,0:T(8,128)(2,1)S(1)}, u32[]{:S(2)}, u32[]{:S(2)}) collective-permute-start(bf16[4,128,256]{2,1,0:T(8,128)(2,1)S(1)} %collective-permute-done.7), channel_id=1, source_target_pairs={{0,4},{1,29},{2,6},{3,31},{4,8},{5,1},{6,10},{7,3},{8,12},{9,5},{1... | collective-permute-start | bytes 786440 | tf_op jit(solution)/shard_map/ppermute | solution.py:205
  77.1 23.6 %copy-start.5 = (f32[512]{0:T(512)S(1)}, f32[512]{0:T(512)}, u32[]{:S(2)}) copy-start(f32[512]{0:T(512)} %param.21) | copy-start | bytes 6148
  77.1 23.8 %copy-start.2 = (f32[512]{0:T(512)S(1)}, f32[512]{0:T(512)}, u32[]{:S(2)}) copy-start(f32[512]{0:T(512)} %param.23) | copy-start | bytes 6148
  84.6 8.5 %collective-permute-start.12 = (bf16[64,32]{1,0:T(8,128)(2,1)}, bf16[64,32]{1,0:T(8,128)(2,1)S(1)}, u32[]{:S(2)}, u32[]{:S(2)}) collective-permute-start(bf16[64,32]{1,0:T(8,128)(2,1)} %get-tuple-element.33), channel_id=1, source_target_pairs={{0,32},{32,0},{1,33},{33,1},{2,34},{34,2},{3,35},{35,3},{4,36},{36... | collective-permute-start | bytes 12296 | tf_op jit(solution)/shard_map/ppermute | solution.py:247
  88.0 6.7 %collective-permute-start.10 = (bf16[64,32]{1,0:T(8,128)(2,1)}, bf16[64,32]{1,0:T(8,128)(2,1)S(1)}, u32[]{:S(2)}, u32[]{:S(2)}) collective-permute-start(bf16[64,32]{1,0:T(8,128)(2,1)} %get-tuple-element.33), channel_id=1, source_target_pairs={{64,32},{32,64},{128,96},{96,128},{192,160},{160,192},{256,224},{2... | collective-permute-start | bytes 12296 | tf_op jit(solution)/shard_map/ppermute | solution.py:249
  91.2 9.5 %collective-permute-start.11 = (bf16[64,32]{1,0:T(8,128)(2,1)}, bf16[64,32]{1,0:T(8,128)(2,1)S(1)}, u32[]{:S(2)}, u32[]{:S(2)}) collective-permute-start(bf16[64,32]{1,0:T(8,128)(2,1)} %get-tuple-element.34), channel_id=1, source_target_pairs={{64,0},{32,96},{128,64},{96,160},{192,128},{160,224},{256,192},{22... | collective-permute-start | bytes 12296 | tf_op jit(solution)/shard_map/ppermute | solution.py:248

commit v2 on v1

--- a/solution.py
+++ b/solution.py
@@ -19,45 +19,118 @@
 INTERPRET = False
 
 
-def weights_kernel(w1_ref, w2_ref, a_ref, b_ref):
-    def iota(shape, dim):
-        return lax.broadcasted_iota(jnp.int32, shape, dim)
-
-    pick = (iota((CH1, ROW1), 1) % CH1 == iota((CH1, ROW1), 0)).astype(BF)
-    w1_wide = jnp.dot(w1_ref[...], pick, preferred_element_type=F32)
+def iota(shape, dim):
+    return lax.broadcasted_iota(jnp.int32, shape, dim)
+
+
+def first_kernel(where_ref, maps_ref, table_ref, start_ref, rows_ref, out_ref, mine_ref):
+    x, frame_block = where_ref[0], where_ref[2]
+    cells = table_ref.shape[1]
+    frames_here = maps_ref.shape[0]
+    mine_ref[...] = maps_ref[x]
+    out_ref[0:cells, :] = maps_ref[1 - x]
+    low = frame_block * frames_here
+    owned = (start_ref[...] >= low) & (start_ref[...] < low + frames_here)
+    row = jnp.where(owned, rows_ref[...], -1)
+    chosen = (iota((cells, row.shape[1]), 0) == row).astype(BF)
+    got = lax.dot_general(
+        chosen, table_ref[0], (((0,), (0,)), ((), ())), preferred_element_type=F32
+    )
+    out_ref[cells:, :] = got.astype(BF)
+
+
+def first_message(where, frame_maps, query_table, start_frame, row_ids):
+    cells, channels = frame_maps.shape[1:]
+    count = start_frame.shape[0]
+    vmem = pl.BlockSpec(memory_space=pltpu.VMEM)
+    return pl.pallas_call(
+        first_kernel,
+        out_shape=(
+            jax.ShapeDtypeStruct((cells + count, channels), BF),
+            jax.ShapeDtypeStruct((cells, channels), BF),
+        ),
+        in_specs=[pl.BlockSpec(memory_space=pltpu.SMEM)] + [vmem] * 4,
+        out_specs=(vmem, vmem),
+        cost_estimate=pl.CostEstimate(flops=2_000_000, bytes_accessed=200_000, transcendentals=0),
+        compiler_params=pltpu.CompilerParams(vmem_limit_bytes=4 << 20),
+        interpret=INTERPRET,
+    )(where, frame_maps, query_table, start_frame[None, :], row_ids[None, :])
+
+
+def merge_kernel(message_ref, mine_ref, theirs_ref, block_ref, queries_ref):
+    cells = mine_ref.shape[0]
+    block_ref[0:cells, :] = mine_ref[...]
+    block_ref[cells:, :] = theirs_ref[0:cells, :]
+    count = message_ref.shape[0] - cells
+    queries_ref[0:count, :] = message_ref[cells:, :]
+    queries_ref[count:, :] = theirs_ref[cells:, :]
+
+
+def merged(message, mine, theirs):
+    cells, channels = mine.shape
+    count = message.shape[0] - cells
+    vmem = pl.BlockSpec(memory_space=pltpu.VMEM)
+    return pl.pallas_call(
+        merge_kernel,
+        out_shape=(
+            jax.ShapeDtypeStruct((2 * cells, channels), BF),
+            jax.ShapeDtypeStruct((2 * count, channels), BF),
+        ),
+        in_specs=[vmem] * 3,
+        out_specs=(vmem, vmem),
+        cost_estimate=pl.CostEstimate(flops=0, bytes_accessed=300_000, transcendentals=0),
+        compiler_params=pltpu.CompilerParams(vmem_limit_bytes=4 << 20),
+        interpret=INTERPRET,
+    )(message, mine, theirs)
+
+
+def weights_kernel(w1_ref, w2_ref, bias1_ref, bias2_ref, a_ref, b_ref, wide1_ref, wide2_ref):
+    spread = (iota((CH1, ROW1), 1) % CH1 == iota((CH1, ROW1), 0)).astype(BF)
+    wide1_ref[...] = jnp.concatenate([bias1_ref[...]] * HALF1, axis=1)
+    wide2_ref[...] = jnp.concatenate([bias2_ref[...]] * HALF2, axis=1)
+
     in_x = iota((MAP, ROW1), 0)
     out_x = iota((MAP, ROW1), 1) // CH1
     a_ref[0:MAP, :] = jnp.zeros((MAP, ROW1), BF)
     for dy in range(3):
+        wide = jnp.dot(w1_ref[dy], spread, preferred_element_type=F32)
         block = jnp.zeros((MAP, ROW1), F32)
         for dx in range(3):
-            tap = w1_wide[3 * dy + dx : 3 * dy + dx + 1, :]
-            block = jnp.where(in_x == 2 * out_x + dx - 1, tap, block)
+            block = jnp.where(in_x == 2 * out_x + dx - 1, wide[dx : dx + 1, :], block)
         a_ref[MAP * (dy + 1) : MAP * (dy + 2), :] = block.astype(BF)
 
-    rows = (iota((ROW1, CH1), 0) % CH1 == iota((ROW1, CH1), 1)).astype(BF)
-    cols = (iota((CH2, ROW2), 1) % CH2 == iota((CH2, ROW2), 0)).astype(BF)
-    in_x = iota((ROW1, ROW2), 0) // CH1
-    out_x = iota((ROW1, ROW2), 1) // CH2
+    b_ref[...] = jnp.zeros(b_ref.shape, BF)
     for dy in range(3):
-        block = jnp.zeros((ROW1, ROW2), F32)
-        for dx in range(3):
-            wide = jnp.dot(w2_ref[3 * dy + dx], cols, preferred_element_type=F32).astype(BF)
-            tall = jnp.dot(rows, wide, preferred_element_type=F32)
-            block = jnp.where(in_x == 2 * out_x + dx - 1, tall, block)
-        b_ref[ROW1 * dy : ROW1 * (dy + 1), :] = block.astype(BF)
-
-
-def banded_weights(conv1_w, conv2_w):
+        taps = jnp.concatenate([w2_ref[3 * dy + dx] for dx in range(3)], axis=0)
+        taps = jnp.concatenate([taps] * (128 // CH2), axis=1)
+        for out_x in range(HALF2):
+            low = 2 * out_x - 1
+            skip = max(0, -low)
+            lane = CH2 * out_x
+            part = lane % 128
+            b_ref[
+                ROW1 * dy + CH1 * (low + skip) : ROW1 * dy + CH1 * (low + 3), lane : lane + CH2
+            ] = taps[CH1 * skip :, part : part + CH2]
+
+
+def banded_weights(conv1_w, conv1_b, conv2_w, conv2_b):
     return pl.pallas_call(
         weights_kernel,
         out_shape=(
             jax.ShapeDtypeStruct((4 * MAP, ROW1), BF),
             jax.ShapeDtypeStruct((3 * ROW1, ROW2), BF),
+            jax.ShapeDtypeStruct((1, ROW1), F32),
+            jax.ShapeDtypeStruct((1, ROW2), F32),
         ),
-        cost_estimate=pl.CostEstimate(flops=400_000_000, bytes_accessed=2_000_000, transcendentals=0),
-        interpret=INTERPRET,
-    )(conv1_w.reshape(9, CH1), conv2_w.reshape(9, CH1, CH2))
+        cost_estimate=pl.CostEstimate(flops=50_000_000, bytes_accessed=2_000_000, transcendentals=0),
+        compiler_params=pltpu.CompilerParams(vmem_limit_bytes=8 << 20),
+        interpret=INTERPRET,
+    )(
+        jnp.transpose(conv1_w, (0, 2, 1, 3)).reshape(3, 3, CH1),
+        conv2_w.reshape(9, CH1, CH2),
+        conv1_b[None, :],
+        conv2_b[None, :],
+    )
 
 
 def cost_kernel(z_count, where_ref, q_ref, own_ref, *refs):
@@ -154,8 +227,63 @@
         cost_estimate=pl.CostEstimate(
             flops=5_000_000_000, bytes_accessed=4_000_000, transcendentals=0
         ),
+        compiler_params=pltpu.CompilerParams(vmem_limit_bytes=28 << 20),
         interpret=INTERPRET,
     )(where, queries, own, *far, a, b, bias1, bias2)
+
+
+def tail_kernel(
+    frame_count,
+    where_ref,
+    kept_ref,
+    partner_ref,
+    straight_ref,
+    crossed_ref,
+    proj_w_ref,
+    proj_b_ref,
+    time_w_ref,
+    time_b_ref,
+    out_ref,
+):
+    x, frame_block = where_ref[0], where_ref[2]
+    first = x == 0
+    kept, partner = kept_ref[...], partner_ref[...]
+    straight, crossed = straight_ref[...], crossed_ref[...]
+    around = [
+        jnp.where(first, crossed, straight),
+        jnp.where(first, kept, partner),
+        jnp.where(first, partner, kept),
+        jnp.where(first, straight, crossed),
+    ]
+    valid = [frame_block > 0, None, None, frame_block < frame_count - 1]
+    wide = []
+    for pooled, there in zip(around, valid):
+        got = jnp.dot(pooled, proj_w_ref[...], preferred_element_type=F32) + proj_b_ref[...]
+        got = got.astype(BF).astype(F32)
+        if there is not None:
+            got = jnp.where(there, got, 0.0)
+        wide.append(got)
+    for t in range(2):
+        mixed = (
+            time_w_ref[0:1, :] * wide[t]
+            + time_w_ref[1:2, :] * wide[t + 1]
+            + time_w_ref[2:3, :] * wide[t + 2]
+            + time_b_ref[...]
+        )
+        out_ref[:, t, :] = mixed.astype(BF)
+
+
+def tail(frame_count, where, pooled, proj_w, proj_b, time_w, time_b):
+    count, width = pooled[0].shape[0], proj_w.shape[1]
+    vmem = pl.BlockSpec(memory_space=pltpu.VMEM)
+    return pl.pallas_call(
+        functools.partial(tail_kernel, frame_count),
+        out_shape=jax.ShapeDtypeStruct((count, 2, width), BF),
+        in_specs=[pl.BlockSpec(memory_space=pltpu.SMEM)] + [vmem] * 8,
+        out_specs=vmem,
+        compiler_params=pltpu.CompilerParams(vmem_limit_bytes=8 << 20),
+        interpret=INTERPRET,
+    )(where, *pooled, proj_w, proj_b[None, :], time_w, time_b[None, :])
 
 
 def per_device(
@@ -178,21 +306,8 @@
     x = lax.axis_index("xl")
     z = lax.axis_index("z")
     frame_block = lax.axis_index("xh") * y_count + lax.axis_index("y")
-    where = jnp.stack([x, z]).astype(jnp.int32)
+    where = jnp.stack([x, z, frame_block]).astype(jnp.int32)
     swap = [(0, 1), (1, 0)]
-
-    a, b = banded_weights(conv1_w, conv2_w)
-    bias1 = jnp.tile(conv1_b, HALF1)[None, :]
-    bias2 = jnp.tile(conv2_b, HALF2)[None, :]
-
-    mine = jnp.where(x == 0, frame_maps[0], frame_maps[1])
-    other = jnp.where(x == 0, frame_maps[1], frame_maps[0])
-
-    cells_here = query_table.shape[1]
-    owned = start_frame // frame_maps.shape[0] == frame_block
-    chosen = (row_ids[:, None] == jnp.arange(cells_here)[None, :]) & owned[:, None]
-    queries = jnp.dot(chosen.astype(BF), query_table[0], preferred_element_type=F32).astype(BF)
-    other, queries = lax.optimization_barrier((other, queries))
 
     def flip(axis, count, step):
         return lambda v: lax.ppermute(v, axis, [(i, i ^ step) for i in range(count)])
@@ -207,33 +322,35 @@
     def both(block):
         return lax.all_gather(block, "c", axis=0, tiled=True)
 
-    theirs = lax.ppermute(other, "xl", swap)
-    got = flip("y", y_count, 1)(queries)
-    theirs, queries = lax.optimization_barrier((theirs, queries + got))
-
-    own = lax.all_gather(jnp.concatenate([mine, theirs], axis=0), "c", axis=0)
+    message, mine = first_message(where, frame_maps, query_table, start_frame, row_ids)
+    theirs = lax.ppermute(message, "xl", swap)
+    weights = banded_weights(conv1_w, conv1_b, conv2_w, conv2_b)
+    theirs, weights = lax.optimization_barrier((theirs, weights))
+
+    block, queries = merged(message, mine, theirs)
+    own = lax.all_gather(block, "c", axis=0)
+    own, queries = lax.optimization_barrier((own, queries))
     near, next_near = along(own, 1), along(own, 2)
+    queries = queries + flip("y", y_count, 1)(queries)
+    near, next_near, queries = lax.optimization_barrier((near, next_near, queries))
+
+    moving = [jnp.concatenate([near, next_near], axis=0)]
+    moving.append(along(moving[-1], 2))
     if y_count > 2:
         queries = queries + flip("y", y_count, 2)(queries)
-    near, next_near, queries = lax.optimization_barrier((near, next_near, queries))
-
-    moving = jnp.concatenate([near, next_near], axis=0)
-    far = [both(moving)]
-    moving = along(moving, 2)
+    moving, queries = lax.optimization_barrier((moving, queries))
+
+    moving.append(along(moving[-1], 2))
     if xh_count > 1:
         queries = queries + flip("xh", xh_count, 1)(queries)
     moving, queries = lax.optimization_barrier((moving, queries))
 
-    far.append(both(moving))
-    moving = along(moving, 2)
-    queries = jnp.concatenate([queries, lax.ppermute(queries, "xl", swap)], axis=0)
-    moving, queries = lax.optimization_barrier((moving, queries))
-
-    far.append(both(moving))
-    moving = along(moving, 2)
-    far.append(both(moving))
-
-    kept, sent = pooled_costs(where, queries, own, far, a, b, bias1, bias2)
+    last = along(moving[-1], 2)
+    far = [both(v) for v in moving]
+    last, far = lax.optimization_barrier((last, far))
+    far.append(both(last))
+
+    kept, sent = pooled_costs(where, queries, own, far, *weights)
 
     def frame_pairs(cross):
         pairs = []
@@ -247,23 +364,8 @@
     partner = lax.ppermute(sent, "xl", swap)
     straight = lax.ppermute(kept, ("xh", "y", "xl"), frame_pairs(False))
     crossed = lax.ppermute(sent, ("xh", "y", "xl"), frame_pairs(True))
-    first = x == 0
-    around = jnp.stack(
-        [
-            jnp.where(first, crossed, straight),
-            jnp.where(first, kept, partner),
-            jnp.where(first, partner, kept),
-            jnp.where(first, straight, crossed),
-        ]
-    )
-    projected = lax.reduce_precision(
-        jnp.einsum("fqc,cd->fqd", around, proj_w, preferred_element_type=F32) + proj_b, 8, 7
-    )
-    index = jnp.arange(4)
-    valid = ((index > 0) | (frame_block > 0)) & ((index < 3) | (frame_block < frame_count - 1))
-    wide = jnp.where(valid[:, None, None], projected, 0.0)
-    mixed = time_w[0] * wide[:-2] + time_w[1] * wide[1:-1] + time_w[2] * wide[2:] + time_b
-    return jnp.transpose(mixed, (1, 0, 2)).astype(BF)
+    pooled = (kept, partner, straight, crossed)
+    return tail(frame_count, where, pooled, proj_w, proj_b, time_w, time_b)
 
 
 def solution(mesh):

time: 103 us -> 92.2 us (0.90)
  Pallas kernels: 12.4 us -> 7.89 us
  other arithmetic: 3.65 us -> 0.13 us
  starting transfers between devices: 49.2 us -> 47.2 us
  local copies, waits for them, and re-layouts: 4.26 us -> 5.7 us
  matrix products: 1.18 us -> 0 us
    ppermute x3, waiting for transfers between devices: 4.7 us -> 11.4 us  [flip(): lax.ppermute(v, axis, [(i, i ^ step) for i in range(count)])]
    ppermute x1, waiting for transfers between devices: 5.88 us -> 0.01 us  [per_device(): straight = lax.ppermute(kept, ('xh', 'y', 'xl'), frame_pairs(False))]
    unnamed x13 -> x25, local copies, waits for them, and re-layouts: 0.03 us -> 5.69 us
    pallas_call x1, Pallas kernels: 4.86 us -> 0.31 us  [banded_weights(): pl.pallas_call(weights_kernel, out_shape=(jax.ShapeDtypeStruct((4 * MAP,...]
    ppermute x2 -> x1, starting transfers between devices: 6.79 us -> 3.4 us  [per_device(): theirs = lax.ppermute(message, 'xl', swap)]
    ppermute x2 -> x1, waiting for transfers between devices: 2.45 us -> 0.01 us  [per_device(): theirs = lax.ppermute(message, 'xl', swap)]
    pallas_call x0 -> x3, Pallas kernels: none -> 2.25 us  [the longest x1 1.52 us: tail(): pl.pallas_call(functools.partial(tail_kernel, frame_count), out_shape=jax...]
    pallas_call x1, Pallas kernels: 7.5 us -> 5.32 us  [pooled_costs(): pl.pallas_call(functools.partial(cost_kernel, z_count), out_shape=(jax.Sh...]
  transfers between devices with their start and end apart: 13 -> 12, of which waited for: 8 -> 8; matrix products, arithmetic and copies ran while one was open for 5% -> 0% of each run, Pallas kernels for 5% -> 0%
where the time goes in v2:
time: 92.2 us; the launch traced here: 90.7 us
  starting transfers between devices  47.2 us (51%)
  waiting for transfers between devices  19 us (21%)
  blocking collectives  10.6 us (11%)
  Pallas kernels  7.89 us (9%)
  local copies, waits for them, and re-layouts  5.7 us (6%)
    ppermute x5, starting transfers between devices, along(): return lax.ppermute(block, ('z', 'c'), pairs)  22.1 us
    ppermute x3, waiting for transfers between devices, flip(): lax.ppermute(v, axis, [(i, i ^ step) for i in range(count)])  11.4 us
    ppermute x3, starting transfers between devices, flip(): lax.ppermute(v, axis, [(i, i ^ step) for i in range(count)])  10.4 us
    all_gather x4, blocking collectives, both(): return lax.all_gather(block, 'c', axis=0, tiled=True)  8.69 us
    ppermute x5, waiting for transfers between devices, along(): return lax.ppermute(block, ('z', 'c'), pairs)  5.82 us
    unnamed x25, local copies, waits for them, and re-layouts  5.69 us
    pallas_call x1, Pallas kernels, pooled_costs(): pl.pallas_call(functools.partial(cost_kernel, z_count), out_shape=(jax.Sh...  5.32 us
    ppermute x1, starting transfers between devices, per_device(): partner = lax.ppermute(sent, 'xl', swap)  4.9 us
  transfers between devices with their start and end apart: 12, of which 8 were waited for; matrix products, arithmetic and copies ran while one was open for 0% of the time, Pallas kernels for 0%

profile of v2, /device:TPU:24, one launch (start us, length us, event | category | flops | bytes accessed | tf_op | source)
XLA Modules:
  0.0 90.7 jit_solution(11416930482572998365)
XLA Ops:
  3.7 3.4 %collective-permute-start = (bf16[128,256]{1,0:T(8,128)(2,1)S(1)}, bf16[128,256]{1,0:T(8,128)(2,1)S(1)}, u32[]{:S(2)}, u32[]{:S(2)}) collective-permute-start(bf16[128,256]{1,0:T(8,128)(2,1)S(1)} %get-tuple-element.36.message_ref), channel_id=1, source_target_pairs={{0,32},{32,0},{1,33},{33,1},{2,34},{34,2},{3,35},{35,3},{4,36},{36... | collective-permute-start | bytes 196616 | tf_op jit(solution)/shard_map/ppermute | solution.py:326
  10.2 1.9 %all-gather = bf16[256,256]{1,0:T(8,128)(2,1)S(1)} all-gather(bf16[128,256]{1,0:T(8,128)(2,1)S(1)} %get-tuple-element.43), channel_id=2, replica_groups=mesh['xh'=2,'y'=4,'xl'=2,'z'=16,'c'=2] {'c'}, dimensions={0}, use_global_device_ids=true | all-gather | bytes 196608 | tf_op jit(solution)/shard_map/all_gather | solution.py:331
  12.1 5.2 %collective-permute-start.2 = (bf16[2,128,256]{2,1,0:T(8,128)(2,1)S(1)}, bf16[2,128,256]{2,1,0:T(8,128)(2,1)S(1)}, u32[]{:S(2)}, u32[]{:S(2)}) collective-permute-start(bf16[2,128,256]{2,1,0:T(8,128)(2,1)S(1)} %bitcast.12), channel_id=1, source_target_pairs={{0,4},{1,29},{2,6},{3,31},{4,8},{5,1},{6,10},{7,3},{8,12},{9,5},{1... | collective-permute-start | bytes 393224 | tf_op jit(solution)/shard_map/ppermute | solution.py:320
  17.3 3.8 %collective-permute-start.1 = (bf16[2,128,256]{2,1,0:T(8,128)(2,1)S(1)}, bf16[2,128,256]{2,1,0:T(8,128)(2,1)S(1)}, u32[]{:S(2)}, u32[]{:S(2)}) collective-permute-start(bf16[2,128,256]{2,1,0:T(8,128)(2,1)S(1)} %bitcast.13), channel_id=1, source_target_pairs={{0,2},{1,31},{2,4},{3,1},{4,6},{5,3},{6,8},{7,5},{8,10},{9,7},{10,... | collective-permute-start | bytes 393224 | tf_op jit(solution)/shard_map/ppermute | solution.py:320
  21.2 2.7 %collective-permute-start.3 = (bf16[128,256]{1,0:T(8,128)(2,1)S(1)}, bf16[128,256]{1,0:T(8,128)(2,1)S(1)}, u32[]{:S(2)}, u32[]{:S(2)}) collective-permute-start(bf16[128,256]{1,0:T(8,128)(2,1)S(1)} %get-tuple-element.46), channel_id=1, source_target_pairs={{0,64},{64,0},{128,192},{192,128},{1,65},{65,1},{129,193},{193,129... | collective-permute-start | bytes 196616 | tf_op jit(solution)/shard_map/ppermute | solution.py:313
  23.8 3.5 %collective-permute-done.3 = bf16[128,256]{1,0:T(8,128)(2,1)S(1)} collective-permute-done((bf16[128,256]{1,0:T(8,128)(2,1)S(1)}, bf16[128,256]{1,0:T(8,128)(2,1)S(1)}, u32[]{:S(2)}, u32[]{:S(2)}) %collective-permute-start.3) | collective-permute-done | bytes 65568 | tf_op jit(solution)/shard_map/ppermute | solution.py:313
  27.3 1.9 %collective-permute-done.1 = bf16[2,128,256]{2,1,0:T(8,128)(2,1)S(1)} collective-permute-done((bf16[2,128,256]{2,1,0:T(8,128)(2,1)S(1)}, bf16[2,128,256]{2,1,0:T(8,128)(2,1)S(1)}, u32[]{:S(2)}, u32[]{:S(2)}) %collective-permute-start.1) | collective-permute-done | bytes 131104 | tf_op jit(solution)/shard_map/ppermute | solution.py:320
  29.3 4.5 %collective-permute-start.4 = (bf16[4,128,256]{2,1,0:T(8,128)(2,1)S(1)}, bf16[4,128,256]{2,1,0:T(8,128)(2,1)S(1)}, u32[]{:S(2)}, u32[]{:S(2)}) collective-permute-start(bf16[4,128,256]{2,1,0:T(8,128)(2,1)S(1)} %constant_dynamic-update-slice_fusion), channel_id=1, source_target_pairs={{0,4},{1,29},{2,6},{3,31},{4,8},{5,1},{6,10},{7,3},{8,12},{9,5},{1... | collective-permute-start | bytes 786440 | tf_op jit(solution)/shard_map/ppermute | solution.py:320
  33.8 3.1 %collective-permute-start.5 = (bf16[128,256]{1,0:T(8,128)(2,1)S(1)}, bf16[128,256]{1,0:T(8,128)(2,1)S(1)}, u32[]{:S(2)}, u32[]{:S(2)}) collective-permute-start(bf16[128,256]{1,0:T(8,128)(2,1)S(1)} %add.13), channel_id=1, source_target_pairs={{0,128},{64,192},{128,0},{192,64},{1,129},{65,193},{129,1},{193,65... | collective-permute-start | bytes 196616 | tf_op jit(solution)/shard_map/ppermute | solution.py:313
  36.9 4.5 %collective-permute-done.5 = bf16[128,256]{1,0:T(8,128)(2,1)S(1)} collective-permute-done((bf16[128,256]{1,0:T(8,128)(2,1)S(1)}, bf16[128,256]{1,0:T(8,128)(2,1)S(1)}, u32[]{:S(2)}, u32[]{:S(2)}) %collective-permute-start.5) | collective-permute-done | bytes 65568 | tf_op jit(solution)/shard_map/ppermute | solution.py:313
  42.5 4.1 %collective-permute-start.6 = (bf16[4,128,256]{2,1,0:T(8,128)(2,1)S(1)}, bf16[4,128,256]{2,1,0:T(8,128)(2,1)S(1)}, u32[]{:S(2)}, u32[]{:S(2)}) collective-permute-start(bf16[4,128,256]{2,1,0:T(8,128)(2,1)S(1)} %collective-permute-done.4), channel_id=1, source_target_pairs={{0,4},{1,29},{2,6},{3,31},{4,8},{5,1},{6,10},{7,3},{8,12},{9,5},{1... | collective-permute-start | bytes 786440 | tf_op jit(solution)/shard_map/ppermute | solution.py:320
  46.7 4.6 %collective-permute-start.7 = (bf16[128,256]{1,0:T(8,128)(2,1)S(1)}, bf16[128,256]{1,0:T(8,128)(2,1)S(1)}, u32[]{:S(2)}, u32[]{:S(2)}) collective-permute-start(bf16[128,256]{1,0:T(8,128)(2,1)S(1)} %add.14), channel_id=1, source_target_pairs={{0,256},{256,0},{1,257},{257,1},{2,258},{258,2},{3,259},{259,3},{4... | collective-permute-start | bytes 196616 | tf_op jit(solution)/shard_map/ppermute | solution.py:313
  51.3 3.4 %collective-permute-done.7 = bf16[128,256]{1,0:T(8,128)(2,1)S(1)} collective-permute-done((bf16[128,256]{1,0:T(8,128)(2,1)S(1)}, bf16[128,256]{1,0:T(8,128)(2,1)S(1)}, u32[]{:S(2)}, u32[]{:S(2)}) %collective-permute-start.7) | collective-permute-done | bytes 65568 | tf_op jit(solution)/shard_map/ppermute | solution.py:313
  55.4 4.5 %collective-permute-start.8 = (bf16[4,128,256]{2,1,0:T(8,128)(2,1)S(1)}, bf16[4,128,256]{2,1,0:T(8,128)(2,1)S(1)}, u32[]{:S(2)}, u32[]{:S(2)}) collective-permute-start(bf16[4,128,256]{2,1,0:T(8,128)(2,1)S(1)} %collective-permute-done.6), channel_id=1, source_target_pairs={{0,4},{1,29},{2,6},{3,31},{4,8},{5,1},{6,10},{7,3},{8,12},{9,5},{1... | collective-permute-start | bytes 786440 | tf_op jit(solution)/shard_map/ppermute | solution.py:320
  59.9 2.2 %all_gather.22.refs_2_ = bf16[8,128,256]{2,1,0:T(8,128)(2,1)S(1)} all-gather(bf16[4,128,256]{2,1,0:T(8,128)(2,1)S(1)} %collective-permute-done.6), channel_id=1, replica_groups=mesh['xh'=2,'y'=4,'xl'=2,'z'=16,'c'=2] {'c'}, dimensions={0}, use_global_device_ids=true | all-gather | bytes 786432 | tf_op jit(solution)/shard_map/all_gather | solution.py:323
  62.1 2.2 %all_gather.20.refs_0_ = bf16[8,128,256]{2,1,0:T(8,128)(2,1)S(1)} all-gather(bf16[4,128,256]{2,1,0:T(8,128)(2,1)S(1)} %constant_dynamic-update-slice_fusion), channel_id=1, replica_groups=mesh['xh'=2,'y'=4,'xl'=2,'z'=16,'c'=2] {'c'}, dimensions={0}, use_global_device_ids=true | all-gather | bytes 786432 | tf_op jit(solution)/shard_map/all_gather | solution.py:323
  64.2 2.2 %all_gather.21.refs_1_ = bf16[8,128,256]{2,1,0:T(8,128)(2,1)S(1)} all-gather(bf16[4,128,256]{2,1,0:T(8,128)(2,1)S(1)} %collective-permute-done.4), channel_id=1, replica_groups=mesh['xh'=2,'y'=4,'xl'=2,'z'=16,'c'=2] {'c'}, dimensions={0}, use_global_device_ids=true | all-gather | bytes 786432 | tf_op jit(solution)/shard_map/all_gather | solution.py:323
  66.4 2.2 %collective-permute-done.8 = bf16[4,128,256]{2,1,0:T(8,128)(2,1)S(1)} collective-permute-done((bf16[4,128,256]{2,1,0:T(8,128)(2,1)S(1)}, bf16[4,128,256]{2,1,0:T(8,128)(2,1)S(1)}, u32[]{:S(2)}, u32[]{:S(2)}) %collective-permute-start.8) | collective-permute-done | bytes 262176 | tf_op jit(solution)/shard_map/ppermute | solution.py:320
  68.6 2.2 %all_gather.23.refs_3_ = bf16[8,128,256]{2,1,0:T(8,128)(2,1)S(1)} all-gather(bf16[4,128,256]{2,1,0:T(8,128)(2,1)S(1)} %collective-permute-done.8), channel_id=1, replica_groups=mesh['xh'=2,'y'=4,'xl'=2,'z'=16,'c'=2] {'c'}, dimensions={0}, use_global_device_ids=true | all-gather | bytes 786432 | tf_op jit(solution)/shard_map/all_gather | solution.py:323
  70.8 5.3 %shard_map.121 = (bf16[64,32]{1,0:T(8,128)(2,1)S(1)}, bf16[64,32]{1,0:T(8,128)(2,1)S(1)}) custom-call(s32[3]{0:T(128)S(1)} %pad_add_fusion.where_ref, bf16[128,256]{1,0:T(8,128)(2,1)S(1)} %add.15.q_ref, bf16[2,128,256]{2,1,0:T(8,128)(2,1)S(1)} %bitcast.14, bf16[8,128,256]{2,1,0:T(8,128)(2,1)S(1)} %all_gather.20.refs_0_, ...), custom_call_target="tpu_custom_call" | custom-call | flops 5000000000 | bytes 4000000 | tf_op jit(solution)/shard_map/pallas_call | solution.py:217
  76.1 2.7 %collective-permute-start.10 = (bf16[64,32]{1,0:T(8,128)(2,1)S(1)}, bf16[64,32]{1,0:T(8,128)(2,1)S(1)}, u32[]{:S(2)}, u32[]{:S(2)}) collective-permute-start(bf16[64,32]{1,0:T(8,128)(2,1)S(1)} %get-tuple-element.65.kept_ref), channel_id=1, source_target_pairs={{64,0},{32,96},{128,64},{96,160},{192,128},{160,224},{256,192},{22... | collective-permute-start | bytes 12296 | tf_op jit(solution)/shard_map/ppermute | solution.py:365
  78.8 3.8 %collective-permute-start.11 = (bf16[64,32]{1,0:T(8,128)(2,1)S(1)}, bf16[64,32]{1,0:T(8,128)(2,1)S(1)}, u32[]{:S(2)}, u32[]{:S(2)}) collective-permute-start(bf16[64,32]{1,0:T(8,128)(2,1)S(1)} %get-tuple-element.66), channel_id=1, source_target_pairs={{64,32},{32,64},{128,96},{96,128},{192,160},{160,192},{256,224},{2... | collective-permute-start | bytes 12296 | tf_op jit(solution)/shard_map/ppermute | solution.py:366
  82.6 4.9 %collective-permute-start.9 = (bf16[64,32]{1,0:T(8,128)(2,1)S(1)}, bf16[64,32]{1,0:T(8,128)(2,1)S(1)}, u32[]{:S(2)}, u32[]{:S(2)}) collective-permute-start(bf16[64,32]{1,0:T(8,128)(2,1)S(1)} %get-tuple-element.66), channel_id=1, source_target_pairs={{0,32},{32,0},{1,33},{33,1},{2,34},{34,2},{3,35},{35,3},{4,36},{36... | collective-permute-start | bytes 12296 | tf_op jit(solution)/shard_map/ppermute | solution.py:364
  87.5 1.7 %collective-permute-done.9.partner_ref = bf16[64,32]{1,0:T(8,128)(2,1)S(1)} collective-permute-done((bf16[64,32]{1,0:T(8,128)(2,1)S(1)}, bf16[64,32]{1,0:T(8,128)(2,1)S(1)}, u32[]{:S(2)}, u32[]{:S(2)}) %collective-permute-start.9) | collective-permute-done | bytes 4128 | tf_op jit(solution)/shard_map/ppermute | solution.py:364
  (40 shorter events, 10.1 us)
Async XLA Ops:
  0.1 0.8 copy-start
  0.9 0.8 copy-start.1
  1.7 0.7 copy-start.6
  2.3 0.7 copy-start.7
  3.7 6.5 %collective-permute-start = (bf16[128,256]{1,0:T(8,128)(2,1)S(1)}, bf16[128,256]{1,0:T(8,128)(2,1)S(1)}, u32[]{:S(2)}, u32[]{:S(2)}) collective-permute-start(bf16[128,256]{1,0:T(8,128)(2,1)S(1)} %get-tuple-element.36.message_ref), channel_id=1, source_target_pairs={{0,32},{32,0},{1,33},{33,1},{2,34},{34,2},{3,35},{35,3},{4,36},{36... | collective-permute-start | bytes 196616 | tf_op jit(solution)/shard_map/ppermute | solution.py:326
  7.1 0.8 copy-start.8
  7.9 0.7 copy-start.9
  8.6 0.7 copy-start.10
  9.2 0.7 copy-start.11
  12.1 15.2 %collective-permute-start.2 = (bf16[2,128,256]{2,1,0:T(8,128)(2,1)S(1)}, bf16[2,128,256]{2,1,0:T(8,128)(2,1)S(1)}, u32[]{:S(2)}, u32[]{:S(2)}) collective-permute-start(bf16[2,128,256]{2,1,0:T(8,128)(2,1)S(1)} %bitcast.12), channel_id=1, source_target_pairs={{0,4},{1,29},{2,6},{3,31},{4,8},{5,1},{6,10},{7,3},{8,12},{9,5},{1... | collective-permute-start | bytes 393224 | tf_op jit(solution)/shard_map/ppermute | solution.py:320
  17.3 12.0 %collective-permute-start.1 = (bf16[2,128,256]{2,1,0:T(8,128)(2,1)S(1)}, bf16[2,128,256]{2,1,0:T(8,128)(2,1)S(1)}, u32[]{:S(2)}, u32[]{:S(2)}) collective-permute-start(bf16[2,128,256]{2,1,0:T(8,128)(2,1)S(1)} %bitcast.13), channel_id=1, source_target_pairs={{0,2},{1,31},{2,4},{3,1},{4,6},{5,3},{6,8},{7,5},{8,10},{9,7},{10,... | collective-permute-start | bytes 393224 | tf_op jit(solution)/shard_map/ppermute | solution.py:320
  21.2 6.2 %collective-permute-start.3 = (bf16[128,256]{1,0:T(8,128)(2,1)S(1)}, bf16[128,256]{1,0:T(8,128)(2,1)S(1)}, u32[]{:S(2)}, u32[]{:S(2)}) collective-permute-start(bf16[128,256]{1,0:T(8,128)(2,1)S(1)} %get-tuple-element.46), channel_id=1, source_target_pairs={{0,64},{64,0},{128,192},{192,128},{1,65},{65,1},{129,193},{193,129... | collective-permute-start | bytes 196616 | tf_op jit(solution)/shard_map/ppermute | solution.py:313
  29.3 13.2 %collective-permute-start.4 = (bf16[4,128,256]{2,1,0:T(8,128)(2,1)S(1)}, bf16[4,128,256]{2,1,0:T(8,128)(2,1)S(1)}, u32[]{:S(2)}, u32[]{:S(2)}) collective-permute-start(bf16[4,128,256]{2,1,0:T(8,128)(2,1)S(1)} %constant_dynamic-update-slice_fusion), channel_id=1, source_target_pairs={{0,4},{1,29},{2,6},{3,31},{4,8},{5,1},{6,10},{7,3},{8,12},{9,5},{1... | collective-permute-start | bytes 786440 | tf_op jit(solution)/shard_map/ppermute | solution.py:320
  33.8 7.7 %collective-permute-start.5 = (bf16[128,256]{1,0:T(8,128)(2,1)S(1)}, bf16[128,256]{1,0:T(8,128)(2,1)S(1)}, u32[]{:S(2)}, u32[]{:S(2)}) collective-permute-start(bf16[128,256]{1,0:T(8,128)(2,1)S(1)} %add.13), channel_id=1, source_target_pairs={{0,128},{64,192},{128,0},{192,64},{1,129},{65,193},{129,1},{193,65... | collective-permute-start | bytes 196616 | tf_op jit(solution)/shard_map/ppermute | solution.py:313
  42.5 12.8 %collective-permute-start.6 = (bf16[4,128,256]{2,1,0:T(8,128)(2,1)S(1)}, bf16[4,128,256]{2,1,0:T(8,128)(2,1)S(1)}, u32[]{:S(2)}, u32[]{:S(2)}) collective-permute-start(bf16[4,128,256]{2,1,0:T(8,128)(2,1)S(1)} %collective-permute-done.4), channel_id=1, source_target_pairs={{0,4},{1,29},{2,6},{3,31},{4,8},{5,1},{6,10},{7,3},{8,12},{9,5},{1... | collective-permute-start | bytes 786440 | tf_op jit(solution)/shard_map/ppermute | solution.py:320
  46.7 8.1 %collective-permute-start.7 = (bf16[128,256]{1,0:T(8,128)(2,1)S(1)}, bf16[128,256]{1,0:T(8,128)(2,1)S(1)}, u32[]{:S(2)}, u32[]{:S(2)}) collective-permute-start(bf16[128,256]{1,0:T(8,128)(2,1)S(1)} %add.14), channel_id=1, source_target_pairs={{0,256},{256,0},{1,257},{257,1},{2,258},{258,2},{3,259},{259,3},{4... | collective-permute-start | bytes 196616 | tf_op jit(solution)/shard_map/ppermute | solution.py:313
  55.4 13.2 %collective-permute-start.8 = (bf16[4,128,256]{2,1,0:T(8,128)(2,1)S(1)}, bf16[4,128,256]{2,1,0:T(8,128)(2,1)S(1)}, u32[]{:S(2)}, u32[]{:S(2)}) collective-permute-start(bf16[4,128,256]{2,1,0:T(8,128)(2,1)S(1)} %collective-permute-done.6), channel_id=1, source_target_pairs={{0,4},{1,29},{2,6},{3,31},{4,8},{5,1},{6,10},{7,3},{8,12},{9,5},{1... | collective-permute-start | bytes 786440 | tf_op jit(solution)/shard_map/ppermute | solution.py:320
  70.8 18.4 %copy-start.2 = (bf16[32,512]{1,0:T(8,128)(2,1)S(1)}, bf16[32,512]{1,0:T(8,128)(2,1)}, u32[]{:S(2)}) copy-start(bf16[32,512]{1,0:T(8,128)(2,1)} %proj_w_ref.1) | copy-start | bytes 98308
  70.8 18.4 %copy-start.3 = (f32[3,512]{1,0:T(4,128)S(1)}, f32[3,512]{1,0:T(4,128)}, u32[]{:S(2)}) copy-start(f32[3,512]{1,0:T(4,128)} %time_w_ref.1) | copy-start | bytes 18436
  70.8 18.4 %copy-start.4 = (f32[512]{0:T(512)S(1)}, f32[512]{0:T(512)}, u32[]{:S(2)}) copy-start(f32[512]{0:T(512)} %param.21) | copy-start | bytes 6148
  70.8 18.4 %copy-start.5 = (f32[512]{0:T(512)S(1)}, f32[512]{0:T(512)}, u32[]{:S(2)}) copy-start(f32[512]{0:T(512)} %param.23) | copy-start | bytes 6148
  76.1 11.3 %collective-permute-start.10 = (bf16[64,32]{1,0:T(8,128)(2,1)S(1)}, bf16[64,32]{1,0:T(8,128)(2,1)S(1)}, u32[]{:S(2)}, u32[]{:S(2)}) collective-permute-start(bf16[64,32]{1,0:T(8,128)(2,1)S(1)} %get-tuple-element.65.kept_ref), channel_id=1, source_target_pairs={{64,0},{32,96},{128,64},{96,160},{192,128},{160,224},{256,192},{22... | collective-permute-start | bytes 12296 | tf_op jit(solution)/shard_map/ppermute | solution.py:365
  78.8 8.7 %collective-permute-start.11 = (bf16[64,32]{1,0:T(8,128)(2,1)S(1)}, bf16[64,32]{1,0:T(8,128)(2,1)S(1)}, u32[]{:S(2)}, u32[]{:S(2)}) collective-permute-start(bf16[64,32]{1,0:T(8,128)(2,1)S(1)} %get-tuple-element.66), channel_id=1, source_target_pairs={{64,32},{32,64},{128,96},{96,128},{192,160},{160,192},{256,224},{2... | collective-permute-start | bytes 12296 | tf_op jit(solution)/shard_map/ppermute | solution.py:366
  82.6 6.6 %collective-permute-start.9 = (bf16[64,32]{1,0:T(8,128)(2,1)S(1)}, bf16[64,32]{1,0:T(8,128)(2,1)S(1)}, u32[]{:S(2)}, u32[]{:S(2)}) collective-permute-start(bf16[64,32]{1,0:T(8,128)(2,1)S(1)} %get-tuple-element.66), channel_id=1, source_target_pairs={{0,32},{32,0},{1,33},{33,1},{2,34},{34,2},{3,35},{35,3},{4,36},{36... | collective-permute-start | bytes 12296 | tf_op jit(solution)/shard_map/ppermute | solution.py:364

commit v3 on v2

--- a/solution.py
+++ b/solution.py
@@ -6,6 +6,7 @@
 from jax.experimental import pallas as pl
 from jax.experimental.pallas import tpu as pltpu
 from jax.sharding import Mesh, PartitionSpec as P
+
 
 MAP = 64
 CH1 = 16
@@ -23,68 +24,83 @@
     return lax.broadcasted_iota(jnp.int32, shape, dim)
 
 
-def first_kernel(where_ref, maps_ref, table_ref, start_ref, rows_ref, out_ref, mine_ref):
-    x, frame_block = where_ref[0], where_ref[2]
-    cells = table_ref.shape[1]
-    frames_here = maps_ref.shape[0]
-    mine_ref[...] = maps_ref[x]
-    out_ref[0:cells, :] = maps_ref[1 - x]
-    low = frame_block * frames_here
-    owned = (start_ref[...] >= low) & (start_ref[...] < low + frames_here)
-    row = jnp.where(owned, rows_ref[...], -1)
-    chosen = (iota((cells, row.shape[1]), 0) == row).astype(BF)
-    got = lax.dot_general(
-        chosen, table_ref[0], (((0,), (0,)), ((), ())), preferred_element_type=F32
-    )
-    out_ref[cells:, :] = got.astype(BF)
-
-
-def first_message(where, frame_maps, query_table, start_frame, row_ids):
-    cells, channels = frame_maps.shape[1:]
+def in_hbm(array):
+    if INTERPRET:
+        return array
+    return pltpu.with_memory_space_constraint(array, pltpu.HBM)
+
+
+def query_kernel(where_ref, table_hbm, start_hbm, rows_hbm, out_ref, table, start, rows, sems):
+    frames_here = 2
+    copies = [
+        pltpu.make_async_copy(table_hbm, table, sems.at[0]),
+        pltpu.make_async_copy(start_hbm, start, sems.at[1]),
+        pltpu.make_async_copy(rows_hbm, rows, sems.at[2]),
+    ]
+    for copy in copies:
+        copy.start()
+    for copy in copies:
+        copy.wait()
+    low = where_ref[2] * frames_here
+    owned = (start[...] >= low) & (start[...] < low + frames_here)
+    row = jnp.where(owned, rows[...], -1)
+    chosen = (iota((table.shape[1], row.shape[1]), 0) == row).astype(BF)
+    got = lax.dot_general(chosen, table[0], (((0,), (0,)), ((), ())), preferred_element_type=F32)
+    out_ref[...] = got.astype(BF)
+
+
+def own_queries(where, query_table, start_frame, row_ids):
     count = start_frame.shape[0]
-    vmem = pl.BlockSpec(memory_space=pltpu.VMEM)
+    hbm = pl.BlockSpec(memory_space=pltpu.HBM)
     return pl.pallas_call(
-        first_kernel,
-        out_shape=(
-            jax.ShapeDtypeStruct((cells + count, channels), BF),
-            jax.ShapeDtypeStruct((cells, channels), BF),
-        ),
-        in_specs=[pl.BlockSpec(memory_space=pltpu.SMEM)] + [vmem] * 4,
-        out_specs=(vmem, vmem),
+        query_kernel,
+        out_shape=jax.ShapeDtypeStruct((count, query_table.shape[2]), BF),
+        in_specs=[pl.BlockSpec(memory_space=pltpu.SMEM)] + [hbm] * 3,
+        out_specs=pl.BlockSpec(memory_space=pltpu.VMEM),
+        scratch_shapes=[
+            pltpu.VMEM(query_table.shape, BF),
+            pltpu.VMEM((1, count), jnp.int32),
+            pltpu.VMEM((1, count), jnp.int32),
+            pltpu.SemaphoreType.DMA((3,)),
+        ],
         cost_estimate=pl.CostEstimate(flops=2_000_000, bytes_accessed=200_000, transcendentals=0),
         compiler_params=pltpu.CompilerParams(vmem_limit_bytes=4 << 20),
         interpret=INTERPRET,
-    )(where, frame_maps, query_table, start_frame[None, :], row_ids[None, :])
-
-
-def merge_kernel(message_ref, mine_ref, theirs_ref, block_ref, queries_ref):
-    cells = mine_ref.shape[0]
-    block_ref[0:cells, :] = mine_ref[...]
-    block_ref[cells:, :] = theirs_ref[0:cells, :]
-    count = message_ref.shape[0] - cells
-    queries_ref[0:count, :] = message_ref[cells:, :]
-    queries_ref[count:, :] = theirs_ref[cells:, :]
-
-
-def merged(message, mine, theirs):
-    cells, channels = mine.shape
-    count = message.shape[0] - cells
+    )(where, *map(in_hbm, (query_table, start_frame[None, :], row_ids[None, :])))
+
+
+def pick_kernel(where_ref, all_ref, out_ref):
+    x = where_ref[0]
+    cells = all_ref.shape[2]
+    for core in range(2):
+        for side in range(2):
+            out_ref[core, cells * side : cells * (side + 1), :] = all_ref[2 * side + core, x]
+
+
+def picked(where, gathered):
+    cells, channels = gathered.shape[2:]
     vmem = pl.BlockSpec(memory_space=pltpu.VMEM)
     return pl.pallas_call(
-        merge_kernel,
-        out_shape=(
-            jax.ShapeDtypeStruct((2 * cells, channels), BF),
-            jax.ShapeDtypeStruct((2 * count, channels), BF),
-        ),
-        in_specs=[vmem] * 3,
-        out_specs=(vmem, vmem),
+        pick_kernel,
+        out_shape=jax.ShapeDtypeStruct((2, 2 * cells, channels), BF),
+        in_specs=[pl.BlockSpec(memory_space=pltpu.SMEM), vmem],
+        out_specs=vmem,
         cost_estimate=pl.CostEstimate(flops=0, bytes_accessed=300_000, transcendentals=0),
         compiler_params=pltpu.CompilerParams(vmem_limit_bytes=4 << 20),
         interpret=INTERPRET,
-    )(message, mine, theirs)
-
-
-def weights_kernel(w1_ref, w2_ref, bias1_ref, bias2_ref, a_ref, b_ref, wide1_ref, wide2_ref):
+    )(where, gathered)
+
+
+def weights_kernel(*refs):
+    a_ref, b_ref, wide1_ref, wide2_ref, w1_ref, w2_ref, bias1_ref, bias2_ref, sems = refs[4:]
+    copies = [
+        pltpu.make_async_copy(refs[k], refs[8 + k], sems.at[k]) for k in range(4)
+    ]
+    for copy in copies:
+        copy.start()
+    b_ref[...] = jnp.zeros(b_ref.shape, BF)
+    for copy in copies:
+        copy.wait()
     spread = (iota((CH1, ROW1), 1) % CH1 == iota((CH1, ROW1), 0)).astype(BF)
     wide1_ref[...] = jnp.concatenate([bias1_ref[...]] * HALF1, axis=1)
     wide2_ref[...] = jnp.concatenate([bias2_ref[...]] * HALF2, axis=1)
@@ -99,7 +115,6 @@
             block = jnp.where(in_x == 2 * out_x + dx - 1, wide[dx : dx + 1, :], block)
         a_ref[MAP * (dy + 1) : MAP * (dy + 2), :] = block.astype(BF)
 
-    b_ref[...] = jnp.zeros(b_ref.shape, BF)
     for dy in range(3):
         taps = jnp.concatenate([w2_ref[3 * dy + dx] for dx in range(3)], axis=0)
         taps = jnp.concatenate([taps] * (128 // CH2), axis=1)
@@ -122,25 +137,38 @@
             jax.ShapeDtypeStruct((1, ROW1), F32),
             jax.ShapeDtypeStruct((1, ROW2), F32),
         ),
+        in_specs=[pl.BlockSpec(memory_space=pltpu.HBM)] * 4,
+        scratch_shapes=[
+            pltpu.VMEM((3, 3, CH1), BF),
+            pltpu.VMEM((9, CH1, CH2), BF),
+            pltpu.VMEM((1, CH1), F32),
+            pltpu.VMEM((1, CH2), F32),
+            pltpu.SemaphoreType.DMA((4,)),
+        ],
         cost_estimate=pl.CostEstimate(flops=50_000_000, bytes_accessed=2_000_000, transcendentals=0),
         compiler_params=pltpu.CompilerParams(vmem_limit_bytes=8 << 20),
         interpret=INTERPRET,
     )(
-        jnp.transpose(conv1_w, (0, 2, 1, 3)).reshape(3, 3, CH1),
-        conv2_w.reshape(9, CH1, CH2),
-        conv1_b[None, :],
-        conv2_b[None, :],
+        *map(
+            in_hbm,
+            (
+                jnp.transpose(conv1_w, (0, 2, 1, 3)).reshape(3, 3, CH1),
+                conv2_w.reshape(9, CH1, CH2),
+                conv1_b[None, :],
+                conv2_b[None, :],
+            ),
+        )
     )
 
 
-def cost_kernel(z_count, where_ref, q_ref, own_ref, *refs):
+def cost_kernel(z_count, where_ref, kept_q_ref, sent_q_ref, own_ref, *refs):
     far_refs = refs[:-9]
     a_ref, b_ref, bias1_ref, bias2_ref, kept_ref, sent_ref, corr, hid, acc = refs[-9:]
-    x, z = where_ref[0], where_ref[1]
-    n = q_ref.shape[0]
+    z = where_ref[1]
+    n = 2 * kept_q_ref.shape[0]
     corr[0, :, 0:128] = jnp.zeros((n, 128), BF)
     hid[0, :, 0:ROW1] = jnp.zeros((n, ROW1), BF)
-    q = q_ref[...]
+    q = jnp.concatenate([kept_q_ref[...], sent_q_ref[...]], axis=0)
 
     def put(low, high, chip):
         cells = jnp.concatenate([low[0:MAP], high[0:MAP], low[MAP:], high[MAP:]], axis=0)
@@ -148,7 +176,7 @@
         got = (got * 0.0625).astype(BF)
         for side in range(2):
             part = got[:, 128 * side : 128 * (side + 1)]
-            y = (x if side == 0 else 1 - x) * z_count + chip
+            y = side * z_count + chip
             corr[y, :, 128:256] = part
             corr[y + 1, :, 0:128] = part
 
@@ -209,15 +237,15 @@
     sent_ref[...] = pooled[n // 2 :]
 
 
-def pooled_costs(where, queries, own, far, a, b, bias1, bias2):
-    n = queries.shape[0]
+def pooled_costs(where, kept_q, sent_q, own, far, a, b, bias1, bias2):
+    n = 2 * kept_q.shape[0]
     z_count = MAP // 4
     vmem = pl.BlockSpec(memory_space=pltpu.VMEM)
 
     return pl.pallas_call(
         functools.partial(cost_kernel, z_count),
         out_shape=(jax.ShapeDtypeStruct((n // 2, CH2), BF),) * 2,
-        in_specs=[pl.BlockSpec(memory_space=pltpu.SMEM)] + [vmem] * (6 + len(far)),
+        in_specs=[pl.BlockSpec(memory_space=pltpu.SMEM)] + [vmem] * (7 + len(far)),
         out_specs=(vmem, vmem),
         scratch_shapes=[
             pltpu.VMEM((HALF1 + 1, n, 256), BF),
@@ -229,7 +257,7 @@
         ),
         compiler_params=pltpu.CompilerParams(vmem_limit_bytes=28 << 20),
         interpret=INTERPRET,
-    )(where, queries, own, *far, a, b, bias1, bias2)
+    )(where, kept_q, sent_q, own, *far, a, b, bias1, bias2)
 
 
 def tail_kernel(
@@ -286,7 +314,7 @@
     )(where, *pooled, proj_w, proj_b[None, :], time_w, time_b[None, :])
 
 
-def per_device(
+def one_device(
     sizes,
     frame_maps,
     query_table,
@@ -322,35 +350,40 @@
     def both(block):
         return lax.all_gather(block, "c", axis=0, tiled=True)
 
-    message, mine = first_message(where, frame_maps, query_table, start_frame, row_ids)
-    theirs = lax.ppermute(message, "xl", swap)
+    def behind(value, earlier):
+        return lax.optimization_barrier((value, earlier))[0]
+
+    gathered = lax.all_gather(frame_maps, ("xl", "c"), axis=0)
+    own = picked(where, gathered)
     weights = banded_weights(conv1_w, conv1_b, conv2_w, conv2_b)
-    theirs, weights = lax.optimization_barrier((theirs, weights))
-
-    block, queries = merged(message, mine, theirs)
-    own = lax.all_gather(block, "c", axis=0)
-    own, queries = lax.optimization_barrier((own, queries))
-    near, next_near = along(own, 1), along(own, 2)
-    queries = queries + flip("y", y_count, 1)(queries)
-    near, next_near, queries = lax.optimization_barrier((near, next_near, queries))
-
-    moving = [jnp.concatenate([near, next_near], axis=0)]
-    moving.append(along(moving[-1], 2))
+    near = along(own, 1)
+    next_near = along(own, 2)
+    queries = own_queries(where, query_table, start_frame, row_ids)
+    queries = queries + flip("y", y_count, 1)(behind(queries, own))
+    near, next_near, weights = lax.optimization_barrier((near, next_near, weights))
+
+    far = []
+    moving = jnp.concatenate([near, next_near], axis=0)
     if y_count > 2:
-        queries = queries + flip("y", y_count, 2)(queries)
-    moving, queries = lax.optimization_barrier((moving, queries))
-
-    moving.append(along(moving[-1], 2))
+        queries = queries + flip("y", y_count, 2)(behind(queries, moving))
+    far.append(both(moving))
+    moving = along(moving, 2)
+    moving, far = lax.optimization_barrier((moving, far))
+
     if xh_count > 1:
-        queries = queries + flip("xh", xh_count, 1)(queries)
-    moving, queries = lax.optimization_barrier((moving, queries))
-
-    last = along(moving[-1], 2)
-    far = [both(v) for v in moving]
-    last, far = lax.optimization_barrier((last, far))
-    far.append(both(last))
-
-    kept, sent = pooled_costs(where, queries, own, far, *weights)
+        queries = queries + flip("xh", xh_count, 1)(behind(queries, moving))
+    far.append(both(moving))
+    moving = along(moving, 2)
+    moving, far = lax.optimization_barrier((moving, far))
+
+    kept_q = queries
+    sent_q = lax.ppermute(behind(queries, moving), "xl", swap)
+    far.append(both(moving))
+    moving = along(moving, 2)
+    moving, far = lax.optimization_barrier((moving, far))
+    far.append(both(moving))
+
+    kept, sent = pooled_costs(where, kept_q, sent_q, own, far, *weights)
 
     def frame_pairs(cross):
         pairs = []
@@ -377,7 +410,7 @@
     qs = ("xl", "z", "c")
     placed = (P(fr, qs, None), P(fr, qs, None), P(qs), P(qs)) + (P(),) * 8
     return jax.shard_map(
-        functools.partial(per_device, sizes),
+        functools.partial(one_device, sizes),
         mesh=fine,
         in_specs=placed,
         out_specs=P(qs, fr, None),

time: 92.2 us -> 103 us (1.12)
  the two profiles are of different devices: /device:TPU:24 before, /device:TPU:68 now
where the time goes in v3:
time: 103 us
  starting transfers between devices  53.7 us (52%)
  waiting for transfers between devices  24 us (23%)
  blocking collectives  14.7 us (14%)
  Pallas kernels  10 us (10%)
    ppermute x5, starting transfers between devices, along(): return lax.ppermute(block, ('z', 'c'), pairs)  29.6 us
    ppermute x3, starting transfers between devices, flip(): lax.ppermute(v, axis, [(i, i ^ step) for i in range(count)])  10.8 us
    ppermute x5, waiting for transfers between devices, along(): return lax.ppermute(block, ('z', 'c'), pairs)  10.5 us
    ppermute x3, waiting for transfers between devices, flip(): lax.ppermute(v, axis, [(i, i ^ step) for i in range(count)])  9.78 us
    all_gather x4, blocking collectives, both(): return lax.all_gather(block, 'c', axis=0, tiled=True)  8.71 us
    all_gather x1, blocking collectives, one_device(): gathered = lax.all_gather(frame_maps, ('xl', 'c'), axis=0)  5.97 us
    pallas_call x1, Pallas kernels, pooled_costs(): pl.pallas_call(functools.partial(cost_kernel, z_count), out_shape=(jax.Sh...  5.29 us
    ppermute x1, starting transfers between devices, one_device(): straight = lax.ppermute(kept, ('xh', 'y', 'xl'), frame_pairs(False))  4.97 us
  transfers between devices with their start and end apart: 12, of which 8 were waited for; matrix products, arithmetic and copies ran while one was open for 0% of the time, Pallas kernels for 3%

profile of v3, /device:TPU:68, one launch (start us, length us, event | category | flops | bytes accessed | tf_op | source)
XLA Modules:
  0.0 102.8 jit_solution(7034310908136611457)
XLA Ops:
  0.0 6.0 %all-gather = bf16[8,64,256]{2,1,0:T(8,128)(2,1)S(1)} all-gather(bf16[2,64,256]{2,1,0:T(8,128)(2,1)} %param.12), channel_id=2, replica_groups=mesh['xh'=2,'y'=4,'xl'=2,'z'=16,'c'=2] {'xl','c'}, dimensions={0}, use_global_device_ids=true | all-gather | bytes 327680 | tf_op jit(solution)/shard_map/all_gather | solution.py:356
  6.6 6.4 %collective-permute-start.2 = (bf16[2,128,256]{2,1,0:T(8,128)(2,1)S(1)}, bf16[2,128,256]{2,1,0:T(8,128)(2,1)S(1)}, u32[]{:S(2)}, u32[]{:S(2)}) collective-permute-start(bf16[2,128,256]{2,1,0:T(8,128)(2,1)S(1)} %shard_map.119.own_ref), channel_id=1, source_target_pairs={{0,4},{1,29},{2,6},{3,31},{4,8},{5,1},{6,10},{7,3},{8,12},{9,5},{1... | collective-permute-start | bytes 393224 | tf_op jit(solution)/shard_map/ppermute | solution.py:348
  13.0 3.8 %collective-permute-start.1 = (bf16[2,128,256]{2,1,0:T(8,128)(2,1)S(1)}, bf16[2,128,256]{2,1,0:T(8,128)(2,1)S(1)}, u32[]{:S(2)}, u32[]{:S(2)}) collective-permute-start(bf16[2,128,256]{2,1,0:T(8,128)(2,1)S(1)} %shard_map.119.own_ref), channel_id=1, source_target_pairs={{0,2},{1,31},{2,4},{3,1},{4,6},{5,3},{6,8},{7,5},{8,10},{9,7},{10,... | collective-permute-start | bytes 393224 | tf_op jit(solution)/shard_map/ppermute | solution.py:348
  19.9 6.4 %collective-permute-start.4 = (bf16[4,128,256]{2,1,0:T(8,128)(2,1)S(1)}, bf16[4,128,256]{2,1,0:T(8,128)(2,1)S(1)}, u32[]{:S(2)}, u32[]{:S(2)}) collective-permute-start(bf16[4,128,256]{2,1,0:T(8,128)(2,1)S(1)} %constant_dynamic-update-slice_fusion), channel_id=1, source_target_pairs={{0,4},{1,29},{2,6},{3,31},{4,8},{5,1},{6,10},{7,3},{8,12},{9,5},{1... | collective-permute-start | bytes 786440 | tf_op jit(solution)/shard_map/ppermute | solution.py:348
  26.3 2.2 %all_gather.20.refs_0_ = bf16[8,128,256]{2,1,0:T(8,128)(2,1)S(1)} all-gather(bf16[4,128,256]{2,1,0:T(8,128)(2,1)S(1)} %constant_dynamic-update-slice_fusion), channel_id=1, replica_groups=mesh['xh'=2,'y'=4,'xl'=2,'z'=16,'c'=2] {'c'}, dimensions={0}, use_global_device_ids=true | all-gather | bytes 786432 | tf_op jit(solution)/shard_map/all_gather | solution.py:351
  28.5 4.2 %collective-permute-done.4 = bf16[4,128,256]{2,1,0:T(8,128)(2,1)S(1)} collective-permute-done((bf16[4,128,256]{2,1,0:T(8,128)(2,1)S(1)}, bf16[4,128,256]{2,1,0:T(8,128)(2,1)S(1)}, u32[]{:S(2)}, u32[]{:S(2)}) %collective-permute-start.4) | collective-permute-done | bytes 262176 | tf_op jit(solution)/shard_map/ppermute | solution.py:348
  32.7 6.5 %collective-permute-start.6 = (bf16[4,128,256]{2,1,0:T(8,128)(2,1)S(1)}, bf16[4,128,256]{2,1,0:T(8,128)(2,1)S(1)}, u32[]{:S(2)}, u32[]{:S(2)}) collective-permute-start(bf16[4,128,256]{2,1,0:T(8,128)(2,1)S(1)} %collective-permute-done.4), channel_id=1, source_target_pairs={{0,4},{1,29},{2,6},{3,31},{4,8},{5,1},{6,10},{7,3},{8,12},{9,5},{1... | collective-permute-start | bytes 786440 | tf_op jit(solution)/shard_map/ppermute | solution.py:348
  39.2 2.2 %all_gather.21.refs_1_ = bf16[8,128,256]{2,1,0:T(8,128)(2,1)S(1)} all-gather(bf16[4,128,256]{2,1,0:T(8,128)(2,1)S(1)} %collective-permute-done.4), channel_id=1, replica_groups=mesh['xh'=2,'y'=4,'xl'=2,'z'=16,'c'=2] {'c'}, dimensions={0}, use_global_device_ids=true | all-gather | bytes 786432 | tf_op jit(solution)/shard_map/all_gather | solution.py:351
  41.4 4.4 %collective-permute-done.6 = bf16[4,128,256]{2,1,0:T(8,128)(2,1)S(1)} collective-permute-done((bf16[4,128,256]{2,1,0:T(8,128)(2,1)S(1)}, bf16[4,128,256]{2,1,0:T(8,128)(2,1)S(1)}, u32[]{:S(2)}, u32[]{:S(2)}) %collective-permute-start.6) | collective-permute-done | bytes 262176 | tf_op jit(solution)/shard_map/ppermute | solution.py:348
  45.8 6.5 %collective-permute-start.8 = (bf16[4,128,256]{2,1,0:T(8,128)(2,1)S(1)}, bf16[4,128,256]{2,1,0:T(8,128)(2,1)S(1)}, u32[]{:S(2)}, u32[]{:S(2)}) collective-permute-start(bf16[4,128,256]{2,1,0:T(8,128)(2,1)S(1)} %collective-permute-done.6), channel_id=1, source_target_pairs={{0,4},{1,29},{2,6},{3,31},{4,8},{5,1},{6,10},{7,3},{8,12},{9,5},{1... | collective-permute-start | bytes 786440 | tf_op jit(solution)/shard_map/ppermute | solution.py:348
  53.9 3.5 %collective-permute-start = (bf16[64,256]{1,0:T(8,128)(2,1)S(1)}, bf16[64,256]{1,0:T(8,128)(2,1)S(1)}, u32[]{:S(2)}, u32[]{:S(2)}) collective-permute-start(bf16[64,256]{1,0:T(8,128)(2,1)S(1)} %shard_map.118), channel_id=1, source_target_pairs={{0,64},{64,0},{128,192},{192,128},{1,65},{65,1},{129,193},{193,129... | collective-permute-start | bytes 98312 | tf_op jit(solution)/shard_map/ppermute | solution.py:341
  57.4 2.5 %collective-permute-done = bf16[64,256]{1,0:T(8,128)(2,1)S(1)} collective-permute-done((bf16[64,256]{1,0:T(8,128)(2,1)S(1)}, bf16[64,256]{1,0:T(8,128)(2,1)S(1)}, u32[]{:S(2)}, u32[]{:S(2)}) %collective-permute-start) | collective-permute-done | bytes 32800 | tf_op jit(solution)/shard_map/ppermute | solution.py:341
  59.9 4.9 %collective-permute-start.3 = (bf16[64,256]{1,0:T(8,128)(2,1)S(1)}, bf16[64,256]{1,0:T(8,128)(2,1)S(1)}, u32[]{:S(2)}, u32[]{:S(2)}) collective-permute-start(bf16[64,256]{1,0:T(8,128)(2,1)S(1)} %add.13), channel_id=1, source_target_pairs={{0,128},{64,192},{128,0},{192,64},{1,129},{65,193},{129,1},{193,65... | collective-permute-start | bytes 98312 | tf_op jit(solution)/shard_map/ppermute | solution.py:341
  64.8 2.4 %collective-permute-done.3 = bf16[64,256]{1,0:T(8,128)(2,1)S(1)} collective-permute-done((bf16[64,256]{1,0:T(8,128)(2,1)S(1)}, bf16[64,256]{1,0:T(8,128)(2,1)S(1)}, u32[]{:S(2)}, u32[]{:S(2)}) %collective-permute-start.3) | collective-permute-done | bytes 32800 | tf_op jit(solution)/shard_map/ppermute | solution.py:341
  67.2 2.4 %collective-permute-start.5 = (bf16[64,256]{1,0:T(8,128)(2,1)S(1)}, bf16[64,256]{1,0:T(8,128)(2,1)S(1)}, u32[]{:S(2)}, u32[]{:S(2)}) collective-permute-start(bf16[64,256]{1,0:T(8,128)(2,1)S(1)} %add.14), channel_id=1, source_target_pairs={{0,256},{256,0},{1,257},{257,1},{2,258},{258,2},{3,259},{259,3},{4... | collective-permute-start | bytes 98312 | tf_op jit(solution)/shard_map/ppermute | solution.py:341
  69.7 4.9 %collective-permute-done.5 = bf16[64,256]{1,0:T(8,128)(2,1)S(1)} collective-permute-done((bf16[64,256]{1,0:T(8,128)(2,1)S(1)}, bf16[64,256]{1,0:T(8,128)(2,1)S(1)}, u32[]{:S(2)}, u32[]{:S(2)}) %collective-permute-start.5) | collective-permute-done | bytes 32800 | tf_op jit(solution)/shard_map/ppermute | solution.py:341
  74.6 3.1 %collective-permute-start.7 = (bf16[64,256]{1,0:T(8,128)(2,1)S(1)}, bf16[64,256]{1,0:T(8,128)(2,1)S(1)}, u32[]{:S(2)}, u32[]{:S(2)}) collective-permute-start(bf16[64,256]{1,0:T(8,128)(2,1)S(1)} %add.15.kept_q_ref), channel_id=1, source_target_pairs={{0,32},{32,0},{1,33},{33,1},{2,34},{34,2},{3,35},{35,3},{4,36},{36... | collective-permute-start | bytes 98312 | tf_op jit(solution)/shard_map/ppermute | solution.py:380
  77.7 2.2 %all_gather.22.refs_2_ = bf16[8,128,256]{2,1,0:T(8,128)(2,1)S(1)} all-gather(bf16[4,128,256]{2,1,0:T(8,128)(2,1)S(1)} %collective-permute-done.6), channel_id=1, replica_groups=mesh['xh'=2,'y'=4,'xl'=2,'z'=16,'c'=2] {'c'}, dimensions={0}, use_global_device_ids=true | all-gather | bytes 786432 | tf_op jit(solution)/shard_map/all_gather | solution.py:351
  79.9 2.2 %all_gather.23.refs_3_ = bf16[8,128,256]{2,1,0:T(8,128)(2,1)S(1)} all-gather(bf16[4,128,256]{2,1,0:T(8,128)(2,1)S(1)} %collective-permute-done.8), channel_id=1, replica_groups=mesh['xh'=2,'y'=4,'xl'=2,'z'=16,'c'=2] {'c'}, dimensions={0}, use_global_device_ids=true | all-gather | bytes 786432 | tf_op jit(solution)/shard_map/all_gather | solution.py:351
  82.1 5.3 %shard_map.121 = (bf16[64,32]{1,0:T(8,128)(2,1)S(1)}, bf16[64,32]{1,0:T(8,128)(2,1)S(1)}) custom-call(s32[3]{0:T(128)S(1)} %pad_add_fusion.where_ref, bf16[64,256]{1,0:T(8,128)(2,1)S(1)} %add.15.kept_q_ref, bf16[64,256]{1,0:T(8,128)(2,1)S(1)} %collective-permute-done.7.sent_q_ref, bf16[2,128,256]{2,1,0:T(8,128)(2,1)S(1)} %shard_map.119.own_ref, ...), custom_call_target="tpu_custom_call" | custom-call | flops 5000000000 | bytes 4000000 | tf_op jit(solution)/shard_map/pallas_call | solution.py:245
  87.3 5.0 %collective-permute-start.10 = (bf16[64,32]{1,0:T(8,128)(2,1)S(1)}, bf16[64,32]{1,0:T(8,128)(2,1)S(1)}, u32[]{:S(2)}, u32[]{:S(2)}) collective-permute-start(bf16[64,32]{1,0:T(8,128)(2,1)S(1)} %get-tuple-element.53.kept_ref), channel_id=1, source_target_pairs={{64,0},{32,96},{128,64},{96,160},{192,128},{160,224},{256,192},{22... | collective-permute-start | bytes 12296 | tf_op jit(solution)/shard_map/ppermute | solution.py:398
  92.3 3.2 %collective-permute-start.11 = (bf16[64,32]{1,0:T(8,128)(2,1)S(1)}, bf16[64,32]{1,0:T(8,128)(2,1)S(1)}, u32[]{:S(2)}, u32[]{:S(2)}) collective-permute-start(bf16[64,32]{1,0:T(8,128)(2,1)S(1)} %get-tuple-element.54), channel_id=1, source_target_pairs={{64,32},{32,64},{128,96},{96,128},{192,160},{160,192},{256,224},{2... | collective-permute-start | bytes 12296 | tf_op jit(solution)/shard_map/ppermute | solution.py:399
  95.6 1.9 %collective-permute-start.9 = (bf16[64,32]{1,0:T(8,128)(2,1)S(1)}, bf16[64,32]{1,0:T(8,128)(2,1)S(1)}, u32[]{:S(2)}, u32[]{:S(2)}) collective-permute-start(bf16[64,32]{1,0:T(8,128)(2,1)S(1)} %get-tuple-element.54), channel_id=1, source_target_pairs={{0,32},{32,0},{1,33},{33,1},{2,34},{34,2},{3,35},{35,3},{4,36},{36... | collective-permute-start | bytes 12296 | tf_op jit(solution)/shard_map/ppermute | solution.py:397
  97.5 2.5 %collective-permute-done.11.crossed_ref = bf16[64,32]{1,0:T(8,128)(2,1)S(1)} collective-permute-done((bf16[64,32]{1,0:T(8,128)(2,1)S(1)}, bf16[64,32]{1,0:T(8,128)(2,1)S(1)}, u32[]{:S(2)}, u32[]{:S(2)}) %collective-permute-start.11) | collective-permute-done | bytes 4128 | tf_op jit(solution)/shard_map/ppermute | solution.py:399
  (24 shorter events, 7.9 us)
Async XLA Ops:
  6.6 11.4 %collective-permute-start.2 = (bf16[2,128,256]{2,1,0:T(8,128)(2,1)S(1)}, bf16[2,128,256]{2,1,0:T(8,128)(2,1)S(1)}, u32[]{:S(2)}, u32[]{:S(2)}) collective-permute-start(bf16[2,128,256]{2,1,0:T(8,128)(2,1)S(1)} %shard_map.119.own_ref), channel_id=1, source_target_pairs={{0,4},{1,29},{2,6},{3,31},{4,8},{5,1},{6,10},{7,3},{8,12},{9,5},{1... | collective-permute-start | bytes 393224 | tf_op jit(solution)/shard_map/ppermute | solution.py:348
  13.0 6.9 %collective-permute-start.1 = (bf16[2,128,256]{2,1,0:T(8,128)(2,1)S(1)}, bf16[2,128,256]{2,1,0:T(8,128)(2,1)S(1)}, u32[]{:S(2)}, u32[]{:S(2)}) collective-permute-start(bf16[2,128,256]{2,1,0:T(8,128)(2,1)S(1)} %shard_map.119.own_ref), channel_id=1, source_target_pairs={{0,2},{1,31},{2,4},{3,1},{4,6},{5,3},{6,8},{7,5},{8,10},{9,7},{10,... | collective-permute-start | bytes 393224 | tf_op jit(solution)/shard_map/ppermute | solution.py:348
  19.9 12.8 %collective-permute-start.4 = (bf16[4,128,256]{2,1,0:T(8,128)(2,1)S(1)}, bf16[4,128,256]{2,1,0:T(8,128)(2,1)S(1)}, u32[]{:S(2)}, u32[]{:S(2)}) collective-permute-start(bf16[4,128,256]{2,1,0:T(8,128)(2,1)S(1)} %constant_dynamic-update-slice_fusion), channel_id=1, source_target_pairs={{0,4},{1,29},{2,6},{3,31},{4,8},{5,1},{6,10},{7,3},{8,12},{9,5},{1... | collective-permute-start | bytes 786440 | tf_op jit(solution)/shard_map/ppermute | solution.py:348
  32.7 13.1 %collective-permute-start.6 = (bf16[4,128,256]{2,1,0:T(8,128)(2,1)S(1)}, bf16[4,128,256]{2,1,0:T(8,128)(2,1)S(1)}, u32[]{:S(2)}, u32[]{:S(2)}) collective-permute-start(bf16[4,128,256]{2,1,0:T(8,128)(2,1)S(1)} %collective-permute-done.4), channel_id=1, source_target_pairs={{0,4},{1,29},{2,6},{3,31},{4,8},{5,1},{6,10},{7,3},{8,12},{9,5},{1... | collective-permute-start | bytes 786440 | tf_op jit(solution)/shard_map/ppermute | solution.py:348
  45.8 34.0 %collective-permute-start.8 = (bf16[4,128,256]{2,1,0:T(8,128)(2,1)S(1)}, bf16[4,128,256]{2,1,0:T(8,128)(2,1)S(1)}, u32[]{:S(2)}, u32[]{:S(2)}) collective-permute-start(bf16[4,128,256]{2,1,0:T(8,128)(2,1)S(1)} %collective-permute-done.6), channel_id=1, source_target_pairs={{0,4},{1,29},{2,6},{3,31},{4,8},{5,1},{6,10},{7,3},{8,12},{9,5},{1... | collective-permute-start | bytes 786440 | tf_op jit(solution)/shard_map/ppermute | solution.py:348
  53.9 6.0 %collective-permute-start = (bf16[64,256]{1,0:T(8,128)(2,1)S(1)}, bf16[64,256]{1,0:T(8,128)(2,1)S(1)}, u32[]{:S(2)}, u32[]{:S(2)}) collective-permute-start(bf16[64,256]{1,0:T(8,128)(2,1)S(1)} %shard_map.118), channel_id=1, source_target_pairs={{0,64},{64,0},{128,192},{192,128},{1,65},{65,1},{129,193},{193,129... | collective-permute-start | bytes 98312 | tf_op jit(solution)/shard_map/ppermute | solution.py:341
  59.9 7.3 %collective-permute-start.3 = (bf16[64,256]{1,0:T(8,128)(2,1)S(1)}, bf16[64,256]{1,0:T(8,128)(2,1)S(1)}, u32[]{:S(2)}, u32[]{:S(2)}) collective-permute-start(bf16[64,256]{1,0:T(8,128)(2,1)S(1)} %add.13), channel_id=1, source_target_pairs={{0,128},{64,192},{128,0},{192,64},{1,129},{65,193},{129,1},{193,65... | collective-permute-start | bytes 98312 | tf_op jit(solution)/shard_map/ppermute | solution.py:341
  67.2 7.3 %collective-permute-start.5 = (bf16[64,256]{1,0:T(8,128)(2,1)S(1)}, bf16[64,256]{1,0:T(8,128)(2,1)S(1)}, u32[]{:S(2)}, u32[]{:S(2)}) collective-permute-start(bf16[64,256]{1,0:T(8,128)(2,1)S(1)} %add.14), channel_id=1, source_target_pairs={{0,256},{256,0},{1,257},{257,1},{2,258},{258,2},{3,259},{259,3},{4... | collective-permute-start | bytes 98312 | tf_op jit(solution)/shard_map/ppermute | solution.py:341
  74.6 7.5 %collective-permute-start.7 = (bf16[64,256]{1,0:T(8,128)(2,1)S(1)}, bf16[64,256]{1,0:T(8,128)(2,1)S(1)}, u32[]{:S(2)}, u32[]{:S(2)}) collective-permute-start(bf16[64,256]{1,0:T(8,128)(2,1)S(1)} %add.15.kept_q_ref), channel_id=1, source_target_pairs={{0,32},{32,0},{1,33},{33,1},{2,34},{34,2},{3,35},{35,3},{4,36},{36... | collective-permute-start | bytes 98312 | tf_op jit(solution)/shard_map/ppermute | solution.py:380
  82.0 19.2 %copy-start = (bf16[32,512]{1,0:T(8,128)(2,1)S(1)}, bf16[32,512]{1,0:T(8,128)(2,1)}, u32[]{:S(2)}) copy-start(bf16[32,512]{1,0:T(8,128)(2,1)} %proj_w_ref.1) | copy-start | bytes 98308
  82.0 19.2 %copy-start.1 = (f32[3,512]{1,0:T(4,128)S(1)}, f32[3,512]{1,0:T(4,128)}, u32[]{:S(2)}) copy-start(f32[3,512]{1,0:T(4,128)} %time_w_ref.1) | copy-start | bytes 18436
  82.0 19.2 %copy-start.2 = (f32[512]{0:T(512)S(1)}, f32[512]{0:T(512)}, u32[]{:S(2)}) copy-start(f32[512]{0:T(512)} %param.21) | copy-start | bytes 6148
  82.0 19.2 %copy-start.3 = (f32[512]{0:T(512)S(1)}, f32[512]{0:T(512)}, u32[]{:S(2)}) copy-start(f32[512]{0:T(512)} %param.23) | copy-start | bytes 6148
  87.3 10.2 %collective-permute-start.10 = (bf16[64,32]{1,0:T(8,128)(2,1)S(1)}, bf16[64,32]{1,0:T(8,128)(2,1)S(1)}, u32[]{:S(2)}, u32[]{:S(2)}) collective-permute-start(bf16[64,32]{1,0:T(8,128)(2,1)S(1)} %get-tuple-element.53.kept_ref), channel_id=1, source_target_pairs={{64,0},{32,96},{128,64},{96,160},{192,128},{160,224},{256,192},{22... | collective-permute-start | bytes 12296 | tf_op jit(solution)/shard_map/ppermute | solution.py:398
  92.3 7.7 %collective-permute-start.11 = (bf16[64,32]{1,0:T(8,128)(2,1)S(1)}, bf16[64,32]{1,0:T(8,128)(2,1)S(1)}, u32[]{:S(2)}, u32[]{:S(2)}) collective-permute-start(bf16[64,32]{1,0:T(8,128)(2,1)S(1)} %get-tuple-element.54), channel_id=1, source_target_pairs={{64,32},{32,64},{128,96},{96,128},{192,160},{160,192},{256,224},{2... | collective-permute-start | bytes 12296 | tf_op jit(solution)/shard_map/ppermute | solution.py:399
  95.6 5.6 %collective-permute-start.9 = (bf16[64,32]{1,0:T(8,128)(2,1)S(1)}, bf16[64,32]{1,0:T(8,128)(2,1)S(1)}, u32[]{:S(2)}, u32[]{:S(2)}) collective-permute-start(bf16[64,32]{1,0:T(8,128)(2,1)S(1)} %get-tuple-element.54), channel_id=1, source_target_pairs={{0,32},{32,0},{1,33},{33,1},{2,34},{34,2},{3,35},{35,3},{4,36},{36... | collective-permute-start | bytes 12296 | tf_op jit(solution)/shard_map/ppermute | solution.py:397

commit v4 on v3

--- a/solution.py
+++ b/solution.py
@@ -30,61 +30,79 @@
     return pltpu.with_memory_space_constraint(array, pltpu.HBM)
 
 
-def query_kernel(where_ref, table_hbm, start_hbm, rows_hbm, out_ref, table, start, rows, sems):
-    frames_here = 2
+def opening_kernel(
+    where_ref, maps_hbm, table_hbm, start_hbm, rows_hbm, out_ref, table, start, rows, sems
+):
+    frames_here, cells = maps_hbm.shape[0], maps_hbm.shape[1]
     copies = [
-        pltpu.make_async_copy(table_hbm, table, sems.at[0]),
-        pltpu.make_async_copy(start_hbm, start, sems.at[1]),
-        pltpu.make_async_copy(rows_hbm, rows, sems.at[2]),
+        pltpu.make_async_copy(start_hbm, start, sems.at[0]),
+        pltpu.make_async_copy(rows_hbm, rows, sems.at[1]),
+        pltpu.make_async_copy(table_hbm, table, sems.at[2]),
     ]
+    for f in range(frames_here):
+        part = out_ref.at[pl.ds(cells * f, cells)]
+        copies.append(pltpu.make_async_copy(maps_hbm.at[f], part, sems.at[3 + f]))
     for copy in copies:
         copy.start()
-    for copy in copies:
+    for copy in copies[:3]:
         copy.wait()
     low = where_ref[2] * frames_here
     owned = (start[...] >= low) & (start[...] < low + frames_here)
     row = jnp.where(owned, rows[...], -1)
     chosen = (iota((table.shape[1], row.shape[1]), 0) == row).astype(BF)
     got = lax.dot_general(chosen, table[0], (((0,), (0,)), ((), ())), preferred_element_type=F32)
-    out_ref[...] = got.astype(BF)
-
-
-def own_queries(where, query_table, start_frame, row_ids):
+    out_ref[frames_here * cells :, :] = got.astype(BF)
+    for copy in copies[3:]:
+        copy.wait()
+
+
+def opening(where, frame_maps, query_table, start_frame, row_ids):
+    frames_here, cells, channels = frame_maps.shape
     count = start_frame.shape[0]
     hbm = pl.BlockSpec(memory_space=pltpu.HBM)
+    arrays = (frame_maps, query_table, start_frame[None, :], row_ids[None, :])
     return pl.pallas_call(
-        query_kernel,
-        out_shape=jax.ShapeDtypeStruct((count, query_table.shape[2]), BF),
-        in_specs=[pl.BlockSpec(memory_space=pltpu.SMEM)] + [hbm] * 3,
+        opening_kernel,
+        out_shape=jax.ShapeDtypeStruct((frames_here * cells + count, channels), BF),
+        in_specs=[pl.BlockSpec(memory_space=pltpu.SMEM)] + [hbm] * 4,
         out_specs=pl.BlockSpec(memory_space=pltpu.VMEM),
         scratch_shapes=[
             pltpu.VMEM(query_table.shape, BF),
             pltpu.VMEM((1, count), jnp.int32),
             pltpu.VMEM((1, count), jnp.int32),
-            pltpu.SemaphoreType.DMA((3,)),
+            pltpu.SemaphoreType.DMA((5,)),
         ],
         cost_estimate=pl.CostEstimate(flops=2_000_000, bytes_accessed=200_000, transcendentals=0),
         compiler_params=pltpu.CompilerParams(vmem_limit_bytes=4 << 20),
         interpret=INTERPRET,
-    )(where, *map(in_hbm, (query_table, start_frame[None, :], row_ids[None, :])))
-
-
-def pick_kernel(where_ref, all_ref, out_ref):
-    x = where_ref[0]
-    cells = all_ref.shape[2]
-    for core in range(2):
+    )(where, *map(in_hbm, arrays))
+
+
+def pick_kernel(where_ref, all_ref, block_ref, queries_ref):
+    x, core = where_ref[0], where_ref[3]
+    cells = block_ref.shape[1] // 2
+    frame = pl.ds(pl.multiple_of(cells * x, cells), cells)
+    for c in range(2):
         for side in range(2):
-            out_ref[core, cells * side : cells * (side + 1), :] = all_ref[2 * side + core, x]
-
-
-def picked(where, gathered):
-    cells, channels = gathered.shape[2:]
+            block_ref[c, cells * side : cells * (side + 1), :] = all_ref[2 * side + c, frame, :]
+    count = queries_ref.shape[0] // 2
+    first = 2 * cells
+    queries_ref[0:count, :] = all_ref[2 * x + core, first : first + count, :]
+    queries_ref[count:, :] = all_ref[2 * (1 - x) + core, first : first + count, :]
+
+
+def picked(where, gathered, cells):
+    channels = gathered.shape[2]
+    count = gathered.shape[1] - 2 * cells
     vmem = pl.BlockSpec(memory_space=pltpu.VMEM)
     return pl.pallas_call(
         pick_kernel,
-        out_shape=jax.ShapeDtypeStruct((2, 2 * cells, channels), BF),
+        out_shape=(
+            jax.ShapeDtypeStruct((2, 2 * cells, channels), BF),
+            jax.ShapeDtypeStruct((2 * count, channels), BF),
+        ),
         in_specs=[pl.BlockSpec(memory_space=pltpu.SMEM), vmem],
-        out_specs=vmem,
+        out_specs=(vmem, vmem),
         cost_estimate=pl.CostEstimate(flops=0, bytes_accessed=300_000, transcendentals=0),
         compiler_params=pltpu.CompilerParams(vmem_limit_bytes=4 << 20),
         interpret=INTERPRET,
@@ -161,14 +179,14 @@
     )
 
 
-def cost_kernel(z_count, where_ref, kept_q_ref, sent_q_ref, own_ref, *refs):
+def cost_kernel(z_count, where_ref, q_ref, own_ref, *refs):
     far_refs = refs[:-9]
     a_ref, b_ref, bias1_ref, bias2_ref, kept_ref, sent_ref, corr, hid, acc = refs[-9:]
     z = where_ref[1]
-    n = 2 * kept_q_ref.shape[0]
+    n = q_ref.shape[0]
     corr[0, :, 0:128] = jnp.zeros((n, 128), BF)
     hid[0, :, 0:ROW1] = jnp.zeros((n, ROW1), BF)
-    q = jnp.concatenate([kept_q_ref[...], sent_q_ref[...]], axis=0)
+    q = q_ref[...]
 
     def put(low, high, chip):
         cells = jnp.concatenate([low[0:MAP], high[0:MAP], low[MAP:], high[MAP:]], axis=0)
@@ -237,15 +255,15 @@
     sent_ref[...] = pooled[n // 2 :]
 
 
-def pooled_costs(where, kept_q, sent_q, own, far, a, b, bias1, bias2):
-    n = 2 * kept_q.shape[0]
+def pooled_costs(where, queries, own, far, a, b, bias1, bias2):
+    n = queries.shape[0]
     z_count = MAP // 4
     vmem = pl.BlockSpec(memory_space=pltpu.VMEM)
 
     return pl.pallas_call(
         functools.partial(cost_kernel, z_count),
         out_shape=(jax.ShapeDtypeStruct((n // 2, CH2), BF),) * 2,
-        in_specs=[pl.BlockSpec(memory_space=pltpu.SMEM)] + [vmem] * (7 + len(far)),
+        in_specs=[pl.BlockSpec(memory_space=pltpu.SMEM)] + [vmem] * (6 + len(far)),
         out_specs=(vmem, vmem),
         scratch_shapes=[
             pltpu.VMEM((HALF1 + 1, n, 256), BF),
@@ -257,7 +275,7 @@
         ),
         compiler_params=pltpu.CompilerParams(vmem_limit_bytes=28 << 20),
         interpret=INTERPRET,
-    )(where, kept_q, sent_q, own, *far, a, b, bias1, bias2)
+    )(where, queries, own, *far, a, b, bias1, bias2)
 
 
 def tail_kernel(
@@ -334,7 +352,7 @@
     x = lax.axis_index("xl")
     z = lax.axis_index("z")
     frame_block = lax.axis_index("xh") * y_count + lax.axis_index("y")
-    where = jnp.stack([x, z, frame_block]).astype(jnp.int32)
+    where = jnp.stack([x, z, frame_block, lax.axis_index("c")]).astype(jnp.int32)
     swap = [(0, 1), (1, 0)]
 
     def flip(axis, count, step):
@@ -353,37 +371,32 @@
     def behind(value, earlier):
         return lax.optimization_barrier((value, earlier))[0]
 
-    gathered = lax.all_gather(frame_maps, ("xl", "c"), axis=0)
-    own = picked(where, gathered)
+    message = opening(where, frame_maps, query_table, start_frame, row_ids)
+    gathered = lax.all_gather(message, ("xl", "c"), axis=0)
+    own, queries = picked(where, gathered, frame_maps.shape[1])
     weights = banded_weights(conv1_w, conv1_b, conv2_w, conv2_b)
-    near = along(own, 1)
-    next_near = along(own, 2)
-    queries = own_queries(where, query_table, start_frame, row_ids)
-    queries = queries + flip("y", y_count, 1)(behind(queries, own))
-    near, next_near, weights = lax.optimization_barrier((near, next_near, weights))
-
-    far = []
-    moving = jnp.concatenate([near, next_near], axis=0)
+    near = []
+    for distance in (1, 2, 3):
+        near.append(along(own, distance))
+    queries = queries + flip("y", y_count, 1)(queries)
+    near[1], near[2] = lax.optimization_barrier((near[1], near[2]))
+
+    pair = jnp.concatenate([near[1], near[2]], axis=0)
+    far5 = along(pair, 3)
+    far4 = along(near[0], 3)
     if y_count > 2:
-        queries = queries + flip("y", y_count, 2)(behind(queries, moving))
-    far.append(both(moving))
-    moving = along(moving, 2)
-    moving, far = lax.optimization_barrier((moving, far))
-
+        queries = queries + flip("y", y_count, 2)(behind(queries, pair))
+    near1 = both(near[0])
+    far5, near1, weights = lax.optimization_barrier((far5, near1, weights))
+
+    far7 = along(far5, 2)
     if xh_count > 1:
-        queries = queries + flip("xh", xh_count, 1)(behind(queries, moving))
-    far.append(both(moving))
-    moving = along(moving, 2)
-    moving, far = lax.optimization_barrier((moving, far))
-
-    kept_q = queries
-    sent_q = lax.ppermute(behind(queries, moving), "xl", swap)
-    far.append(both(moving))
-    moving = along(moving, 2)
-    moving, far = lax.optimization_barrier((moving, far))
-    far.append(both(moving))
-
-    kept, sent = pooled_costs(where, kept_q, sent_q, own, far, *weights)
+        queries = queries + flip("xh", xh_count, 1)(behind(queries, far5))
+    spread = [near1, both(behind(pair, far5)), both(behind(far4, far5)), both(far5)]
+    far7, spread, queries = lax.optimization_barrier((far7, spread, queries))
+    spread.append(both(far7))
+
+    kept, sent = pooled_costs(where, queries, own, spread, *weights)
 
     def frame_pairs(cross):
         pairs = []

time: 103 us -> 94.5 us (0.917)
  the two profiles are of different devices: /device:TPU:68 before, /device:TPU:4 now
where the time goes in v4:
time: 94.5 us; the launch traced here: 94 us
  starting transfers between devices  53.5 us (57%)
  blocking collectives  16.7 us (18%)
  waiting for transfers between devices  13.3 us (14%)
  Pallas kernels  10.1 us (11%)
    ppermute x6, starting transfers between devices, along(): return lax.ppermute(block, ('z', 'c'), pairs)  31.8 us
    ppermute x3, starting transfers between devices, flip(): lax.ppermute(v, axis, [(i, i ^ step) for i in range(count)])  11.3 us
    all_gather x5, blocking collectives, both(): return lax.all_gather(block, 'c', axis=0, tiled=True)  10.5 us
    ppermute x6, waiting for transfers between devices, along(): return lax.ppermute(block, ('z', 'c'), pairs)  6.87 us
    all_gather x1, blocking collectives, one_device(): gathered = lax.all_gather(message, ('xl', 'c'), axis=0)  6.17 us
    pallas_call x1, Pallas kernels, pooled_costs(): pl.pallas_call(functools.partial(cost_kernel, z_count), out_shape=(jax.Sh...  5.28 us
    ppermute x1, starting transfers between devices, one_device(): crossed = lax.ppermute(sent, ('xh', 'y', 'xl'), frame_pairs(True))  4.64 us
    ppermute x1, starting transfers between devices, one_device(): straight = lax.ppermute(kept, ('xh', 'y', 'xl'), frame_pairs(False))  3.93 us
  transfers between devices with their start and end apart: 12, of which 6 were waited for; matrix products, arithmetic and copies ran while one was open for 0% of the time, Pallas kernels for 1%

profile of v4, /device:TPU:4, one launch (start us, length us, event | category | flops | bytes accessed | tf_op | source)
XLA Modules:
  0.0 94.0 jit_solution(13807858789486777585)
XLA Ops:
  0.1 1.6 %shard_map.118 = bf16[192,256]{1,0:T(8,128)(2,1)S(1)} custom-call(s32[4]{0:T(128)S(1)} %pad_add_fusion.where_ref, bf16[2,64,256]{2,1,0:T(8,128)(2,1)} %maps_hbm.1, bf16[1,64,256]{2,1,0:T(8,128)(2,1)} %table_hbm.1, s32[1,64]{1,0:T(1,128)} %bitcast.16, s32[1,64]{1,0:T(1,128)} %bitcast.17), custom_call_target="tpu_custom_call" | custom-call | flops 2000000 | bytes 200000 | tf_op jit(solution)/shard_map/pallas_call | solution.py:64
  1.7 6.2 %all-gather = bf16[768,256]{1,0:T(8,128)(2,1)S(1)} all-gather(bf16[192,256]{1,0:T(8,128)(2,1)S(1)} %shard_map.118), channel_id=2, replica_groups=mesh['xh'=2,'y'=4,'xl'=2,'z'=16,'c'=2] {'xl','c'}, dimensions={0}, use_global_device_ids=true | all-gather | bytes 491520 | tf_op jit(solution)/shard_map/all_gather | solution.py:375
  8.4 6.5 %collective-permute-start.1 = (bf16[2,128,256]{2,1,0:T(8,128)(2,1)S(1)}, bf16[2,128,256]{2,1,0:T(8,128)(2,1)S(1)}, u32[]{:S(2)}, u32[]{:S(2)}) collective-permute-start(bf16[2,128,256]{2,1,0:T(8,128)(2,1)S(1)} %get-tuple-element.31.own_ref), channel_id=1, source_target_pairs={{0,6},{1,27},{2,8},{3,29},{4,10},{5,31},{6,12},{7,1},{8,14},{9,3},... | collective-permute-start | bytes 393224 | tf_op jit(solution)/shard_map/ppermute | solution.py:366
  14.9 6.4 %collective-permute-start = (bf16[2,128,256]{2,1,0:T(8,128)(2,1)S(1)}, bf16[2,128,256]{2,1,0:T(8,128)(2,1)S(1)}, u32[]{:S(2)}, u32[]{:S(2)}) collective-permute-start(bf16[2,128,256]{2,1,0:T(8,128)(2,1)S(1)} %get-tuple-element.31.own_ref), channel_id=1, source_target_pairs={{0,4},{1,29},{2,6},{3,31},{4,8},{5,1},{6,10},{7,3},{8,12},{9,5},{1... | collective-permute-start | bytes 393224 | tf_op jit(solution)/shard_map/ppermute | solution.py:366
  21.3 2.5 %collective-permute-done.1 = bf16[2,128,256]{2,1,0:T(8,128)(2,1)S(1)} collective-permute-done((bf16[2,128,256]{2,1,0:T(8,128)(2,1)S(1)}, bf16[2,128,256]{2,1,0:T(8,128)(2,1)S(1)}, u32[]{:S(2)}, u32[]{:S(2)}) %collective-permute-start.1) | collective-permute-done | bytes 131104 | tf_op jit(solution)/shard_map/ppermute | solution.py:366
  23.8 4.4 %collective-permute-done = bf16[2,128,256]{2,1,0:T(8,128)(2,1)S(1)} collective-permute-done((bf16[2,128,256]{2,1,0:T(8,128)(2,1)S(1)}, bf16[2,128,256]{2,1,0:T(8,128)(2,1)S(1)}, u32[]{:S(2)}, u32[]{:S(2)}) %collective-permute-start) | collective-permute-done | bytes 131104 | tf_op jit(solution)/shard_map/ppermute | solution.py:366
  28.2 3.8 %collective-permute-start.2 = (bf16[4,128,256]{2,1,0:T(8,128)(2,1)S(1)}, bf16[4,128,256]{2,1,0:T(8,128)(2,1)S(1)}, u32[]{:S(2)}, u32[]{:S(2)}) collective-permute-start(bf16[4,128,256]{2,1,0:T(8,128)(2,1)S(1)} %constant_dynamic-update-slice_fusion), channel_id=1, source_target_pairs={{0,6},{1,27},{2,8},{3,29},{4,10},{5,31},{6,12},{7,1},{8,14},{9,3},... | collective-permute-start | bytes 786440 | tf_op jit(solution)/shard_map/ppermute | solution.py:366
  32.0 4.6 %collective-permute-start.3 = (bf16[2,128,256]{2,1,0:T(8,128)(2,1)S(1)}, bf16[2,128,256]{2,1,0:T(8,128)(2,1)S(1)}, u32[]{:S(2)}, u32[]{:S(2)}) collective-permute-start(bf16[2,128,256]{2,1,0:T(8,128)(2,1)S(1)} %get-tuple-element.31.own_ref), channel_id=1, source_target_pairs={{0,2},{1,31},{2,4},{3,1},{4,6},{5,3},{6,8},{7,5},{8,10},{9,7},{10,... | collective-permute-start | bytes 393224 | tf_op jit(solution)/shard_map/ppermute | solution.py:366
  36.6 3.5 %collective-permute-start.6 = (bf16[128,256]{1,0:T(8,128)(2,1)S(1)}, bf16[128,256]{1,0:T(8,128)(2,1)S(1)}, u32[]{:S(2)}, u32[]{:S(2)}) collective-permute-start(bf16[128,256]{1,0:T(8,128)(2,1)S(1)} %get-tuple-element.42), channel_id=1, source_target_pairs={{0,64},{64,0},{128,192},{192,128},{1,65},{65,1},{129,193},{193,129... | collective-permute-start | bytes 196616 | tf_op jit(solution)/shard_map/ppermute | solution.py:359
  41.3 2.0 %collective-permute-done.6 = bf16[128,256]{1,0:T(8,128)(2,1)S(1)} collective-permute-done((bf16[128,256]{1,0:T(8,128)(2,1)S(1)}, bf16[128,256]{1,0:T(8,128)(2,1)S(1)}, u32[]{:S(2)}, u32[]{:S(2)}) %collective-permute-start.6) | collective-permute-done | bytes 65568 | tf_op jit(solution)/shard_map/ppermute | solution.py:359
  43.2 5.1 %collective-permute-start.7 = (bf16[128,256]{1,0:T(8,128)(2,1)S(1)}, bf16[128,256]{1,0:T(8,128)(2,1)S(1)}, u32[]{:S(2)}, u32[]{:S(2)}) collective-permute-start(bf16[128,256]{1,0:T(8,128)(2,1)S(1)} %add.13), channel_id=1, source_target_pairs={{0,128},{64,192},{128,0},{192,64},{1,129},{65,193},{129,1},{193,65... | collective-permute-start | bytes 196616 | tf_op jit(solution)/shard_map/ppermute | solution.py:359
  48.4 4.6 %collective-permute-start.5 = (bf16[2,128,256]{2,1,0:T(8,128)(2,1)S(1)}, bf16[2,128,256]{2,1,0:T(8,128)(2,1)S(1)}, u32[]{:S(2)}, u32[]{:S(2)}) collective-permute-start(bf16[2,128,256]{2,1,0:T(8,128)(2,1)S(1)} %collective-permute-done.3), channel_id=1, source_target_pairs={{0,6},{1,27},{2,8},{3,29},{4,10},{5,31},{6,12},{7,1},{8,14},{9,3},... | collective-permute-start | bytes 393224 | tf_op jit(solution)/shard_map/ppermute | solution.py:366
  53.0 2.0 %all_gather.23.refs_0_ = bf16[4,128,256]{2,1,0:T(8,128)(2,1)S(1)} all-gather(bf16[2,128,256]{2,1,0:T(8,128)(2,1)S(1)} %collective-permute-done.3), channel_id=1, replica_groups=mesh['xh'=2,'y'=4,'xl'=2,'z'=16,'c'=2] {'c'}, dimensions={0}, use_global_device_ids=true | all-gather | bytes 393216 | tf_op jit(solution)/shard_map/all_gather | solution.py:369
  55.0 5.8 %collective-permute-start.4 = (bf16[4,128,256]{2,1,0:T(8,128)(2,1)S(1)}, bf16[4,128,256]{2,1,0:T(8,128)(2,1)S(1)}, u32[]{:S(2)}, u32[]{:S(2)}) collective-permute-start(bf16[4,128,256]{2,1,0:T(8,128)(2,1)S(1)} %collective-permute-done.2), channel_id=1, source_target_pairs={{0,4},{1,29},{2,6},{3,31},{4,8},{5,1},{6,10},{7,3},{8,12},{9,5},{1... | collective-permute-start | bytes 786440 | tf_op jit(solution)/shard_map/ppermute | solution.py:366
  60.8 2.2 %all_gather.26.refs_3_ = bf16[8,128,256]{2,1,0:T(8,128)(2,1)S(1)} all-gather(bf16[4,128,256]{2,1,0:T(8,128)(2,1)S(1)} %collective-permute-done.2), channel_id=1, replica_groups=mesh['xh'=2,'y'=4,'xl'=2,'z'=16,'c'=2] {'c'}, dimensions={0}, use_global_device_ids=true | all-gather | bytes 786432 | tf_op jit(solution)/shard_map/all_gather | solution.py:369
  63.0 2.7 %collective-permute-start.8 = (bf16[128,256]{1,0:T(8,128)(2,1)S(1)}, bf16[128,256]{1,0:T(8,128)(2,1)S(1)}, u32[]{:S(2)}, u32[]{:S(2)}) collective-permute-start(bf16[128,256]{1,0:T(8,128)(2,1)S(1)} %add.14), channel_id=1, source_target_pairs={{0,256},{256,0},{1,257},{257,1},{2,258},{258,2},{3,259},{259,3},{4... | collective-permute-start | bytes 196616 | tf_op jit(solution)/shard_map/ppermute | solution.py:359
  65.7 2.2 %all_gather.24.refs_1_ = bf16[8,128,256]{2,1,0:T(8,128)(2,1)S(1)} all-gather(bf16[4,128,256]{2,1,0:T(8,128)(2,1)S(1)} %constant_dynamic-update-slice_fusion), channel_id=1, replica_groups=mesh['xh'=2,'y'=4,'xl'=2,'z'=16,'c'=2] {'c'}, dimensions={0}, use_global_device_ids=true | all-gather | bytes 786432 | tf_op jit(solution)/shard_map/all_gather | solution.py:369
  67.9 2.0 %all_gather.25.refs_2_ = bf16[4,128,256]{2,1,0:T(8,128)(2,1)S(1)} all-gather(bf16[2,128,256]{2,1,0:T(8,128)(2,1)S(1)} %collective-permute-done.5), channel_id=1, replica_groups=mesh['xh'=2,'y'=4,'xl'=2,'z'=16,'c'=2] {'c'}, dimensions={0}, use_global_device_ids=true | all-gather | bytes 393216 | tf_op jit(solution)/shard_map/all_gather | solution.py:369
  70.7 2.2 %all_gather.27.refs_4_ = bf16[8,128,256]{2,1,0:T(8,128)(2,1)S(1)} all-gather(bf16[4,128,256]{2,1,0:T(8,128)(2,1)S(1)} %collective-permute-done.4), channel_id=1, replica_groups=mesh['xh'=2,'y'=4,'xl'=2,'z'=16,'c'=2] {'c'}, dimensions={0}, use_global_device_ids=true | all-gather | bytes 786432 | tf_op jit(solution)/shard_map/all_gather | solution.py:369
  72.9 5.3 %shard_map.121 = (bf16[64,32]{1,0:T(8,128)(2,1)S(1)}, bf16[64,32]{1,0:T(8,128)(2,1)S(1)}) custom-call(s32[4]{0:T(128)S(1)} %pad_add_fusion.where_ref, bf16[128,256]{1,0:T(8,128)(2,1)S(1)} %add.15.q_ref, bf16[2,128,256]{2,1,0:T(8,128)(2,1)S(1)} %get-tuple-element.31.own_ref, bf16[4,128,256]{2,1,0:T(8,128)(2,1)S(1)} %all_gather.23.refs_0_, ...), custom_call_target="tpu_custom_call" | custom-call | flops 5000000000 | bytes 4000000 | tf_op jit(solution)/shard_map/pallas_call | solution.py:263
  78.2 3.9 %collective-permute-start.10 = (bf16[64,32]{1,0:T(8,128)(2,1)S(1)}, bf16[64,32]{1,0:T(8,128)(2,1)S(1)}, u32[]{:S(2)}, u32[]{:S(2)}) collective-permute-start(bf16[64,32]{1,0:T(8,128)(2,1)S(1)} %get-tuple-element.55.kept_ref), channel_id=1, source_target_pairs={{64,0},{32,96},{128,64},{96,160},{192,128},{160,224},{256,192},{22... | collective-permute-start | bytes 12296 | tf_op jit(solution)/shard_map/ppermute | solution.py:411
  82.1 4.6 %collective-permute-start.11 = (bf16[64,32]{1,0:T(8,128)(2,1)S(1)}, bf16[64,32]{1,0:T(8,128)(2,1)S(1)}, u32[]{:S(2)}, u32[]{:S(2)}) collective-permute-start(bf16[64,32]{1,0:T(8,128)(2,1)S(1)} %get-tuple-element.56), channel_id=1, source_target_pairs={{64,32},{32,64},{128,96},{96,128},{192,160},{160,192},{256,224},{2... | collective-permute-start | bytes 12296 | tf_op jit(solution)/shard_map/ppermute | solution.py:412
  86.8 1.9 %collective-permute-start.9 = (bf16[64,32]{1,0:T(8,128)(2,1)S(1)}, bf16[64,32]{1,0:T(8,128)(2,1)S(1)}, u32[]{:S(2)}, u32[]{:S(2)}) collective-permute-start(bf16[64,32]{1,0:T(8,128)(2,1)S(1)} %get-tuple-element.56), channel_id=1, source_target_pairs={{0,32},{32,0},{1,33},{33,1},{2,34},{34,2},{3,35},{35,3},{4,36},{36... | collective-permute-start | bytes 12296 | tf_op jit(solution)/shard_map/ppermute | solution.py:410
  89.9 2.5 %collective-permute-done.9.partner_ref = bf16[64,32]{1,0:T(8,128)(2,1)S(1)} collective-permute-done((bf16[64,32]{1,0:T(8,128)(2,1)S(1)}, bf16[64,32]{1,0:T(8,128)(2,1)S(1)}, u32[]{:S(2)}, u32[]{:S(2)}) %collective-permute-start.9) | collective-permute-done | bytes 4128 | tf_op jit(solution)/shard_map/ppermute | solution.py:410
  (25 shorter events, 5.3 us)
Async XLA Ops:
  8.4 15.4 %collective-permute-start.1 = (bf16[2,128,256]{2,1,0:T(8,128)(2,1)S(1)}, bf16[2,128,256]{2,1,0:T(8,128)(2,1)S(1)}, u32[]{:S(2)}, u32[]{:S(2)}) collective-permute-start(bf16[2,128,256]{2,1,0:T(8,128)(2,1)S(1)} %get-tuple-element.31.own_ref), channel_id=1, source_target_pairs={{0,6},{1,27},{2,8},{3,29},{4,10},{5,31},{6,12},{7,1},{8,14},{9,3},... | collective-permute-start | bytes 393224 | tf_op jit(solution)/shard_map/ppermute | solution.py:366
  14.9 13.3 %collective-permute-start = (bf16[2,128,256]{2,1,0:T(8,128)(2,1)S(1)}, bf16[2,128,256]{2,1,0:T(8,128)(2,1)S(1)}, u32[]{:S(2)}, u32[]{:S(2)}) collective-permute-start(bf16[2,128,256]{2,1,0:T(8,128)(2,1)S(1)} %get-tuple-element.31.own_ref), channel_id=1, source_target_pairs={{0,4},{1,29},{2,6},{3,31},{4,8},{5,1},{6,10},{7,3},{8,12},{9,5},{1... | collective-permute-start | bytes 393224 | tf_op jit(solution)/shard_map/ppermute | solution.py:366
  28.2 26.8 %collective-permute-start.2 = (bf16[4,128,256]{2,1,0:T(8,128)(2,1)S(1)}, bf16[4,128,256]{2,1,0:T(8,128)(2,1)S(1)}, u32[]{:S(2)}, u32[]{:S(2)}) collective-permute-start(bf16[4,128,256]{2,1,0:T(8,128)(2,1)S(1)} %constant_dynamic-update-slice_fusion), channel_id=1, source_target_pairs={{0,6},{1,27},{2,8},{3,29},{4,10},{5,31},{6,12},{7,1},{8,14},{9,3},... | collective-permute-start | bytes 786440 | tf_op jit(solution)/shard_map/ppermute | solution.py:366
  32.0 16.3 %collective-permute-start.3 = (bf16[2,128,256]{2,1,0:T(8,128)(2,1)S(1)}, bf16[2,128,256]{2,1,0:T(8,128)(2,1)S(1)}, u32[]{:S(2)}, u32[]{:S(2)}) collective-permute-start(bf16[2,128,256]{2,1,0:T(8,128)(2,1)S(1)} %get-tuple-element.31.own_ref), channel_id=1, source_target_pairs={{0,2},{1,31},{2,4},{3,1},{4,6},{5,3},{6,8},{7,5},{8,10},{9,7},{10,... | collective-permute-start | bytes 393224 | tf_op jit(solution)/shard_map/ppermute | solution.py:366
  36.6 6.6 %collective-permute-start.6 = (bf16[128,256]{1,0:T(8,128)(2,1)S(1)}, bf16[128,256]{1,0:T(8,128)(2,1)S(1)}, u32[]{:S(2)}, u32[]{:S(2)}) collective-permute-start(bf16[128,256]{1,0:T(8,128)(2,1)S(1)} %get-tuple-element.42), channel_id=1, source_target_pairs={{0,64},{64,0},{128,192},{192,128},{1,65},{65,1},{129,193},{193,129... | collective-permute-start | bytes 196616 | tf_op jit(solution)/shard_map/ppermute | solution.py:359
  43.2 11.7 %collective-permute-start.7 = (bf16[128,256]{1,0:T(8,128)(2,1)S(1)}, bf16[128,256]{1,0:T(8,128)(2,1)S(1)}, u32[]{:S(2)}, u32[]{:S(2)}) collective-permute-start(bf16[128,256]{1,0:T(8,128)(2,1)S(1)} %add.13), channel_id=1, source_target_pairs={{0,128},{64,192},{128,0},{192,64},{1,129},{65,193},{129,1},{193,65... | collective-permute-start | bytes 196616 | tf_op jit(solution)/shard_map/ppermute | solution.py:359
  48.4 14.7 %collective-permute-start.5 = (bf16[2,128,256]{2,1,0:T(8,128)(2,1)S(1)}, bf16[2,128,256]{2,1,0:T(8,128)(2,1)S(1)}, u32[]{:S(2)}, u32[]{:S(2)}) collective-permute-start(bf16[2,128,256]{2,1,0:T(8,128)(2,1)S(1)} %collective-permute-done.3), channel_id=1, source_target_pairs={{0,6},{1,27},{2,8},{3,29},{4,10},{5,31},{6,12},{7,1},{8,14},{9,3},... | collective-permute-start | bytes 393224 | tf_op jit(solution)/shard_map/ppermute | solution.py:366
  55.0 15.7 %collective-permute-start.4 = (bf16[4,128,256]{2,1,0:T(8,128)(2,1)S(1)}, bf16[4,128,256]{2,1,0:T(8,128)(2,1)S(1)}, u32[]{:S(2)}, u32[]{:S(2)}) collective-permute-start(bf16[4,128,256]{2,1,0:T(8,128)(2,1)S(1)} %collective-permute-done.2), channel_id=1, source_target_pairs={{0,4},{1,29},{2,6},{3,31},{4,8},{5,1},{6,10},{7,3},{8,12},{9,5},{1... | collective-permute-start | bytes 786440 | tf_op jit(solution)/shard_map/ppermute | solution.py:366
  63.0 7.7 %collective-permute-start.8 = (bf16[128,256]{1,0:T(8,128)(2,1)S(1)}, bf16[128,256]{1,0:T(8,128)(2,1)S(1)}, u32[]{:S(2)}, u32[]{:S(2)}) collective-permute-start(bf16[128,256]{1,0:T(8,128)(2,1)S(1)} %add.14), channel_id=1, source_target_pairs={{0,256},{256,0},{1,257},{257,1},{2,258},{258,2},{3,259},{259,3},{4... | collective-permute-start | bytes 196616 | tf_op jit(solution)/shard_map/ppermute | solution.py:359
  72.9 19.5 %copy-start = (bf16[32,512]{1,0:T(8,128)(2,1)S(1)}, bf16[32,512]{1,0:T(8,128)(2,1)}, u32[]{:S(2)}) copy-start(bf16[32,512]{1,0:T(8,128)(2,1)} %proj_w_ref.1) | copy-start | bytes 98308
  72.9 19.5 %copy-start.1 = (f32[3,512]{1,0:T(4,128)S(1)}, f32[3,512]{1,0:T(4,128)}, u32[]{:S(2)}) copy-start(f32[3,512]{1,0:T(4,128)} %time_w_ref.1) | copy-start | bytes 18436
  72.9 19.5 %copy-start.2 = (f32[512]{0:T(512)S(1)}, f32[512]{0:T(512)}, u32[]{:S(2)}) copy-start(f32[512]{0:T(512)} %param.21) | copy-start | bytes 6148
  72.9 19.5 %copy-start.3 = (f32[512]{0:T(512)S(1)}, f32[512]{0:T(512)}, u32[]{:S(2)}) copy-start(f32[512]{0:T(512)} %param.23) | copy-start | bytes 6148
  78.2 10.5 %collective-permute-start.10 = (bf16[64,32]{1,0:T(8,128)(2,1)S(1)}, bf16[64,32]{1,0:T(8,128)(2,1)S(1)}, u32[]{:S(2)}, u32[]{:S(2)}) collective-permute-start(bf16[64,32]{1,0:T(8,128)(2,1)S(1)} %get-tuple-element.55.kept_ref), channel_id=1, source_target_pairs={{64,0},{32,96},{128,64},{96,160},{192,128},{160,224},{256,192},{22... | collective-permute-start | bytes 12296 | tf_op jit(solution)/shard_map/ppermute | solution.py:411
  82.1 7.7 %collective-permute-start.11 = (bf16[64,32]{1,0:T(8,128)(2,1)S(1)}, bf16[64,32]{1,0:T(8,128)(2,1)S(1)}, u32[]{:S(2)}, u32[]{:S(2)}) collective-permute-start(bf16[64,32]{1,0:T(8,128)(2,1)S(1)} %get-tuple-element.56), channel_id=1, source_target_pairs={{64,32},{32,64},{128,96},{96,128},{192,160},{160,192},{256,224},{2... | collective-permute-start | bytes 12296 | tf_op jit(solution)/shard_map/ppermute | solution.py:412
  86.8 5.6 %collective-permute-start.9 = (bf16[64,32]{1,0:T(8,128)(2,1)S(1)}, bf16[64,32]{1,0:T(8,128)(2,1)S(1)}, u32[]{:S(2)}, u32[]{:S(2)}) collective-permute-start(bf16[64,32]{1,0:T(8,128)(2,1)S(1)} %get-tuple-element.56), channel_id=1, source_target_pairs={{0,32},{32,0},{1,33},{33,1},{2,34},{34,2},{3,35},{35,3},{4,36},{36... | collective-permute-start | bytes 12296 | tf_op jit(solution)/shard_map/ppermute | solution.py:410

commit v5 on v4

--- a/solution.py
+++ b/solution.py
@@ -179,16 +179,42 @@
     )
 
 
+def join_kernel(*refs):
+    low = 0
+    for ref in refs[:-1]:
+        high = low + ref.shape[0]
+        refs[-1][low:high] = ref[...]
+        low = high
+
+
+def joined(*blocks):
+    count = sum(block.shape[0] for block in blocks)
+    vmem = pl.BlockSpec(memory_space=pltpu.VMEM)
+    shape = (count,) + blocks[0].shape[1:]
+    return pl.pallas_call(
+        join_kernel,
+        out_shape=jax.ShapeDtypeStruct(shape, BF),
+        in_specs=[vmem] * len(blocks),
+        out_specs=vmem,
+        cost_estimate=pl.CostEstimate(flops=0, bytes_accessed=300_000, transcendentals=0),
+        compiler_params=pltpu.CompilerParams(vmem_limit_bytes=4 << 20),
+        interpret=INTERPRET,
+    )(*blocks)
+
+
 def cost_kernel(z_count, where_ref, q_ref, own_ref, *refs):
-    far_refs = refs[:-9]
+    *mine_refs, cross_ref, last_ref = refs[:-9]
     a_ref, b_ref, bias1_ref, bias2_ref, kept_ref, sent_ref, corr, hid, acc = refs[-9:]
     z = where_ref[1]
+    toward = 2 * where_ref[3] - 1
     n = q_ref.shape[0]
     corr[0, :, 0:128] = jnp.zeros((n, 128), BF)
     hid[0, :, 0:ROW1] = jnp.zeros((n, ROW1), BF)
     q = q_ref[...]
 
-    def put(low, high, chip):
+    def put(ref, k, shift):
+        low, high = ref[k], ref[k + 1]
+        chip = lax.rem(z + z_count + shift, z_count)
         cells = jnp.concatenate([low[0:MAP], high[0:MAP], low[MAP:], high[MAP:]], axis=0)
         got = lax.dot_general(q, cells, (((1,), (1,)), ((), ())), preferred_element_type=F32)
         got = (got * 0.0625).astype(BF)
@@ -198,17 +224,19 @@
             corr[y, :, 128:256] = part
             corr[y + 1, :, 0:128] = part
 
-    put(own_ref[0], own_ref[1], z)
+    put(own_ref, 0, 0)
     distance = 0
-    for ref in far_refs:
-        per = ref.shape[0] // 4
-        for i in range(per):
+    for ref in mine_refs:
+        for k in range(0, ref.shape[0], 2):
             distance += 1
-            k = 2 * i
-            put(ref[k], ref[k + 1], lax.rem(z + z_count - distance, z_count))
-            if 2 * distance < z_count:
-                k += 2 * per
-                put(ref[k], ref[k + 1], lax.rem(z + distance, z_count))
+            put(ref, k, toward * distance)
+            put(cross_ref, 2 * distance - 2, -toward * distance)
+    half = last_ref.shape[0] // 2
+    for k in range(0, half, 2):
+        distance += 1
+        put(last_ref, k, -distance)
+        if 2 * distance < z_count:
+            put(last_ref, half + k, distance)
 
     bias1 = bias1_ref[...]
     rows1 = 8
@@ -381,20 +409,20 @@
     queries = queries + flip("y", y_count, 1)(queries)
     near[1], near[2] = lax.optimization_barrier((near[1], near[2]))
 
-    pair = jnp.concatenate([near[1], near[2]], axis=0)
+    pair = joined(near[1], near[2])
     far5 = along(pair, 3)
     far4 = along(near[0], 3)
     if y_count > 2:
         queries = queries + flip("y", y_count, 2)(behind(queries, pair))
-    near1 = both(near[0])
-    far5, near1, weights = lax.optimization_barrier((far5, near1, weights))
+    far5, weights = lax.optimization_barrier((far5, weights))
 
     far7 = along(far5, 2)
     if xh_count > 1:
         queries = queries + flip("xh", xh_count, 1)(behind(queries, far5))
-    spread = [near1, both(behind(pair, far5)), both(behind(far4, far5)), both(far5)]
-    far7, spread, queries = lax.optimization_barrier((far7, spread, queries))
-    spread.append(both(far7))
+    mine = [near[0], pair, far4, far5]
+    cross = lax.ppermute(joined(*mine), "c", swap)
+    far7, cross, queries = lax.optimization_barrier((far7, cross, queries))
+    spread = mine + [cross, both(far7)]
 
     kept, sent = pooled_costs(where, queries, own, spread, *weights)
 

time: 94.5 us -> 112 us (1.19)
  the two profiles are of different devices: /device:TPU:4 before, /device:TPU:68 now
where the time goes in v5:
time: 112 us; the launch traced here: 111 us
  starting transfers between devices  60 us (54%)
  waiting for transfers between devices  32.3 us (29%)
  Pallas kernels  10.1 us (9%)
  blocking collectives  8.35 us (7%)
    ppermute x6, starting transfers between devices, along(): return lax.ppermute(block, ('z', 'c'), pairs)  35.5 us
    ppermute x6, waiting for transfers between devices, along(): return lax.ppermute(block, ('z', 'c'), pairs)  17.2 us
    ppermute x3, starting transfers between devices, flip(): lax.ppermute(v, axis, [(i, i ^ step) for i in range(count)])  11.3 us
    ppermute x3, waiting for transfers between devices, flip(): lax.ppermute(v, axis, [(i, i ^ step) for i in range(count)])  10.2 us
    all_gather x1, blocking collectives, one_device(): gathered = lax.all_gather(message, ('xl', 'c'), axis=0)  6.17 us
    ppermute x1, starting transfers between devices, one_device(): straight = lax.ppermute(kept, ('xh', 'y', 'xl'), frame_pairs(False))  5.5 us
    pallas_call x1, Pallas kernels, pooled_costs(): pl.pallas_call(functools.partial(cost_kernel, z_count), out_shape=(jax.Sh...  5.29 us
    ppermute x1, waiting for transfers between devices, one_device(): crossed = lax.ppermute(sent, ('xh', 'y', 'xl'), frame_pairs(True))  4.97 us
  transfers between devices with their start and end apart: 13, of which 7 were waited for; matrix products, arithmetic and copies ran while one was open for 0% of the time, Pallas kernels for 1%

profile of v5, /device:TPU:68, one launch (start us, length us, event | category | flops | bytes accessed | tf_op | source)
XLA Modules:
  0.0 111.2 jit_solution(5969881586721739020)
XLA Ops:
  0.1 1.6 %shard_map.118 = bf16[192,256]{1,0:T(8,128)(2,1)S(1)} custom-call(s32[4]{0:T(128)S(1)} %pad_add_fusion.where_ref, bf16[2,64,256]{2,1,0:T(8,128)(2,1)} %maps_hbm.1, bf16[1,64,256]{2,1,0:T(8,128)(2,1)} %table_hbm.1, s32[1,64]{1,0:T(1,128)} %bitcast.16, s32[1,64]{1,0:T(1,128)} %bitcast.17), custom_call_target="tpu_custom_call" | custom-call | flops 2000000 | bytes 200000 | tf_op jit(solution)/shard_map/pallas_call | solution.py:64
  1.7 6.2 %all-gather = bf16[768,256]{1,0:T(8,128)(2,1)S(1)} all-gather(bf16[192,256]{1,0:T(8,128)(2,1)S(1)} %shard_map.118), channel_id=2, replica_groups=mesh['xh'=2,'y'=4,'xl'=2,'z'=16,'c'=2] {'xl','c'}, dimensions={0}, use_global_device_ids=true | all-gather | bytes 491520 | tf_op jit(solution)/shard_map/all_gather | solution.py:403
  8.4 6.4 %collective-permute-start = (bf16[2,128,256]{2,1,0:T(8,128)(2,1)S(1)}, bf16[2,128,256]{2,1,0:T(8,128)(2,1)S(1)}, u32[]{:S(2)}, u32[]{:S(2)}) collective-permute-start(bf16[2,128,256]{2,1,0:T(8,128)(2,1)S(1)} %get-tuple-element.25.own_ref), channel_id=1, source_target_pairs={{0,4},{1,29},{2,6},{3,31},{4,8},{5,1},{6,10},{7,3},{8,12},{9,5},{1... | collective-permute-start | bytes 393224 | tf_op jit(solution)/shard_map/ppermute | solution.py:394
  14.8 6.5 %collective-permute-start.1 = (bf16[2,128,256]{2,1,0:T(8,128)(2,1)S(1)}, bf16[2,128,256]{2,1,0:T(8,128)(2,1)S(1)}, u32[]{:S(2)}, u32[]{:S(2)}) collective-permute-start(bf16[2,128,256]{2,1,0:T(8,128)(2,1)S(1)} %get-tuple-element.25.own_ref), channel_id=1, source_target_pairs={{0,6},{1,27},{2,8},{3,29},{4,10},{5,31},{6,12},{7,1},{8,14},{9,3},... | collective-permute-start | bytes 393224 | tf_op jit(solution)/shard_map/ppermute | solution.py:394
  21.3 5.2 %collective-permute-done.1.refs_1_ = bf16[2,128,256]{2,1,0:T(8,128)(2,1)S(1)} collective-permute-done((bf16[2,128,256]{2,1,0:T(8,128)(2,1)S(1)}, bf16[2,128,256]{2,1,0:T(8,128)(2,1)S(1)}, u32[]{:S(2)}, u32[]{:S(2)}) %collective-permute-start.1) | collective-permute-done | bytes 131104 | tf_op jit(solution)/shard_map/ppermute | solution.py:394
  26.6 5.9 %collective-permute-start.2 = (bf16[4,128,256]{2,1,0:T(8,128)(2,1)S(1)}, bf16[4,128,256]{2,1,0:T(8,128)(2,1)S(1)}, u32[]{:S(2)}, u32[]{:S(2)}) collective-permute-start(bf16[4,128,256]{2,1,0:T(8,128)(2,1)S(1)} %shard_map.120.refs_1_), channel_id=1, source_target_pairs={{0,6},{1,27},{2,8},{3,29},{4,10},{5,31},{6,12},{7,1},{8,14},{9,3},... | collective-permute-start | bytes 786440 | tf_op jit(solution)/shard_map/ppermute | solution.py:394
  32.4 4.7 %collective-permute-start.4 = (bf16[2,128,256]{2,1,0:T(8,128)(2,1)S(1)}, bf16[2,128,256]{2,1,0:T(8,128)(2,1)S(1)}, u32[]{:S(2)}, u32[]{:S(2)}) collective-permute-start(bf16[2,128,256]{2,1,0:T(8,128)(2,1)S(1)} %get-tuple-element.25.own_ref), channel_id=1, source_target_pairs={{0,2},{1,31},{2,4},{3,1},{4,6},{5,3},{6,8},{7,5},{8,10},{9,7},{10,... | collective-permute-start | bytes 393224 | tf_op jit(solution)/shard_map/ppermute | solution.py:394
  37.1 7.8 %collective-permute-done.4.refs_0_ = bf16[2,128,256]{2,1,0:T(8,128)(2,1)S(1)} collective-permute-done((bf16[2,128,256]{2,1,0:T(8,128)(2,1)S(1)}, bf16[2,128,256]{2,1,0:T(8,128)(2,1)S(1)}, u32[]{:S(2)}, u32[]{:S(2)}) %collective-permute-start.4) | collective-permute-done | bytes 131104 | tf_op jit(solution)/shard_map/ppermute | solution.py:394
  45.0 5.8 %collective-permute-start.5 = (bf16[2,128,256]{2,1,0:T(8,128)(2,1)S(1)}, bf16[2,128,256]{2,1,0:T(8,128)(2,1)S(1)}, u32[]{:S(2)}, u32[]{:S(2)}) collective-permute-start(bf16[2,128,256]{2,1,0:T(8,128)(2,1)S(1)} %collective-permute-done.4.refs_0_), channel_id=1, source_target_pairs={{0,6},{1,27},{2,8},{3,29},{4,10},{5,31},{6,12},{7,1},{8,14},{9,3},... | collective-permute-start | bytes 393224 | tf_op jit(solution)/shard_map/ppermute | solution.py:394
  51.9 4.1 %collective-permute-done.5.refs_2_ = bf16[2,128,256]{2,1,0:T(8,128)(2,1)S(1)} collective-permute-done((bf16[2,128,256]{2,1,0:T(8,128)(2,1)S(1)}, bf16[2,128,256]{2,1,0:T(8,128)(2,1)S(1)}, u32[]{:S(2)}, u32[]{:S(2)}) %collective-permute-start.5) | collective-permute-done | bytes 131104 | tf_op jit(solution)/shard_map/ppermute | solution.py:394
  56.1 1.9 %collective-permute-start.6 = (bf16[12,128,256]{2,1,0:T(8,128)(2,1)S(1)}, bf16[12,128,256]{2,1,0:T(8,128)(2,1)S(1)}, u32[]{:S(2)}, u32[]{:S(2)}) collective-permute-start(bf16[12,128,256]{2,1,0:T(8,128)(2,1)S(1)} %shard_map.122), channel_id=1, source_target_pairs={{0,1},{1,0},{2,3},{3,2},{4,5},{5,4},{6,7},{7,6},{8,9},{9,8},{10,11... | collective-permute-start | bytes 2359304 | tf_op jit(solution)/shard_map/ppermute | solution.py:423
  58.0 6.2 %collective-permute-start.3 = (bf16[4,128,256]{2,1,0:T(8,128)(2,1)S(1)}, bf16[4,128,256]{2,1,0:T(8,128)(2,1)S(1)}, u32[]{:S(2)}, u32[]{:S(2)}) collective-permute-start(bf16[4,128,256]{2,1,0:T(8,128)(2,1)S(1)} %collective-permute-done.2.refs_3_), channel_id=1, source_target_pairs={{0,4},{1,29},{2,6},{3,31},{4,8},{5,1},{6,10},{7,3},{8,12},{9,5},{1... | collective-permute-start | bytes 786440 | tf_op jit(solution)/shard_map/ppermute | solution.py:394
  64.2 3.5 %collective-permute-start.7 = (bf16[128,256]{1,0:T(8,128)(2,1)S(1)}, bf16[128,256]{1,0:T(8,128)(2,1)S(1)}, u32[]{:S(2)}, u32[]{:S(2)}) collective-permute-start(bf16[128,256]{1,0:T(8,128)(2,1)S(1)} %get-tuple-element.33), channel_id=1, source_target_pairs={{0,64},{64,0},{128,192},{192,128},{1,65},{65,1},{129,193},{193,129... | collective-permute-start | bytes 196616 | tf_op jit(solution)/shard_map/ppermute | solution.py:387
  67.7 2.7 %collective-permute-done.7 = bf16[128,256]{1,0:T(8,128)(2,1)S(1)} collective-permute-done((bf16[128,256]{1,0:T(8,128)(2,1)S(1)}, bf16[128,256]{1,0:T(8,128)(2,1)S(1)}, u32[]{:S(2)}, u32[]{:S(2)}) %collective-permute-start.7) | collective-permute-done | bytes 65568 | tf_op jit(solution)/shard_map/ppermute | solution.py:387
  70.4 5.1 %collective-permute-start.8 = (bf16[128,256]{1,0:T(8,128)(2,1)S(1)}, bf16[128,256]{1,0:T(8,128)(2,1)S(1)}, u32[]{:S(2)}, u32[]{:S(2)}) collective-permute-start(bf16[128,256]{1,0:T(8,128)(2,1)S(1)} %add.13), channel_id=1, source_target_pairs={{0,128},{64,192},{128,0},{192,64},{1,129},{65,193},{129,1},{193,65... | collective-permute-start | bytes 196616 | tf_op jit(solution)/shard_map/ppermute | solution.py:387
  75.5 2.6 %collective-permute-done.8 = bf16[128,256]{1,0:T(8,128)(2,1)S(1)} collective-permute-done((bf16[128,256]{1,0:T(8,128)(2,1)S(1)}, bf16[128,256]{1,0:T(8,128)(2,1)S(1)}, u32[]{:S(2)}, u32[]{:S(2)}) %collective-permute-start.8) | collective-permute-done | bytes 65568 | tf_op jit(solution)/shard_map/ppermute | solution.py:387
  78.1 2.7 %collective-permute-start.9 = (bf16[128,256]{1,0:T(8,128)(2,1)S(1)}, bf16[128,256]{1,0:T(8,128)(2,1)S(1)}, u32[]{:S(2)}, u32[]{:S(2)}) collective-permute-start(bf16[128,256]{1,0:T(8,128)(2,1)S(1)} %add.14), channel_id=1, source_target_pairs={{0,256},{256,0},{1,257},{257,1},{2,258},{258,2},{3,259},{259,3},{4... | collective-permute-start | bytes 196616 | tf_op jit(solution)/shard_map/ppermute | solution.py:387
  80.8 4.9 %collective-permute-done.9 = bf16[128,256]{1,0:T(8,128)(2,1)S(1)} collective-permute-done((bf16[128,256]{1,0:T(8,128)(2,1)S(1)}, bf16[128,256]{1,0:T(8,128)(2,1)S(1)}, u32[]{:S(2)}, u32[]{:S(2)}) %collective-permute-start.9) | collective-permute-done | bytes 65568 | tf_op jit(solution)/shard_map/ppermute | solution.py:387
  85.8 2.2 %all_gather.11.refs_5_ = bf16[8,128,256]{2,1,0:T(8,128)(2,1)S(1)} all-gather(bf16[4,128,256]{2,1,0:T(8,128)(2,1)S(1)} %collective-permute-done.3), channel_id=1, replica_groups=mesh['xh'=2,'y'=4,'xl'=2,'z'=16,'c'=2] {'c'}, dimensions={0}, use_global_device_ids=true | all-gather | bytes 786432 | tf_op jit(solution)/shard_map/all_gather | solution.py:397
  88.0 5.3 %shard_map.123 = (bf16[64,32]{1,0:T(8,128)(2,1)S(1)}, bf16[64,32]{1,0:T(8,128)(2,1)S(1)}) custom-call(s32[4]{0:T(128)S(1)} %pad_add_fusion.where_ref, bf16[128,256]{1,0:T(8,128)(2,1)S(1)} %add.15.q_ref, bf16[2,128,256]{2,1,0:T(8,128)(2,1)S(1)} %get-tuple-element.25.own_ref, bf16[2,128,256]{2,1,0:T(8,128)(2,1)S(1)} %collective-permute-done.4.refs_0_, ...), custom_call_target="tpu_custom_call" | custom-call | flops 5000000000 | bytes 4000000 | tf_op jit(solution)/shard_map/pallas_call | solution.py:291
  93.3 3.1 %collective-permute-start.10 = (bf16[64,32]{1,0:T(8,128)(2,1)S(1)}, bf16[64,32]{1,0:T(8,128)(2,1)S(1)}, u32[]{:S(2)}, u32[]{:S(2)}) collective-permute-start(bf16[64,32]{1,0:T(8,128)(2,1)S(1)} %get-tuple-element.44), channel_id=1, source_target_pairs={{0,32},{32,0},{1,33},{33,1},{2,34},{34,2},{3,35},{35,3},{4,36},{36... | collective-permute-start | bytes 12296 | tf_op jit(solution)/shard_map/ppermute | solution.py:438
  96.4 5.5 %collective-permute-start.11 = (bf16[64,32]{1,0:T(8,128)(2,1)S(1)}, bf16[64,32]{1,0:T(8,128)(2,1)S(1)}, u32[]{:S(2)}, u32[]{:S(2)}) collective-permute-start(bf16[64,32]{1,0:T(8,128)(2,1)S(1)} %get-tuple-element.43.kept_ref), channel_id=1, source_target_pairs={{64,0},{32,96},{128,64},{96,160},{192,128},{160,224},{256,192},{22... | collective-permute-start | bytes 12296 | tf_op jit(solution)/shard_map/ppermute | solution.py:439
  101.9 2.7 %collective-permute-start.12 = (bf16[64,32]{1,0:T(8,128)(2,1)S(1)}, bf16[64,32]{1,0:T(8,128)(2,1)S(1)}, u32[]{:S(2)}, u32[]{:S(2)}) collective-permute-start(bf16[64,32]{1,0:T(8,128)(2,1)S(1)} %get-tuple-element.44), channel_id=1, source_target_pairs={{64,32},{32,64},{128,96},{96,128},{192,160},{160,192},{256,224},{2... | collective-permute-start | bytes 12296 | tf_op jit(solution)/shard_map/ppermute | solution.py:440
  104.7 5.0 %collective-permute-done.12.crossed_ref = bf16[64,32]{1,0:T(8,128)(2,1)S(1)} collective-permute-done((bf16[64,32]{1,0:T(8,128)(2,1)S(1)}, bf16[64,32]{1,0:T(8,128)(2,1)S(1)}, u32[]{:S(2)}, u32[]{:S(2)}) %collective-permute-start.12) | collective-permute-done | bytes 4128 | tf_op jit(solution)/shard_map/ppermute | solution.py:440
  (23 shorter events, 3.4 us)
Async XLA Ops:
  8.4 12.9 %collective-permute-start = (bf16[2,128,256]{2,1,0:T(8,128)(2,1)S(1)}, bf16[2,128,256]{2,1,0:T(8,128)(2,1)S(1)}, u32[]{:S(2)}, u32[]{:S(2)}) collective-permute-start(bf16[2,128,256]{2,1,0:T(8,128)(2,1)S(1)} %get-tuple-element.25.own_ref), channel_id=1, source_target_pairs={{0,4},{1,29},{2,6},{3,31},{4,8},{5,1},{6,10},{7,3},{8,12},{9,5},{1... | collective-permute-start | bytes 393224 | tf_op jit(solution)/shard_map/ppermute | solution.py:394
  14.8 11.8 %collective-permute-start.1 = (bf16[2,128,256]{2,1,0:T(8,128)(2,1)S(1)}, bf16[2,128,256]{2,1,0:T(8,128)(2,1)S(1)}, u32[]{:S(2)}, u32[]{:S(2)}) collective-permute-start(bf16[2,128,256]{2,1,0:T(8,128)(2,1)S(1)} %get-tuple-element.25.own_ref), channel_id=1, source_target_pairs={{0,6},{1,27},{2,8},{3,29},{4,10},{5,31},{6,12},{7,1},{8,14},{9,3},... | collective-permute-start | bytes 393224 | tf_op jit(solution)/shard_map/ppermute | solution.py:394
  26.6 25.3 %collective-permute-start.2 = (bf16[4,128,256]{2,1,0:T(8,128)(2,1)S(1)}, bf16[4,128,256]{2,1,0:T(8,128)(2,1)S(1)}, u32[]{:S(2)}, u32[]{:S(2)}) collective-permute-start(bf16[4,128,256]{2,1,0:T(8,128)(2,1)S(1)} %shard_map.120.refs_1_), channel_id=1, source_target_pairs={{0,6},{1,27},{2,8},{3,29},{4,10},{5,31},{6,12},{7,1},{8,14},{9,3},... | collective-permute-start | bytes 786440 | tf_op jit(solution)/shard_map/ppermute | solution.py:394
  32.4 12.5 %collective-permute-start.4 = (bf16[2,128,256]{2,1,0:T(8,128)(2,1)S(1)}, bf16[2,128,256]{2,1,0:T(8,128)(2,1)S(1)}, u32[]{:S(2)}, u32[]{:S(2)}) collective-permute-start(bf16[2,128,256]{2,1,0:T(8,128)(2,1)S(1)} %get-tuple-element.25.own_ref), channel_id=1, source_target_pairs={{0,2},{1,31},{2,4},{3,1},{4,6},{5,3},{6,8},{7,5},{8,10},{9,7},{10,... | collective-permute-start | bytes 393224 | tf_op jit(solution)/shard_map/ppermute | solution.py:394
  45.0 11.1 %collective-permute-start.5 = (bf16[2,128,256]{2,1,0:T(8,128)(2,1)S(1)}, bf16[2,128,256]{2,1,0:T(8,128)(2,1)S(1)}, u32[]{:S(2)}, u32[]{:S(2)}) collective-permute-start(bf16[2,128,256]{2,1,0:T(8,128)(2,1)S(1)} %collective-permute-done.4.refs_0_), channel_id=1, source_target_pairs={{0,6},{1,27},{2,8},{3,29},{4,10},{5,31},{6,12},{7,1},{8,14},{9,3},... | collective-permute-start | bytes 393224 | tf_op jit(solution)/shard_map/ppermute | solution.py:394
  56.1 29.7 %collective-permute-start.6 = (bf16[12,128,256]{2,1,0:T(8,128)(2,1)S(1)}, bf16[12,128,256]{2,1,0:T(8,128)(2,1)S(1)}, u32[]{:S(2)}, u32[]{:S(2)}) collective-permute-start(bf16[12,128,256]{2,1,0:T(8,128)(2,1)S(1)} %shard_map.122), channel_id=1, source_target_pairs={{0,1},{1,0},{2,3},{3,2},{4,5},{5,4},{6,7},{7,6},{8,9},{9,8},{10,11... | collective-permute-start | bytes 2359304 | tf_op jit(solution)/shard_map/ppermute | solution.py:423
  58.0 27.8 %collective-permute-start.3 = (bf16[4,128,256]{2,1,0:T(8,128)(2,1)S(1)}, bf16[4,128,256]{2,1,0:T(8,128)(2,1)S(1)}, u32[]{:S(2)}, u32[]{:S(2)}) collective-permute-start(bf16[4,128,256]{2,1,0:T(8,128)(2,1)S(1)} %collective-permute-done.2.refs_3_), channel_id=1, source_target_pairs={{0,4},{1,29},{2,6},{3,31},{4,8},{5,1},{6,10},{7,3},{8,12},{9,5},{1... | collective-permute-start | bytes 786440 | tf_op jit(solution)/shard_map/ppermute | solution.py:394
  64.2 6.2 %collective-permute-start.7 = (bf16[128,256]{1,0:T(8,128)(2,1)S(1)}, bf16[128,256]{1,0:T(8,128)(2,1)S(1)}, u32[]{:S(2)}, u32[]{:S(2)}) collective-permute-start(bf16[128,256]{1,0:T(8,128)(2,1)S(1)} %get-tuple-element.33), channel_id=1, source_target_pairs={{0,64},{64,0},{128,192},{192,128},{1,65},{65,1},{129,193},{193,129... | collective-permute-start | bytes 196616 | tf_op jit(solution)/shard_map/ppermute | solution.py:387
  70.4 7.7 %collective-permute-start.8 = (bf16[128,256]{1,0:T(8,128)(2,1)S(1)}, bf16[128,256]{1,0:T(8,128)(2,1)S(1)}, u32[]{:S(2)}, u32[]{:S(2)}) collective-permute-start(bf16[128,256]{1,0:T(8,128)(2,1)S(1)} %add.13), channel_id=1, source_target_pairs={{0,128},{64,192},{128,0},{192,64},{1,129},{65,193},{129,1},{193,65... | collective-permute-start | bytes 196616 | tf_op jit(solution)/shard_map/ppermute | solution.py:387
  78.1 7.7 %collective-permute-start.9 = (bf16[128,256]{1,0:T(8,128)(2,1)S(1)}, bf16[128,256]{1,0:T(8,128)(2,1)S(1)}, u32[]{:S(2)}, u32[]{:S(2)}) collective-permute-start(bf16[128,256]{1,0:T(8,128)(2,1)S(1)} %add.14), channel_id=1, source_target_pairs={{0,256},{256,0},{1,257},{257,1},{2,258},{258,2},{3,259},{259,3},{4... | collective-permute-start | bytes 196616 | tf_op jit(solution)/shard_map/ppermute | solution.py:387
  88.0 21.7 %copy-start = (bf16[32,512]{1,0:T(8,128)(2,1)S(1)}, bf16[32,512]{1,0:T(8,128)(2,1)}, u32[]{:S(2)}) copy-start(bf16[32,512]{1,0:T(8,128)(2,1)} %proj_w_ref.1) | copy-start | bytes 98308
  88.0 21.7 %copy-start.1 = (f32[3,512]{1,0:T(4,128)S(1)}, f32[3,512]{1,0:T(4,128)}, u32[]{:S(2)}) copy-start(f32[3,512]{1,0:T(4,128)} %time_w_ref.1) | copy-start | bytes 18436
  88.0 21.7 %copy-start.2 = (f32[512]{0:T(512)S(1)}, f32[512]{0:T(512)}, u32[]{:S(2)}) copy-start(f32[512]{0:T(512)} %param.21) | copy-start | bytes 6148
  88.0 21.7 %copy-start.3 = (f32[512]{0:T(512)S(1)}, f32[512]{0:T(512)}, u32[]{:S(2)}) copy-start(f32[512]{0:T(512)} %param.23) | copy-start | bytes 6148
  93.3 11.3 %collective-permute-start.10 = (bf16[64,32]{1,0:T(8,128)(2,1)S(1)}, bf16[64,32]{1,0:T(8,128)(2,1)S(1)}, u32[]{:S(2)}, u32[]{:S(2)}) collective-permute-start(bf16[64,32]{1,0:T(8,128)(2,1)S(1)} %get-tuple-element.44), channel_id=1, source_target_pairs={{0,32},{32,0},{1,33},{33,1},{2,34},{34,2},{3,35},{35,3},{4,36},{36... | collective-permute-start | bytes 12296 | tf_op jit(solution)/shard_map/ppermute | solution.py:438
  96.4 8.3 %collective-permute-start.11 = (bf16[64,32]{1,0:T(8,128)(2,1)S(1)}, bf16[64,32]{1,0:T(8,128)(2,1)S(1)}, u32[]{:S(2)}, u32[]{:S(2)}) collective-permute-start(bf16[64,32]{1,0:T(8,128)(2,1)S(1)} %get-tuple-element.43.kept_ref), channel_id=1, source_target_pairs={{64,0},{32,96},{128,64},{96,160},{192,128},{160,224},{256,192},{22... | collective-permute-start | bytes 12296 | tf_op jit(solution)/shard_map/ppermute | solution.py:439
  101.9 7.7 %collective-permute-start.12 = (bf16[64,32]{1,0:T(8,128)(2,1)S(1)}, bf16[64,32]{1,0:T(8,128)(2,1)S(1)}, u32[]{:S(2)}, u32[]{:S(2)}) collective-permute-start(bf16[64,32]{1,0:T(8,128)(2,1)S(1)} %get-tuple-element.44), channel_id=1, source_target_pairs={{64,32},{32,64},{128,96},{96,128},{192,160},{160,192},{256,224},{2... | collective-permute-start | bytes 12296 | tf_op jit(solution)/shard_map/ppermute | solution.py:440

commit v6 on v5

--- a/solution.py
+++ b/solution.py
@@ -404,25 +404,26 @@
     own, queries = picked(where, gathered, frame_maps.shape[1])
     weights = banded_weights(conv1_w, conv1_b, conv2_w, conv2_b)
     near = []
-    for distance in (1, 2, 3):
+    for distance in (1, 2):
         near.append(along(own, distance))
     queries = queries + flip("y", y_count, 1)(queries)
-    near[1], near[2] = lax.optimization_barrier((near[1], near[2]))
-
-    pair = joined(near[1], near[2])
-    far5 = along(pair, 3)
-    far4 = along(near[0], 3)
+    near = lax.optimization_barrier(near)
+
+    ring = [joined(*near)]
+    ring.append(along(ring[0], 2))
     if y_count > 2:
-        queries = queries + flip("y", y_count, 2)(behind(queries, pair))
-    far5, weights = lax.optimization_barrier((far5, weights))
-
-    far7 = along(far5, 2)
+        queries = queries + flip("y", y_count, 2)(behind(queries, ring[0]))
+    ring[1], weights = lax.optimization_barrier((ring[1], weights))
+
+    ring.append(along(ring[1], 2))
     if xh_count > 1:
-        queries = queries + flip("xh", xh_count, 1)(behind(queries, far5))
-    mine = [near[0], pair, far4, far5]
-    cross = lax.ppermute(joined(*mine), "c", swap)
-    far7, cross, queries = lax.optimization_barrier((far7, cross, queries))
-    spread = mine + [cross, both(far7)]
+        queries = queries + flip("xh", xh_count, 1)(behind(queries, ring[1]))
+    ring[2] = lax.optimization_barrier(ring[2])
+
+    last = along(ring[2], 2)
+    cross = lax.ppermute(joined(*ring), "c", swap)
+    last, cross, queries = lax.optimization_barrier((last, cross, queries))
+    spread = ring + [cross, both(last)]
 
     kept, sent = pooled_costs(where, queries, own, spread, *weights)
 

time: 112 us -> 101 us (0.902)
  the two profiles are of different devices: /device:TPU:68 before, /device:TPU:100 now
where the time goes in v6:
time: 101 us; the launch traced here: 100 us
  starting transfers between devices  53.4 us (53%)
  waiting for transfers between devices  28 us (28%)
  Pallas kernels  10.1 us (10%)
  blocking collectives  8.35 us (8%)
    ppermute x5, starting transfers between devices, along(): return lax.ppermute(block, ('z', 'c'), pairs)  29.7 us
    ppermute x5, waiting for transfers between devices, along(): return lax.ppermute(block, ('z', 'c'), pairs)  14.1 us
    ppermute x3, starting transfers between devices, flip(): lax.ppermute(v, axis, [(i, i ^ step) for i in range(count)])  11.3 us
    ppermute x3, waiting for transfers between devices, flip(): lax.ppermute(v, axis, [(i, i ^ step) for i in range(count)])  10.2 us
    all_gather x1, blocking collectives, one_device(): gathered = lax.all_gather(message, ('xl', 'c'), axis=0)  6.17 us
    pallas_call x1, Pallas kernels, pooled_costs(): pl.pallas_call(functools.partial(cost_kernel, z_count), out_shape=(jax.Sh...  5.29 us
    ppermute x1, starting transfers between devices, one_device(): straight = lax.ppermute(kept, ('xh', 'y', 'xl'), frame_pairs(False))  5.16 us
    ppermute x1, starting transfers between devices, one_device(): crossed = lax.ppermute(sent, ('xh', 'y', 'xl'), frame_pairs(True))  3.41 us
  transfers between devices with their start and end apart: 12, of which 8 were waited for; matrix products, arithmetic and copies ran while one was open for 0% of the time, Pallas kernels for 1%

profile of v6, /device:TPU:100, one launch (start us, length us, event | category | flops | bytes accessed | tf_op | source)
XLA Modules:
  0.0 100.1 jit_solution(16864084618808646477)
XLA Ops:
  0.1 1.6 %shard_map.118 = bf16[192,256]{1,0:T(8,128)(2,1)S(1)} custom-call(s32[4]{0:T(128)S(1)} %pad_add_fusion.where_ref, bf16[2,64,256]{2,1,0:T(8,128)(2,1)} %maps_hbm.1, bf16[1,64,256]{2,1,0:T(8,128)(2,1)} %table_hbm.1, s32[1,64]{1,0:T(1,128)} %bitcast.16, s32[1,64]{1,0:T(1,128)} %bitcast.17), custom_call_target="tpu_custom_call" | custom-call | flops 2000000 | bytes 200000 | tf_op jit(solution)/shard_map/pallas_call | solution.py:64
  1.7 6.2 %all-gather = bf16[768,256]{1,0:T(8,128)(2,1)S(1)} all-gather(bf16[192,256]{1,0:T(8,128)(2,1)S(1)} %shard_map.118), channel_id=2, replica_groups=mesh['xh'=2,'y'=4,'xl'=2,'z'=16,'c'=2] {'xl','c'}, dimensions={0}, use_global_device_ids=true | all-gather | bytes 491520 | tf_op jit(solution)/shard_map/all_gather | solution.py:403
  8.4 5.0 %collective-permute-start = (bf16[2,128,256]{2,1,0:T(8,128)(2,1)S(1)}, bf16[2,128,256]{2,1,0:T(8,128)(2,1)S(1)}, u32[]{:S(2)}, u32[]{:S(2)}) collective-permute-start(bf16[2,128,256]{2,1,0:T(8,128)(2,1)S(1)} %get-tuple-element.25.own_ref), channel_id=1, source_target_pairs={{0,2},{1,31},{2,4},{3,1},{4,6},{5,3},{6,8},{7,5},{8,10},{9,7},{10,... | collective-permute-start | bytes 393224 | tf_op jit(solution)/shard_map/ppermute | solution.py:394
  13.4 5.2 %collective-permute-start.1 = (bf16[2,128,256]{2,1,0:T(8,128)(2,1)S(1)}, bf16[2,128,256]{2,1,0:T(8,128)(2,1)S(1)}, u32[]{:S(2)}, u32[]{:S(2)}) collective-permute-start(bf16[2,128,256]{2,1,0:T(8,128)(2,1)S(1)} %get-tuple-element.25.own_ref), channel_id=1, source_target_pairs={{0,4},{1,29},{2,6},{3,31},{4,8},{5,1},{6,10},{7,3},{8,12},{9,5},{1... | collective-permute-start | bytes 393224 | tf_op jit(solution)/shard_map/ppermute | solution.py:394
  18.6 3.8 %collective-permute-done.1.refs_1_ = bf16[2,128,256]{2,1,0:T(8,128)(2,1)S(1)} collective-permute-done((bf16[2,128,256]{2,1,0:T(8,128)(2,1)S(1)}, bf16[2,128,256]{2,1,0:T(8,128)(2,1)S(1)}, u32[]{:S(2)}, u32[]{:S(2)}) %collective-permute-start.1) | collective-permute-done | bytes 131104 | tf_op jit(solution)/shard_map/ppermute | solution.py:394
  22.5 6.5 %collective-permute-start.2 = (bf16[4,128,256]{2,1,0:T(8,128)(2,1)S(1)}, bf16[4,128,256]{2,1,0:T(8,128)(2,1)S(1)}, u32[]{:S(2)}, u32[]{:S(2)}) collective-permute-start(bf16[4,128,256]{2,1,0:T(8,128)(2,1)S(1)} %shard_map.120.refs_0_), channel_id=1, source_target_pairs={{0,4},{1,29},{2,6},{3,31},{4,8},{5,1},{6,10},{7,3},{8,12},{9,5},{1... | collective-permute-start | bytes 786440 | tf_op jit(solution)/shard_map/ppermute | solution.py:394
  30.1 4.8 %collective-permute-done.2.refs_1_ = bf16[4,128,256]{2,1,0:T(8,128)(2,1)S(1)} collective-permute-done((bf16[4,128,256]{2,1,0:T(8,128)(2,1)S(1)}, bf16[4,128,256]{2,1,0:T(8,128)(2,1)S(1)}, u32[]{:S(2)}, u32[]{:S(2)}) %collective-permute-start.2) | collective-permute-done | bytes 262176 | tf_op jit(solution)/shard_map/ppermute | solution.py:394
  34.9 6.5 %collective-permute-start.3 = (bf16[4,128,256]{2,1,0:T(8,128)(2,1)S(1)}, bf16[4,128,256]{2,1,0:T(8,128)(2,1)S(1)}, u32[]{:S(2)}, u32[]{:S(2)}) collective-permute-start(bf16[4,128,256]{2,1,0:T(8,128)(2,1)S(1)} %collective-permute-done.2.refs_1_), channel_id=1, source_target_pairs={{0,4},{1,29},{2,6},{3,31},{4,8},{5,1},{6,10},{7,3},{8,12},{9,5},{1... | collective-permute-start | bytes 786440 | tf_op jit(solution)/shard_map/ppermute | solution.py:394
  41.4 5.5 %collective-permute-done.3.refs_2_ = bf16[4,128,256]{2,1,0:T(8,128)(2,1)S(1)} collective-permute-done((bf16[4,128,256]{2,1,0:T(8,128)(2,1)S(1)}, bf16[4,128,256]{2,1,0:T(8,128)(2,1)S(1)}, u32[]{:S(2)}, u32[]{:S(2)}) %collective-permute-start.3) | collective-permute-done | bytes 262176 | tf_op jit(solution)/shard_map/ppermute | solution.py:394
  46.9 1.9 %collective-permute-start.5 = (bf16[12,128,256]{2,1,0:T(8,128)(2,1)S(1)}, bf16[12,128,256]{2,1,0:T(8,128)(2,1)S(1)}, u32[]{:S(2)}, u32[]{:S(2)}) collective-permute-start(bf16[12,128,256]{2,1,0:T(8,128)(2,1)S(1)} %shard_map.122), channel_id=1, source_target_pairs={{0,1},{1,0},{2,3},{3,2},{4,5},{5,4},{6,7},{7,6},{8,9},{9,8},{10,11... | collective-permute-start | bytes 2359304 | tf_op jit(solution)/shard_map/ppermute | solution.py:424
  48.8 6.5 %collective-permute-start.4 = (bf16[4,128,256]{2,1,0:T(8,128)(2,1)S(1)}, bf16[4,128,256]{2,1,0:T(8,128)(2,1)S(1)}, u32[]{:S(2)}, u32[]{:S(2)}) collective-permute-start(bf16[4,128,256]{2,1,0:T(8,128)(2,1)S(1)} %collective-permute-done.3.refs_2_), channel_id=1, source_target_pairs={{0,4},{1,29},{2,6},{3,31},{4,8},{5,1},{6,10},{7,3},{8,12},{9,5},{1... | collective-permute-start | bytes 786440 | tf_op jit(solution)/shard_map/ppermute | solution.py:394
  55.3 3.5 %collective-permute-start.6 = (bf16[128,256]{1,0:T(8,128)(2,1)S(1)}, bf16[128,256]{1,0:T(8,128)(2,1)S(1)}, u32[]{:S(2)}, u32[]{:S(2)}) collective-permute-start(bf16[128,256]{1,0:T(8,128)(2,1)S(1)} %get-tuple-element.33), channel_id=1, source_target_pairs={{0,64},{64,0},{128,192},{192,128},{1,65},{65,1},{129,193},{193,129... | collective-permute-start | bytes 196616 | tf_op jit(solution)/shard_map/ppermute | solution.py:387
  58.8 2.7 %collective-permute-done.6 = bf16[128,256]{1,0:T(8,128)(2,1)S(1)} collective-permute-done((bf16[128,256]{1,0:T(8,128)(2,1)S(1)}, bf16[128,256]{1,0:T(8,128)(2,1)S(1)}, u32[]{:S(2)}, u32[]{:S(2)}) %collective-permute-start.6) | collective-permute-done | bytes 65568 | tf_op jit(solution)/shard_map/ppermute | solution.py:387
  61.5 5.1 %collective-permute-start.7 = (bf16[128,256]{1,0:T(8,128)(2,1)S(1)}, bf16[128,256]{1,0:T(8,128)(2,1)S(1)}, u32[]{:S(2)}, u32[]{:S(2)}) collective-permute-start(bf16[128,256]{1,0:T(8,128)(2,1)S(1)} %add.13), channel_id=1, source_target_pairs={{0,128},{64,192},{128,0},{192,64},{1,129},{65,193},{129,1},{193,65... | collective-permute-start | bytes 196616 | tf_op jit(solution)/shard_map/ppermute | solution.py:387
  66.6 2.6 %collective-permute-done.7 = bf16[128,256]{1,0:T(8,128)(2,1)S(1)} collective-permute-done((bf16[128,256]{1,0:T(8,128)(2,1)S(1)}, bf16[128,256]{1,0:T(8,128)(2,1)S(1)}, u32[]{:S(2)}, u32[]{:S(2)}) %collective-permute-start.7) | collective-permute-done | bytes 65568 | tf_op jit(solution)/shard_map/ppermute | solution.py:387
  69.2 2.7 %collective-permute-start.8 = (bf16[128,256]{1,0:T(8,128)(2,1)S(1)}, bf16[128,256]{1,0:T(8,128)(2,1)S(1)}, u32[]{:S(2)}, u32[]{:S(2)}) collective-permute-start(bf16[128,256]{1,0:T(8,128)(2,1)S(1)} %add.14), channel_id=1, source_target_pairs={{0,256},{256,0},{1,257},{257,1},{2,258},{258,2},{3,259},{259,3},{4... | collective-permute-start | bytes 196616 | tf_op jit(solution)/shard_map/ppermute | solution.py:387
  71.9 4.9 %collective-permute-done.8 = bf16[128,256]{1,0:T(8,128)(2,1)S(1)} collective-permute-done((bf16[128,256]{1,0:T(8,128)(2,1)S(1)}, bf16[128,256]{1,0:T(8,128)(2,1)S(1)}, u32[]{:S(2)}, u32[]{:S(2)}) %collective-permute-start.8) | collective-permute-done | bytes 65568 | tf_op jit(solution)/shard_map/ppermute | solution.py:387
  76.9 2.2 %all_gather.11.refs_4_ = bf16[8,128,256]{2,1,0:T(8,128)(2,1)S(1)} all-gather(bf16[4,128,256]{2,1,0:T(8,128)(2,1)S(1)} %collective-permute-done.4), channel_id=1, replica_groups=mesh['xh'=2,'y'=4,'xl'=2,'z'=16,'c'=2] {'c'}, dimensions={0}, use_global_device_ids=true | all-gather | bytes 786432 | tf_op jit(solution)/shard_map/all_gather | solution.py:397
  79.1 5.3 %shard_map.123 = (bf16[64,32]{1,0:T(8,128)(2,1)S(1)}, bf16[64,32]{1,0:T(8,128)(2,1)S(1)}) custom-call(s32[4]{0:T(128)S(1)} %pad_add_fusion.where_ref, bf16[128,256]{1,0:T(8,128)(2,1)S(1)} %add.15.q_ref, bf16[2,128,256]{2,1,0:T(8,128)(2,1)S(1)} %get-tuple-element.25.own_ref, bf16[4,128,256]{2,1,0:T(8,128)(2,1)S(1)} %shard_map.120.refs_0_, ...), custom_call_target="tpu_custom_call" | custom-call | flops 5000000000 | bytes 4000000 | tf_op jit(solution)/shard_map/pallas_call | solution.py:291
  84.4 5.2 %collective-permute-start.10 = (bf16[64,32]{1,0:T(8,128)(2,1)S(1)}, bf16[64,32]{1,0:T(8,128)(2,1)S(1)}, u32[]{:S(2)}, u32[]{:S(2)}) collective-permute-start(bf16[64,32]{1,0:T(8,128)(2,1)S(1)} %get-tuple-element.43.kept_ref), channel_id=1, source_target_pairs={{64,0},{32,96},{128,64},{96,160},{192,128},{160,224},{256,192},{22... | collective-permute-start | bytes 12296 | tf_op jit(solution)/shard_map/ppermute | solution.py:440
  89.6 3.4 %collective-permute-start.11 = (bf16[64,32]{1,0:T(8,128)(2,1)S(1)}, bf16[64,32]{1,0:T(8,128)(2,1)S(1)}, u32[]{:S(2)}, u32[]{:S(2)}) collective-permute-start(bf16[64,32]{1,0:T(8,128)(2,1)S(1)} %get-tuple-element.44), channel_id=1, source_target_pairs={{64,32},{32,64},{128,96},{96,128},{192,160},{160,192},{256,224},{2... | collective-permute-start | bytes 12296 | tf_op jit(solution)/shard_map/ppermute | solution.py:441
  93.0 1.9 %collective-permute-start.9 = (bf16[64,32]{1,0:T(8,128)(2,1)S(1)}, bf16[64,32]{1,0:T(8,128)(2,1)S(1)}, u32[]{:S(2)}, u32[]{:S(2)}) collective-permute-start(bf16[64,32]{1,0:T(8,128)(2,1)S(1)} %get-tuple-element.44), channel_id=1, source_target_pairs={{0,32},{32,0},{1,33},{33,1},{2,34},{34,2},{3,35},{35,3},{4,36},{36... | collective-permute-start | bytes 12296 | tf_op jit(solution)/shard_map/ppermute | solution.py:439
  94.9 2.4 %collective-permute-done.11.crossed_ref = bf16[64,32]{1,0:T(8,128)(2,1)S(1)} collective-permute-done((bf16[64,32]{1,0:T(8,128)(2,1)S(1)}, bf16[64,32]{1,0:T(8,128)(2,1)S(1)}, u32[]{:S(2)}, u32[]{:S(2)}) %collective-permute-start.11) | collective-permute-done | bytes 4128 | tf_op jit(solution)/shard_map/ppermute | solution.py:441
  98.6 1.5 %shard_map.124 = bf16[64,2,512]{2,1,0:T(2,128)(2,1)} custom-call(s32[4]{0:T(128)S(1)} %pad_add_fusion.where_ref, bf16[64,32]{1,0:T(8,128)(2,1)S(1)} %get-tuple-element.43.kept_ref, bf16[64,32]{1,0:T(8,128)(2,1)S(1)} %collective-permute-done.9.partner_ref, bf16[64,32]{1,0:T(8,128)(2,1)S(1)} %collective-permute-done.10.straight_ref, ...), custom_call_target="tpu_custom_call" | custom-call | tf_op jit(solution)/shard_map/pallas_call | solution.py:353
  (21 shorter events, 3.2 us)
Async XLA Ops:
  8.4 10.2 %collective-permute-start = (bf16[2,128,256]{2,1,0:T(8,128)(2,1)S(1)}, bf16[2,128,256]{2,1,0:T(8,128)(2,1)S(1)}, u32[]{:S(2)}, u32[]{:S(2)}) collective-permute-start(bf16[2,128,256]{2,1,0:T(8,128)(2,1)S(1)} %get-tuple-element.25.own_ref), channel_id=1, source_target_pairs={{0,2},{1,31},{2,4},{3,1},{4,6},{5,3},{6,8},{7,5},{8,10},{9,7},{10,... | collective-permute-start | bytes 393224 | tf_op jit(solution)/shard_map/ppermute | solution.py:394
  13.4 9.0 %collective-permute-start.1 = (bf16[2,128,256]{2,1,0:T(8,128)(2,1)S(1)}, bf16[2,128,256]{2,1,0:T(8,128)(2,1)S(1)}, u32[]{:S(2)}, u32[]{:S(2)}) collective-permute-start(bf16[2,128,256]{2,1,0:T(8,128)(2,1)S(1)} %get-tuple-element.25.own_ref), channel_id=1, source_target_pairs={{0,4},{1,29},{2,6},{3,31},{4,8},{5,1},{6,10},{7,3},{8,12},{9,5},{1... | collective-permute-start | bytes 393224 | tf_op jit(solution)/shard_map/ppermute | solution.py:394
  22.5 12.4 %collective-permute-start.2 = (bf16[4,128,256]{2,1,0:T(8,128)(2,1)S(1)}, bf16[4,128,256]{2,1,0:T(8,128)(2,1)S(1)}, u32[]{:S(2)}, u32[]{:S(2)}) collective-permute-start(bf16[4,128,256]{2,1,0:T(8,128)(2,1)S(1)} %shard_map.120.refs_0_), channel_id=1, source_target_pairs={{0,4},{1,29},{2,6},{3,31},{4,8},{5,1},{6,10},{7,3},{8,12},{9,5},{1... | collective-permute-start | bytes 786440 | tf_op jit(solution)/shard_map/ppermute | solution.py:394
  34.9 12.0 %collective-permute-start.3 = (bf16[4,128,256]{2,1,0:T(8,128)(2,1)S(1)}, bf16[4,128,256]{2,1,0:T(8,128)(2,1)S(1)}, u32[]{:S(2)}, u32[]{:S(2)}) collective-permute-start(bf16[4,128,256]{2,1,0:T(8,128)(2,1)S(1)} %collective-permute-done.2.refs_1_), channel_id=1, source_target_pairs={{0,4},{1,29},{2,6},{3,31},{4,8},{5,1},{6,10},{7,3},{8,12},{9,5},{1... | collective-permute-start | bytes 786440 | tf_op jit(solution)/shard_map/ppermute | solution.py:394
  46.9 30.0 %collective-permute-start.5 = (bf16[12,128,256]{2,1,0:T(8,128)(2,1)S(1)}, bf16[12,128,256]{2,1,0:T(8,128)(2,1)S(1)}, u32[]{:S(2)}, u32[]{:S(2)}) collective-permute-start(bf16[12,128,256]{2,1,0:T(8,128)(2,1)S(1)} %shard_map.122), channel_id=1, source_target_pairs={{0,1},{1,0},{2,3},{3,2},{4,5},{5,4},{6,7},{7,6},{8,9},{9,8},{10,11... | collective-permute-start | bytes 2359304 | tf_op jit(solution)/shard_map/ppermute | solution.py:424
  48.8 28.1 %collective-permute-start.4 = (bf16[4,128,256]{2,1,0:T(8,128)(2,1)S(1)}, bf16[4,128,256]{2,1,0:T(8,128)(2,1)S(1)}, u32[]{:S(2)}, u32[]{:S(2)}) collective-permute-start(bf16[4,128,256]{2,1,0:T(8,128)(2,1)S(1)} %collective-permute-done.3.refs_2_), channel_id=1, source_target_pairs={{0,4},{1,29},{2,6},{3,31},{4,8},{5,1},{6,10},{7,3},{8,12},{9,5},{1... | collective-permute-start | bytes 786440 | tf_op jit(solution)/shard_map/ppermute | solution.py:394
  55.3 6.2 %collective-permute-start.6 = (bf16[128,256]{1,0:T(8,128)(2,1)S(1)}, bf16[128,256]{1,0:T(8,128)(2,1)S(1)}, u32[]{:S(2)}, u32[]{:S(2)}) collective-permute-start(bf16[128,256]{1,0:T(8,128)(2,1)S(1)} %get-tuple-element.33), channel_id=1, source_target_pairs={{0,64},{64,0},{128,192},{192,128},{1,65},{65,1},{129,193},{193,129... | collective-permute-start | bytes 196616 | tf_op jit(solution)/shard_map/ppermute | solution.py:387
  61.5 7.7 %collective-permute-start.7 = (bf16[128,256]{1,0:T(8,128)(2,1)S(1)}, bf16[128,256]{1,0:T(8,128)(2,1)S(1)}, u32[]{:S(2)}, u32[]{:S(2)}) collective-permute-start(bf16[128,256]{1,0:T(8,128)(2,1)S(1)} %add.13), channel_id=1, source_target_pairs={{0,128},{64,192},{128,0},{192,64},{1,129},{65,193},{129,1},{193,65... | collective-permute-start | bytes 196616 | tf_op jit(solution)/shard_map/ppermute | solution.py:387
  69.2 7.7 %collective-permute-start.8 = (bf16[128,256]{1,0:T(8,128)(2,1)S(1)}, bf16[128,256]{1,0:T(8,128)(2,1)S(1)}, u32[]{:S(2)}, u32[]{:S(2)}) collective-permute-start(bf16[128,256]{1,0:T(8,128)(2,1)S(1)} %add.14), channel_id=1, source_target_pairs={{0,256},{256,0},{1,257},{257,1},{2,258},{258,2},{3,259},{259,3},{4... | collective-permute-start | bytes 196616 | tf_op jit(solution)/shard_map/ppermute | solution.py:387
  79.1 19.5 %copy-start = (bf16[32,512]{1,0:T(8,128)(2,1)S(1)}, bf16[32,512]{1,0:T(8,128)(2,1)}, u32[]{:S(2)}) copy-start(bf16[32,512]{1,0:T(8,128)(2,1)} %proj_w_ref.1) | copy-start | bytes 98308
  79.1 19.5 %copy-start.1 = (f32[3,512]{1,0:T(4,128)S(1)}, f32[3,512]{1,0:T(4,128)}, u32[]{:S(2)}) copy-start(f32[3,512]{1,0:T(4,128)} %time_w_ref.1) | copy-start | bytes 18436
  79.1 19.5 %copy-start.2 = (f32[512]{0:T(512)S(1)}, f32[512]{0:T(512)}, u32[]{:S(2)}) copy-start(f32[512]{0:T(512)} %param.21) | copy-start | bytes 6148
  79.1 19.5 %copy-start.3 = (f32[512]{0:T(512)S(1)}, f32[512]{0:T(512)}, u32[]{:S(2)}) copy-start(f32[512]{0:T(512)} %param.23) | copy-start | bytes 6148
  84.4 10.5 %collective-permute-start.10 = (bf16[64,32]{1,0:T(8,128)(2,1)S(1)}, bf16[64,32]{1,0:T(8,128)(2,1)S(1)}, u32[]{:S(2)}, u32[]{:S(2)}) collective-permute-start(bf16[64,32]{1,0:T(8,128)(2,1)S(1)} %get-tuple-element.43.kept_ref), channel_id=1, source_target_pairs={{64,0},{32,96},{128,64},{96,160},{192,128},{160,224},{256,192},{22... | collective-permute-start | bytes 12296 | tf_op jit(solution)/shard_map/ppermute | solution.py:440
  89.6 7.7 %collective-permute-start.11 = (bf16[64,32]{1,0:T(8,128)(2,1)S(1)}, bf16[64,32]{1,0:T(8,128)(2,1)S(1)}, u32[]{:S(2)}, u32[]{:S(2)}) collective-permute-start(bf16[64,32]{1,0:T(8,128)(2,1)S(1)} %get-tuple-element.44), channel_id=1, source_target_pairs={{64,32},{32,64},{128,96},{96,128},{192,160},{160,192},{256,224},{2... | collective-permute-start | bytes 12296 | tf_op jit(solution)/shard_map/ppermute | solution.py:441
  93.0 5.6 %collective-permute-start.9 = (bf16[64,32]{1,0:T(8,128)(2,1)S(1)}, bf16[64,32]{1,0:T(8,128)(2,1)S(1)}, u32[]{:S(2)}, u32[]{:S(2)}) collective-permute-start(bf16[64,32]{1,0:T(8,128)(2,1)S(1)} %get-tuple-element.44), channel_id=1, source_target_pairs={{0,32},{32,0},{1,33},{33,1},{2,34},{34,2},{3,35},{35,3},{4,36},{36... | collective-permute-start | bytes 12296 | tf_op jit(solution)/shard_map/ppermute | solution.py:439

commit v7 on v5

--- a/solution.py
+++ b/solution.py
@@ -203,7 +203,7 @@
 
 
 def cost_kernel(z_count, where_ref, q_ref, own_ref, *refs):
-    *mine_refs, cross_ref, last_ref = refs[:-9]
+    *mine_refs, cross_ref, seven_ref, eight_ref = refs[:-9]
     a_ref, b_ref, bias1_ref, bias2_ref, kept_ref, sent_ref, corr, hid, acc = refs[-9:]
     z = where_ref[1]
     toward = 2 * where_ref[3] - 1
@@ -231,12 +231,9 @@
             distance += 1
             put(ref, k, toward * distance)
             put(cross_ref, 2 * distance - 2, -toward * distance)
-    half = last_ref.shape[0] // 2
-    for k in range(0, half, 2):
-        distance += 1
-        put(last_ref, k, -distance)
-        if 2 * distance < z_count:
-            put(last_ref, half + k, distance)
+    put(seven_ref, 0, -distance - 1)
+    put(seven_ref, 2, distance + 1)
+    put(eight_ref, 0, distance + 2)
 
     bias1 = bias1_ref[...]
     rows1 = 8
@@ -396,33 +393,26 @@
     def both(block):
         return lax.all_gather(block, "c", axis=0, tiled=True)
 
-    def behind(value, earlier):
-        return lax.optimization_barrier((value, earlier))[0]
-
     message = opening(where, frame_maps, query_table, start_frame, row_ids)
     gathered = lax.all_gather(message, ("xl", "c"), axis=0)
     own, queries = picked(where, gathered, frame_maps.shape[1])
     weights = banded_weights(conv1_w, conv1_b, conv2_w, conv2_b)
-    near = []
-    for distance in (1, 2, 3):
-        near.append(along(own, distance))
+    ring = {}
+    for distance in range(1, 9):
+        if distance <= 2:
+            ring[distance] = along(own, distance)
+        else:
+            ring[distance] = along(ring[distance - 2], 2)
     queries = queries + flip("y", y_count, 1)(queries)
-    near[1], near[2] = lax.optimization_barrier((near[1], near[2]))
-
-    pair = joined(near[1], near[2])
-    far5 = along(pair, 3)
-    far4 = along(near[0], 3)
     if y_count > 2:
-        queries = queries + flip("y", y_count, 2)(behind(queries, pair))
-    far5, weights = lax.optimization_barrier((far5, weights))
-
-    far7 = along(far5, 2)
+        queries = queries + flip("y", y_count, 2)(queries)
     if xh_count > 1:
-        queries = queries + flip("xh", xh_count, 1)(behind(queries, far5))
-    mine = [near[0], pair, far4, far5]
+        queries = queries + flip("xh", xh_count, 1)(queries)
+    mine = [ring[distance] for distance in range(1, 7)]
     cross = lax.ppermute(joined(*mine), "c", swap)
-    far7, cross, queries = lax.optimization_barrier((far7, cross, queries))
-    spread = mine + [cross, both(far7)]
+    seven = both(ring[7])
+    eight, seven, cross, weights = lax.optimization_barrier((ring[8], seven, cross, weights))
+    spread = mine + [cross, seven, eight]
 
     kept, sent = pooled_costs(where, queries, own, spread, *weights)
 

time: 112 us -> 98.4 us (0.88)
  the two profiles are of different devices: /device:TPU:68 before, /device:TPU:58 now
where the time goes in v7:
time: 98.4 us; the launch traced here: 97.7 us
  starting transfers between devices  55.4 us (56%)
  waiting for transfers between devices  23.7 us (24%)
  Pallas kernels  10.1 us (10%)
  blocking collectives  8.13 us (8%)
    ppermute x8, starting transfers between devices, along(): return lax.ppermute(block, ('z', 'c'), pairs)  32.9 us
    ppermute x8, waiting for transfers between devices, along(): return lax.ppermute(block, ('z', 'c'), pairs)  15.9 us
    ppermute x3, starting transfers between devices, flip(): lax.ppermute(v, axis, [(i, i ^ step) for i in range(count)])  9.83 us
    all_gather x1, blocking collectives, one_device(): gathered = lax.all_gather(message, ('xl', 'c'), axis=0)  6.14 us
    pallas_call x1, Pallas kernels, pooled_costs(): pl.pallas_call(functools.partial(cost_kernel, z_count), out_shape=(jax.Sh...  5.3 us
    ppermute x1, starting transfers between devices, one_device(): crossed = lax.ppermute(sent, ('xh', 'y', 'xl'), frame_pairs(True))  5.24 us
    ppermute x3, waiting for transfers between devices, flip(): lax.ppermute(v, axis, [(i, i ^ step) for i in range(count)])  4.1 us
    ppermute x1, starting transfers between devices, one_device(): straight = lax.ppermute(kept, ('xh', 'y', 'xl'), frame_pairs(False))  3.61 us
  transfers between devices with their start and end apart: 15, of which 10 were waited for; matrix products, arithmetic and copies ran while one was open for 0% of the time, Pallas kernels for 1%

profile of v7, /device:TPU:58, one launch (start us, length us, event | category | flops | bytes accessed | tf_op | source)
XLA Modules:
  0.0 97.7 jit_solution(16985097242878421965)
XLA Ops:
  1.7 6.1 %all-gather = bf16[768,256]{1,0:T(8,128)(2,1)S(1)} all-gather(bf16[192,256]{1,0:T(8,128)(2,1)S(1)} %shard_map.118), channel_id=2, replica_groups=mesh['xh'=2,'y'=4,'xl'=2,'z'=16,'c'=2] {'xl','c'}, dimensions={0}, use_global_device_ids=true | all-gather | bytes 491520 | tf_op jit(solution)/shard_map/all_gather | solution.py:397
  8.4 5.2 %collective-permute-start.4 = (bf16[2,128,256]{2,1,0:T(8,128)(2,1)S(1)}, bf16[2,128,256]{2,1,0:T(8,128)(2,1)S(1)}, u32[]{:S(2)}, u32[]{:S(2)}) collective-permute-start(bf16[2,128,256]{2,1,0:T(8,128)(2,1)S(1)} %get-tuple-element.21.own_ref), channel_id=1, source_target_pairs={{0,4},{1,29},{2,6},{3,31},{4,8},{5,1},{6,10},{7,3},{8,12},{9,5},{1... | collective-permute-start | bytes 393224 | tf_op jit(solution)/shard_map/ppermute | solution.py:391
  13.5 5.0 %collective-permute-start.3 = (bf16[2,128,256]{2,1,0:T(8,128)(2,1)S(1)}, bf16[2,128,256]{2,1,0:T(8,128)(2,1)S(1)}, u32[]{:S(2)}, u32[]{:S(2)}) collective-permute-start(bf16[2,128,256]{2,1,0:T(8,128)(2,1)S(1)} %get-tuple-element.21.own_ref), channel_id=1, source_target_pairs={{0,2},{1,31},{2,4},{3,1},{4,6},{5,3},{6,8},{7,5},{8,10},{9,7},{10,... | collective-permute-start | bytes 393224 | tf_op jit(solution)/shard_map/ppermute | solution.py:391
  18.6 5.1 %collective-permute-done.4.refs_1_ = bf16[2,128,256]{2,1,0:T(8,128)(2,1)S(1)} collective-permute-done((bf16[2,128,256]{2,1,0:T(8,128)(2,1)S(1)}, bf16[2,128,256]{2,1,0:T(8,128)(2,1)S(1)}, u32[]{:S(2)}, u32[]{:S(2)}) %collective-permute-start.4) | collective-permute-done | bytes 131104 | tf_op jit(solution)/shard_map/ppermute | solution.py:391
  23.6 1.9 %collective-permute-start.6 = (bf16[2,128,256]{2,1,0:T(8,128)(2,1)S(1)}, bf16[2,128,256]{2,1,0:T(8,128)(2,1)S(1)}, u32[]{:S(2)}, u32[]{:S(2)}) collective-permute-start(bf16[2,128,256]{2,1,0:T(8,128)(2,1)S(1)} %collective-permute-done.4.refs_1_), channel_id=1, source_target_pairs={{0,4},{1,29},{2,6},{3,31},{4,8},{5,1},{6,10},{7,3},{8,12},{9,5},{1... | collective-permute-start | bytes 393224 | tf_op jit(solution)/shard_map/ppermute | solution.py:391
  25.6 4.7 %collective-permute-start.5 = (bf16[2,128,256]{2,1,0:T(8,128)(2,1)S(1)}, bf16[2,128,256]{2,1,0:T(8,128)(2,1)S(1)}, u32[]{:S(2)}, u32[]{:S(2)}) collective-permute-start(bf16[2,128,256]{2,1,0:T(8,128)(2,1)S(1)} %collective-permute-done.3.refs_0_), channel_id=1, source_target_pairs={{0,4},{1,29},{2,6},{3,31},{4,8},{5,1},{6,10},{7,3},{8,12},{9,5},{1... | collective-permute-start | bytes 393224 | tf_op jit(solution)/shard_map/ppermute | solution.py:391
  30.3 3.5 %collective-permute-done.6.refs_3_ = bf16[2,128,256]{2,1,0:T(8,128)(2,1)S(1)} collective-permute-done((bf16[2,128,256]{2,1,0:T(8,128)(2,1)S(1)}, bf16[2,128,256]{2,1,0:T(8,128)(2,1)S(1)}, u32[]{:S(2)}, u32[]{:S(2)}) %collective-permute-start.6) | collective-permute-done | bytes 131104 | tf_op jit(solution)/shard_map/ppermute | solution.py:391
  33.7 1.9 %collective-permute-start.8 = (bf16[2,128,256]{2,1,0:T(8,128)(2,1)S(1)}, bf16[2,128,256]{2,1,0:T(8,128)(2,1)S(1)}, u32[]{:S(2)}, u32[]{:S(2)}) collective-permute-start(bf16[2,128,256]{2,1,0:T(8,128)(2,1)S(1)} %collective-permute-done.6.refs_3_), channel_id=1, source_target_pairs={{0,4},{1,29},{2,6},{3,31},{4,8},{5,1},{6,10},{7,3},{8,12},{9,5},{1... | collective-permute-start | bytes 393224 | tf_op jit(solution)/shard_map/ppermute | solution.py:391
  36.0 5.1 %collective-permute-start.7 = (bf16[2,128,256]{2,1,0:T(8,128)(2,1)S(1)}, bf16[2,128,256]{2,1,0:T(8,128)(2,1)S(1)}, u32[]{:S(2)}, u32[]{:S(2)}) collective-permute-start(bf16[2,128,256]{2,1,0:T(8,128)(2,1)S(1)} %collective-permute-done.5.refs_2_), channel_id=1, source_target_pairs={{0,4},{1,29},{2,6},{3,31},{4,8},{5,1},{6,10},{7,3},{8,12},{9,5},{1... | collective-permute-start | bytes 393224 | tf_op jit(solution)/shard_map/ppermute | solution.py:391
  42.7 3.2 %collective-permute-done.7.refs_4_ = bf16[2,128,256]{2,1,0:T(8,128)(2,1)S(1)} collective-permute-done((bf16[2,128,256]{2,1,0:T(8,128)(2,1)S(1)}, bf16[2,128,256]{2,1,0:T(8,128)(2,1)S(1)}, u32[]{:S(2)}, u32[]{:S(2)}) %collective-permute-start.7) | collective-permute-done | bytes 131104 | tf_op jit(solution)/shard_map/ppermute | solution.py:391
  45.9 1.9 %collective-permute-start.11 = (bf16[12,128,256]{2,1,0:T(8,128)(2,1)S(1)}, bf16[12,128,256]{2,1,0:T(8,128)(2,1)S(1)}, u32[]{:S(2)}, u32[]{:S(2)}) collective-permute-start(bf16[12,128,256]{2,1,0:T(8,128)(2,1)S(1)} %shard_map.120), channel_id=1, source_target_pairs={{0,1},{1,0},{2,3},{3,2},{4,5},{5,4},{6,7},{7,6},{8,9},{9,8},{10,11... | collective-permute-start | bytes 2359304 | tf_op jit(solution)/shard_map/ppermute | solution.py:412
  47.9 2.7 %collective-permute-start = (bf16[128,256]{1,0:T(8,128)(2,1)S(1)}, bf16[128,256]{1,0:T(8,128)(2,1)S(1)}, u32[]{:S(2)}, u32[]{:S(2)}) collective-permute-start(bf16[128,256]{1,0:T(8,128)(2,1)S(1)} %get-tuple-element.20), channel_id=1, source_target_pairs={{0,64},{64,0},{128,192},{192,128},{1,65},{65,1},{129,193},{193,129... | collective-permute-start | bytes 196616 | tf_op jit(solution)/shard_map/ppermute | solution.py:384
  50.5 3.7 %collective-permute-done = bf16[128,256]{1,0:T(8,128)(2,1)S(1)} collective-permute-done((bf16[128,256]{1,0:T(8,128)(2,1)S(1)}, bf16[128,256]{1,0:T(8,128)(2,1)S(1)}, u32[]{:S(2)}, u32[]{:S(2)}) %collective-permute-start) | collective-permute-done | bytes 65568 | tf_op jit(solution)/shard_map/ppermute | solution.py:384
  54.3 3.1 %collective-permute-start.1 = (bf16[128,256]{1,0:T(8,128)(2,1)S(1)}, bf16[128,256]{1,0:T(8,128)(2,1)S(1)}, u32[]{:S(2)}, u32[]{:S(2)}) collective-permute-start(bf16[128,256]{1,0:T(8,128)(2,1)S(1)} %add.13), channel_id=1, source_target_pairs={{0,128},{64,192},{128,0},{192,64},{1,129},{65,193},{129,1},{193,65... | collective-permute-start | bytes 196616 | tf_op jit(solution)/shard_map/ppermute | solution.py:384
  57.4 4.1 %collective-permute-start.10 = (bf16[2,128,256]{2,1,0:T(8,128)(2,1)S(1)}, bf16[2,128,256]{2,1,0:T(8,128)(2,1)S(1)}, u32[]{:S(2)}, u32[]{:S(2)}) collective-permute-start(bf16[2,128,256]{2,1,0:T(8,128)(2,1)S(1)} %collective-permute-done.7.refs_4_), channel_id=1, source_target_pairs={{0,4},{1,29},{2,6},{3,31},{4,8},{5,1},{6,10},{7,3},{8,12},{9,5},{1... | collective-permute-start | bytes 393224 | tf_op jit(solution)/shard_map/ppermute | solution.py:391
  62.0 4.0 %collective-permute-start.2 = (bf16[128,256]{1,0:T(8,128)(2,1)S(1)}, bf16[128,256]{1,0:T(8,128)(2,1)S(1)}, u32[]{:S(2)}, u32[]{:S(2)}) collective-permute-start(bf16[128,256]{1,0:T(8,128)(2,1)S(1)} %add.14), channel_id=1, source_target_pairs={{0,256},{256,0},{1,257},{257,1},{2,258},{258,2},{3,259},{259,3},{4... | collective-permute-start | bytes 196616 | tf_op jit(solution)/shard_map/ppermute | solution.py:384
  66.0 4.9 %collective-permute-start.9 = (bf16[2,128,256]{2,1,0:T(8,128)(2,1)S(1)}, bf16[2,128,256]{2,1,0:T(8,128)(2,1)S(1)}, u32[]{:S(2)}, u32[]{:S(2)}) collective-permute-start(bf16[2,128,256]{2,1,0:T(8,128)(2,1)S(1)} %collective-permute-done.8.refs_5_), channel_id=1, source_target_pairs={{0,4},{1,29},{2,6},{3,31},{4,8},{5,1},{6,10},{7,3},{8,12},{9,5},{1... | collective-permute-start | bytes 393224 | tf_op jit(solution)/shard_map/ppermute | solution.py:391
  72.1 2.0 %all_gather.11.refs_7_ = bf16[4,128,256]{2,1,0:T(8,128)(2,1)S(1)} all-gather(bf16[2,128,256]{2,1,0:T(8,128)(2,1)S(1)} %collective-permute-done.10), channel_id=1, replica_groups=mesh['xh'=2,'y'=4,'xl'=2,'z'=16,'c'=2] {'c'}, dimensions={0}, use_global_device_ids=true | all-gather | bytes 393216 | tf_op jit(solution)/shard_map/all_gather | solution.py:394
  74.1 2.3 %collective-permute-done.9.refs_8_ = bf16[2,128,256]{2,1,0:T(8,128)(2,1)S(1)} collective-permute-done((bf16[2,128,256]{2,1,0:T(8,128)(2,1)S(1)}, bf16[2,128,256]{2,1,0:T(8,128)(2,1)S(1)}, u32[]{:S(2)}, u32[]{:S(2)}) %collective-permute-start.9) | collective-permute-done | bytes 131104 | tf_op jit(solution)/shard_map/ppermute | solution.py:391
  76.4 5.3 %shard_map.122 = (bf16[64,32]{1,0:T(8,128)(2,1)S(1)}, bf16[64,32]{1,0:T(8,128)(2,1)S(1)}) custom-call(s32[4]{0:T(128)S(1)} %pad_add_fusion.where_ref, bf16[128,256]{1,0:T(8,128)(2,1)S(1)} %add.15.q_ref, bf16[2,128,256]{2,1,0:T(8,128)(2,1)S(1)} %get-tuple-element.21.own_ref, bf16[2,128,256]{2,1,0:T(8,128)(2,1)S(1)} %collective-permute-done.3.refs_0_, ...), custom_call_target="tpu_custom_call" | custom-call | flops 5000000000 | bytes 4000000 | tf_op jit(solution)/shard_map/pallas_call | solution.py:288
  81.7 3.6 %collective-permute-start.13 = (bf16[64,32]{1,0:T(8,128)(2,1)S(1)}, bf16[64,32]{1,0:T(8,128)(2,1)S(1)}, u32[]{:S(2)}, u32[]{:S(2)}) collective-permute-start(bf16[64,32]{1,0:T(8,128)(2,1)S(1)} %get-tuple-element.33.kept_ref), channel_id=1, source_target_pairs={{64,0},{32,96},{128,64},{96,160},{192,128},{160,224},{256,192},{22... | collective-permute-start | bytes 12296 | tf_op jit(solution)/shard_map/ppermute | solution.py:429
  85.3 5.2 %collective-permute-start.14 = (bf16[64,32]{1,0:T(8,128)(2,1)S(1)}, bf16[64,32]{1,0:T(8,128)(2,1)S(1)}, u32[]{:S(2)}, u32[]{:S(2)}) collective-permute-start(bf16[64,32]{1,0:T(8,128)(2,1)S(1)} %get-tuple-element.34), channel_id=1, source_target_pairs={{64,32},{32,64},{128,96},{96,128},{192,160},{160,192},{256,224},{2... | collective-permute-start | bytes 12296 | tf_op jit(solution)/shard_map/ppermute | solution.py:430
  90.6 1.9 %collective-permute-start.12 = (bf16[64,32]{1,0:T(8,128)(2,1)S(1)}, bf16[64,32]{1,0:T(8,128)(2,1)S(1)}, u32[]{:S(2)}, u32[]{:S(2)}) collective-permute-start(bf16[64,32]{1,0:T(8,128)(2,1)S(1)} %get-tuple-element.34), channel_id=1, source_target_pairs={{0,32},{32,0},{1,33},{33,1},{2,34},{34,2},{3,35},{35,3},{4,36},{36... | collective-permute-start | bytes 12296 | tf_op jit(solution)/shard_map/ppermute | solution.py:428
  93.1 3.1 %collective-permute-done.12.partner_ref = bf16[64,32]{1,0:T(8,128)(2,1)S(1)} collective-permute-done((bf16[64,32]{1,0:T(8,128)(2,1)S(1)}, bf16[64,32]{1,0:T(8,128)(2,1)S(1)}, u32[]{:S(2)}, u32[]{:S(2)}) %collective-permute-start.12) | collective-permute-done | bytes 4128 | tf_op jit(solution)/shard_map/ppermute | solution.py:428
  (26 shorter events, 7.8 us)
Async XLA Ops:
  8.4 15.3 %collective-permute-start.4 = (bf16[2,128,256]{2,1,0:T(8,128)(2,1)S(1)}, bf16[2,128,256]{2,1,0:T(8,128)(2,1)S(1)}, u32[]{:S(2)}, u32[]{:S(2)}) collective-permute-start(bf16[2,128,256]{2,1,0:T(8,128)(2,1)S(1)} %get-tuple-element.21.own_ref), channel_id=1, source_target_pairs={{0,4},{1,29},{2,6},{3,31},{4,8},{5,1},{6,10},{7,3},{8,12},{9,5},{1... | collective-permute-start | bytes 393224 | tf_op jit(solution)/shard_map/ppermute | solution.py:391
  13.5 12.0 %collective-permute-start.3 = (bf16[2,128,256]{2,1,0:T(8,128)(2,1)S(1)}, bf16[2,128,256]{2,1,0:T(8,128)(2,1)S(1)}, u32[]{:S(2)}, u32[]{:S(2)}) collective-permute-start(bf16[2,128,256]{2,1,0:T(8,128)(2,1)S(1)} %get-tuple-element.21.own_ref), channel_id=1, source_target_pairs={{0,2},{1,31},{2,4},{3,1},{4,6},{5,3},{6,8},{7,5},{8,10},{9,7},{10,... | collective-permute-start | bytes 393224 | tf_op jit(solution)/shard_map/ppermute | solution.py:391
  23.6 10.1 %collective-permute-start.6 = (bf16[2,128,256]{2,1,0:T(8,128)(2,1)S(1)}, bf16[2,128,256]{2,1,0:T(8,128)(2,1)S(1)}, u32[]{:S(2)}, u32[]{:S(2)}) collective-permute-start(bf16[2,128,256]{2,1,0:T(8,128)(2,1)S(1)} %collective-permute-done.4.refs_1_), channel_id=1, source_target_pairs={{0,4},{1,29},{2,6},{3,31},{4,8},{5,1},{6,10},{7,3},{8,12},{9,5},{1... | collective-permute-start | bytes 393224 | tf_op jit(solution)/shard_map/ppermute | solution.py:391
  25.6 10.4 %collective-permute-start.5 = (bf16[2,128,256]{2,1,0:T(8,128)(2,1)S(1)}, bf16[2,128,256]{2,1,0:T(8,128)(2,1)S(1)}, u32[]{:S(2)}, u32[]{:S(2)}) collective-permute-start(bf16[2,128,256]{2,1,0:T(8,128)(2,1)S(1)} %collective-permute-done.3.refs_0_), channel_id=1, source_target_pairs={{0,4},{1,29},{2,6},{3,31},{4,8},{5,1},{6,10},{7,3},{8,12},{9,5},{1... | collective-permute-start | bytes 393224 | tf_op jit(solution)/shard_map/ppermute | solution.py:391
  33.7 9.0 %collective-permute-start.8 = (bf16[2,128,256]{2,1,0:T(8,128)(2,1)S(1)}, bf16[2,128,256]{2,1,0:T(8,128)(2,1)S(1)}, u32[]{:S(2)}, u32[]{:S(2)}) collective-permute-start(bf16[2,128,256]{2,1,0:T(8,128)(2,1)S(1)} %collective-permute-done.6.refs_3_), channel_id=1, source_target_pairs={{0,4},{1,29},{2,6},{3,31},{4,8},{5,1},{6,10},{7,3},{8,12},{9,5},{1... | collective-permute-start | bytes 393224 | tf_op jit(solution)/shard_map/ppermute | solution.py:391
  36.0 9.9 %collective-permute-start.7 = (bf16[2,128,256]{2,1,0:T(8,128)(2,1)S(1)}, bf16[2,128,256]{2,1,0:T(8,128)(2,1)S(1)}, u32[]{:S(2)}, u32[]{:S(2)}) collective-permute-start(bf16[2,128,256]{2,1,0:T(8,128)(2,1)S(1)} %collective-permute-done.5.refs_2_), channel_id=1, source_target_pairs={{0,4},{1,29},{2,6},{3,31},{4,8},{5,1},{6,10},{7,3},{8,12},{9,5},{1... | collective-permute-start | bytes 393224 | tf_op jit(solution)/shard_map/ppermute | solution.py:391
  45.9 30.4 %collective-permute-start.11 = (bf16[12,128,256]{2,1,0:T(8,128)(2,1)S(1)}, bf16[12,128,256]{2,1,0:T(8,128)(2,1)S(1)}, u32[]{:S(2)}, u32[]{:S(2)}) collective-permute-start(bf16[12,128,256]{2,1,0:T(8,128)(2,1)S(1)} %shard_map.120), channel_id=1, source_target_pairs={{0,1},{1,0},{2,3},{3,2},{4,5},{5,4},{6,7},{7,6},{8,9},{9,8},{10,11... | collective-permute-start | bytes 2359304 | tf_op jit(solution)/shard_map/ppermute | solution.py:412
  47.9 6.4 %collective-permute-start = (bf16[128,256]{1,0:T(8,128)(2,1)S(1)}, bf16[128,256]{1,0:T(8,128)(2,1)S(1)}, u32[]{:S(2)}, u32[]{:S(2)}) collective-permute-start(bf16[128,256]{1,0:T(8,128)(2,1)S(1)} %get-tuple-element.20), channel_id=1, source_target_pairs={{0,64},{64,0},{128,192},{192,128},{1,65},{65,1},{129,193},{193,129... | collective-permute-start | bytes 196616 | tf_op jit(solution)/shard_map/ppermute | solution.py:384
  54.3 7.7 %collective-permute-start.1 = (bf16[128,256]{1,0:T(8,128)(2,1)S(1)}, bf16[128,256]{1,0:T(8,128)(2,1)S(1)}, u32[]{:S(2)}, u32[]{:S(2)}) collective-permute-start(bf16[128,256]{1,0:T(8,128)(2,1)S(1)} %add.13), channel_id=1, source_target_pairs={{0,128},{64,192},{128,0},{192,64},{1,129},{65,193},{129,1},{193,65... | collective-permute-start | bytes 196616 | tf_op jit(solution)/shard_map/ppermute | solution.py:384
  57.4 14.6 %collective-permute-start.10 = (bf16[2,128,256]{2,1,0:T(8,128)(2,1)S(1)}, bf16[2,128,256]{2,1,0:T(8,128)(2,1)S(1)}, u32[]{:S(2)}, u32[]{:S(2)}) collective-permute-start(bf16[2,128,256]{2,1,0:T(8,128)(2,1)S(1)} %collective-permute-done.7.refs_4_), channel_id=1, source_target_pairs={{0,4},{1,29},{2,6},{3,31},{4,8},{5,1},{6,10},{7,3},{8,12},{9,5},{1... | collective-permute-start | bytes 393224 | tf_op jit(solution)/shard_map/ppermute | solution.py:391
  62.0 10.1 %collective-permute-start.2 = (bf16[128,256]{1,0:T(8,128)(2,1)S(1)}, bf16[128,256]{1,0:T(8,128)(2,1)S(1)}, u32[]{:S(2)}, u32[]{:S(2)}) collective-permute-start(bf16[128,256]{1,0:T(8,128)(2,1)S(1)} %add.14), channel_id=1, source_target_pairs={{0,256},{256,0},{1,257},{257,1},{2,258},{258,2},{3,259},{259,3},{4... | collective-permute-start | bytes 196616 | tf_op jit(solution)/shard_map/ppermute | solution.py:384
  66.0 10.4 %collective-permute-start.9 = (bf16[2,128,256]{2,1,0:T(8,128)(2,1)S(1)}, bf16[2,128,256]{2,1,0:T(8,128)(2,1)S(1)}, u32[]{:S(2)}, u32[]{:S(2)}) collective-permute-start(bf16[2,128,256]{2,1,0:T(8,128)(2,1)S(1)} %collective-permute-done.8.refs_5_), channel_id=1, source_target_pairs={{0,4},{1,29},{2,6},{3,31},{4,8},{5,1},{6,10},{7,3},{8,12},{9,5},{1... | collective-permute-start | bytes 393224 | tf_op jit(solution)/shard_map/ppermute | solution.py:391
  76.4 19.8 %copy-start = (bf16[32,512]{1,0:T(8,128)(2,1)S(1)}, bf16[32,512]{1,0:T(8,128)(2,1)}, u32[]{:S(2)}) copy-start(bf16[32,512]{1,0:T(8,128)(2,1)} %proj_w_ref.1) | copy-start | bytes 98308
  76.4 19.8 %copy-start.1 = (f32[3,512]{1,0:T(4,128)S(1)}, f32[3,512]{1,0:T(4,128)}, u32[]{:S(2)}) copy-start(f32[3,512]{1,0:T(4,128)} %time_w_ref.1) | copy-start | bytes 18436
  76.4 19.8 %copy-start.2 = (f32[512]{0:T(512)S(1)}, f32[512]{0:T(512)}, u32[]{:S(2)}) copy-start(f32[512]{0:T(512)} %param.21) | copy-start | bytes 6148
  76.4 19.8 %copy-start.3 = (f32[512]{0:T(512)S(1)}, f32[512]{0:T(512)}, u32[]{:S(2)}) copy-start(f32[512]{0:T(512)} %param.23) | copy-start | bytes 6148
  81.7 10.8 %collective-permute-start.13 = (bf16[64,32]{1,0:T(8,128)(2,1)S(1)}, bf16[64,32]{1,0:T(8,128)(2,1)S(1)}, u32[]{:S(2)}, u32[]{:S(2)}) collective-permute-start(bf16[64,32]{1,0:T(8,128)(2,1)S(1)} %get-tuple-element.33.kept_ref), channel_id=1, source_target_pairs={{64,0},{32,96},{128,64},{96,160},{192,128},{160,224},{256,192},{22... | collective-permute-start | bytes 12296 | tf_op jit(solution)/shard_map/ppermute | solution.py:429
  85.3 7.7 %collective-permute-start.14 = (bf16[64,32]{1,0:T(8,128)(2,1)S(1)}, bf16[64,32]{1,0:T(8,128)(2,1)S(1)}, u32[]{:S(2)}, u32[]{:S(2)}) collective-permute-start(bf16[64,32]{1,0:T(8,128)(2,1)S(1)} %get-tuple-element.34), channel_id=1, source_target_pairs={{64,32},{32,64},{128,96},{96,128},{192,160},{160,192},{256,224},{2... | collective-permute-start | bytes 12296 | tf_op jit(solution)/shard_map/ppermute | solution.py:430
  90.6 5.6 %collective-permute-start.12 = (bf16[64,32]{1,0:T(8,128)(2,1)S(1)}, bf16[64,32]{1,0:T(8,128)(2,1)S(1)}, u32[]{:S(2)}, u32[]{:S(2)}) collective-permute-start(bf16[64,32]{1,0:T(8,128)(2,1)S(1)} %get-tuple-element.34), channel_id=1, source_target_pairs={{0,32},{32,0},{1,33},{33,1},{2,34},{34,2},{3,35},{35,3},{4,36},{36... | collective-permute-start | bytes 12296 | tf_op jit(solution)/shard_map/ppermute | solution.py:428
